TPU v7x, 256 devices: a whole 4x4x8 slice. The times are simulated.
256 devices in a mesh: ctx: 32 (over y, z), heads: 8 (over x, core).
Axes of the slice: x: 4, y: 4, z: 8, core: 2. Of those that a mesh axis runs over, the one named last changes fastest.
Arguments:
- queries: bfloat16 [32768, 4096], P('ctx', 'heads'), may hold values from -8 to 8
- keys: bfloat16 [32768, 4096], P('ctx', 'heads'), may hold values from -8 to 8
- values: bfloat16 [32768, 4096], P('ctx', 'heads'), may hold values from -8 to 8
- gate_bias: float32 [32], P('heads'), may hold values from -2 to 2
- out_weight: bfloat16 [4096, 4096], P('heads'), may hold values from -0.09375 to 0.09375
Outputs:
- layer_out: bfloat16 [32768, 4096], P('ctx', 'heads')
All inputs are finite; a program needn't handle non-finite values.
Results may differ from a plain program's by a relative error of at most 0.0051.
Values may be sent and summed in bfloat16 or wider, within the bound.
No kernel may reach another device: no remote copies, remote signals or barrier semaphores. Data moves between devices by JAX's collectives and lax.ppermute only.
A program may use at most 128 MiB of HBM per device.

v0:
```python
import math

import jax
import jax.numpy as jnp
from jax import lax
from jax.sharding import Mesh
from jax.sharding import PartitionSpec as P

HD = 128
CTX = ("ctx_0", "ctx_1")


masked_score = -1e30


def nothing_yet(array, identity):
    return jax.tree.map(
        lambda a, e: jnp.broadcast_to(jnp.asarray(e, a.dtype), a.shape), array, identity
    )


def entering(array, axes, combine, identity):
    before = start = nothing_yet(array, identity)
    subtotal = array
    for axis in reversed(axes):
        size, mine = (lax.axis_size(axis), lax.axis_index(axis))
        pieces = jax.tree.map(lambda part: lax.all_gather(part, axis), subtotal)
        inside, subtotal = (start, start)
        for k in range(size):
            passed = k < mine
            subtotal = combine(subtotal, jax.tree.map(lambda part: part[k], pieces))
            inside = jax.tree.map(lambda new, old: jnp.where(passed, new, old), subtotal, inside)
        before = combine(inside, before)
    return before


def features(inputs):
    return jax.nn.elu(inputs) + 1.0


def add_pair(earlier, later):
    return (earlier[0] + later[0], earlier[1] + later[1])


def local_attention(query_heads, key_heads, value_heads):
    tok_rows = query_heads.shape[0]
    block_rows = min(512, tok_rows)
    score_scale = 1.0 / math.sqrt(HD)
    outputs = []
    for block_index in range(tok_rows // block_rows):
        first_query = block_index * block_rows
        key_end = first_query + block_rows
        scores = (
            jnp.einsum(
                "qhd,khd->hqk",
                query_heads[first_query:key_end],
                key_heads[:key_end],
                preferred_element_type=jnp.float32,
            )
            * score_scale
        )
        query_pos = first_query + lax.iota(jnp.int32, block_rows)
        key_pos = lax.iota(jnp.int32, key_end)
        allowed = key_pos[None, :] <= query_pos[:, None]
        scores = jnp.where(allowed[None], scores, masked_score)
        row_max = jnp.max(scores, axis=-1, keepdims=True)
        weights = jnp.exp(scores - row_max)
        probabilities = (weights / jnp.sum(weights, axis=-1, keepdims=True)).astype(jnp.bfloat16)
        outputs.append(
            jnp.einsum(
                "hqk,khd->qhd",
                probabilities,
                value_heads[:key_end],
                preferred_element_type=jnp.float32,
            )
        )
    return jnp.concatenate(outputs, axis=0)


def local(queries, keys, values, gate_bias, out_weight):
    tok_rows = queries.shape[0]
    local_heads = gate_bias.shape[0]
    query_heads = queries.reshape(tok_rows, local_heads, HD)
    key_heads = keys.reshape(tok_rows, local_heads, HD)
    value_heads = values.reshape(tok_rows, local_heads, HD)
    feat_key = features(key_heads.astype(jnp.float32))
    delta_memory = jnp.einsum("thd,the->hde", feat_key, value_heads.astype(jnp.float32))
    delta_normal = jnp.sum(feat_key, axis=0)
    zero_memory = jnp.zeros_like(delta_memory)
    zero_normal = jnp.zeros_like(delta_normal)
    prior_memory, prior_normal = entering(
        (delta_memory, delta_normal), CTX, add_pair, (zero_memory, zero_normal)
    )
    local_out = local_attention(query_heads, key_heads, value_heads)
    feat_query = features(query_heads.astype(jnp.float32))
    numer = jnp.einsum("thd,hde->the", feat_query, prior_memory)
    denom = jnp.maximum(jnp.einsum("thd,hd->th", feat_query, prior_normal), 1.0)
    retrieved = numer / denom[..., None]
    mix_gate = jax.nn.sigmoid(gate_bias)[None, :, None]
    attended = (mix_gate * retrieved + (1.0 - mix_gate) * local_out).astype(jnp.bfloat16)
    attended = attended.reshape(tok_rows, local_heads * HD)
    partial_terms = jnp.dot(attended, out_weight, preferred_element_type=jnp.float32)
    summed = lax.psum_scatter(partial_terms, "heads", scatter_dimension=1, tiled=True)
    return summed.astype(jnp.bfloat16)


def solution(mesh):
    finer = Mesh(mesh.devices.reshape(4, 8, mesh.shape["heads"]), ("ctx_0", "ctx_1", "heads"))
    placed = (P(CTX, "heads"), P(CTX, "heads"), P(CTX, "heads"), P("heads"), P("heads", None))
    return jax.shard_map(
        local, mesh=finer, in_specs=placed, out_specs=P(CTX, "heads"), check_vma=False
    )
```

profile of v0, /device:TPU:1, one launch (start us, length us, event | category | flops | bytes accessed | tf_op | source)
XLA Modules:
  0.0 212.2 jit_solution(11448984378752005559)
XLA Ops:
  6.5 0.0 all-gather.6.cloned.1.call-start
  6.5 3.4 %fusion.10 = f32[4,128,128]{2,1,0:T(8,128)} fusion(bf16[1024,512]{1,0:T(8,128)(2,1)} %param.7, bf16[1024,512]{1,0:T(8,128)(2,1)} %param.6), kind=kOutput, calls=%fused_computation.22 | convolution fusion | flops 136839168 | bytes 2359296 | tf_op jit(solution)/shard_map/thd,the->hde/dot_general | solution.py:87
  10.0 0.0 copy-start.4
  10.0 0.0 all-gather.6.cloned.1.call-update
  10.0 0.0 all-gather.4.cloned.1.call-start
  10.1 1.1 copy-done.4
  11.2 0.0 slice-start
  11.2 0.9 fusion.90
  12.1 0.0 slice-start.1
  12.1 0.0 copy-start
  12.1 1.4 copy.72
  13.4 1.0 copy.70
  14.4 0.0 slice-done
  14.4 0.2 copy.71
  14.7 0.0 slice-done.1
  14.7 0.2 copy.69
  14.9 0.0 copy-done
  14.9 1.0 fusion.16
  15.9 22.1 %all_gather.24 = f32[8,4,128]{2,1,0:T(4,128)S(1)} all-gather(f32[1,4,128]{2,1,0:T(4,128)S(1)} %bitcast.86), channel_id=1, replica_groups=mesh['ctx_0'=4,'ctx_1'=8,'heads'=8] {'ctx_1'}, dimensions={0}, use_global_device_ids=true | all-gather | bytes 18432 | tf_op jit(solution)/shard_map/all_gather | solution.py:27
  37.9 9.8 %all_gather.25 = f32[4,4,128]{2,1,0:T(4,128)S(1)} all-gather(f32[1,4,128]{2,1,0:T(4,128)S(1)} %get-tuple-element.7), channel_id=1, replica_groups=mesh['ctx_0'=4,'ctx_1'=8,'heads'=8] {'ctx_0'}, dimensions={0}, use_global_device_ids=true | all-gather | bytes 10240 | tf_op jit(solution)/shard_map/all_gather | solution.py:27
  47.7 0.1 iota_compare_fusion.1
  47.8 1.2 iota_compare_fusion
  49.0 0.0 copy-start.6
  49.0 2.3 %fusion.26 = f32[4,1,1024]{2,1,0:T(1,128)S(1)} fusion(f32[4,128,1]{1,2,0:T(1,128)S(1)} %bitcast.87, bf16[1024,512]{1,0:T(8,128)(2,1)} %param.5), kind=kOutput, calls=%fused_computation.41 | convolution fusion | flops 3670016 | bytes 1067008 | tf_op jit(solution)/shard_map/thd,hd->th/dot_general | solution.py:97
  51.3 0.0 copy-done.6
  51.3 3.7 %fusion.92 = (f32[4,512]{1,0:T(4,128)S(1)}, f32[4,512,512]{1,2,0:T(8,128)}) fusion(pred[512,512]{0,1:T(8,128)(4,1)S(1)} %iota_compare_fusion.1, bf16[512,4,128]{0,2,1:T(8,128)(2,1)S(1)} %bitcast.84, bf16[512,4,128]{0,2,1:T(8,128)(2,1)S(1)} %bitcast.85), kind=kOutput, calls=%fused_computation.129 | convolution fusion | flops 272630272 | bytes 5513216 | tf_op jit(solution)/shard_map/sub | solution.py:67
  55.0 0.0 copy-start.9
  55.0 1.3 fusion.31
  56.3 0.9 copy-done.9
  57.2 0.0 copy-start.7
  57.2 1.5 fusion.24
  58.7 0.0 copy-done.7
  58.7 5.9 %fusion.91 = (f32[4,512]{1,0:T(4,128)S(1)}, f32[4,512,1024]{2,1,0:T(8,128)}) fusion(f32[4,512,1024]{2,1,0:T(8,128)S(1)} %fusion.31, pred[512,1024]{1,0:T(8,128)(4,1)S(1)} %copy-done.7), kind=kOutput, calls=%fused_computation.128 | output fusion | flops 12583935 | bytes 17309696 | tf_op jit(solution)/shard_map/sub | solution.py:67
  64.6 0.0 copy-start.8
  64.6 0.0 copy-start.2
  64.6 0.0 all-gather.6.cloned.1.call-done
  64.6 2.4 %fusion.50 = (f32[1,4,128,128]{3,2,1,0:T(8,128)}, f32[4,128,128]{2,1,0:T(8,128)S(1)}) fusion(f32[32,128,128]{2,1,0:T(8,128)} %all-gather.6.cloned.1.call-done), kind=kLoop, calls=%fused_computation.66 | loop fusion | flops 458752 | bytes 2621440 | tf_op jit(solution)/shard_map/add | solution.py:42
  67.0 0.0 all-gather.4.cloned.1.call-update
  67.1 0.2 reduce-scatter.2.cloned.1.call-start
  67.3 0.0 copy-done.8
  67.3 0.0 copy-done.2
  67.3 0.0 copy-start.3
  67.3 0.0 copy-start.5
  67.4 6.1 %fusion.25 = f32[512,4,128]{0,2,1:T(8,128)} fusion(f32[4,512,1024]{2,1,0:T(8,128)} %get-tuple-element.14, f32[4,512]{1,0:T(4,128)S(1)} %get-tuple-element.13, bf16[1024,512]{1,0:T(8,128)(2,1)S(1)} %copy-done.2), kind=kOutput, calls=%fused_computation.40 | convolution fusion | flops 541065216 | bytes 10493952 | tf_op jit(solution)/shard_map/hqk,khd->qhd/dot_general | solution.py:70
  73.4 22.3 %all-gather.4.cloned.1.call-done = f32[4,4,128,128]{3,2,1,0:T(8,128)} async-done(((f32[1,4,128,128]{3,2,1,0:T(8,128)}), f32[4,4,128,128]{3,2,1,0:T(8,128)}) %all-gather.4.cloned.1.call-update) | async-done | bytes 1048592 | tf_op jit(solution)/shard_map/all_gather | solution.py:27
  95.7 0.0 copy-done.3
  95.7 0.0 copy-done.5
  95.7 0.0 copy-start.1
  95.8 4.0 %fusion.18 = bf16[1024,4,128]{0,2,1:T(8,128)(2,1)S(1)} fusion(f32[512,4,128]{0,2,1:T(8,128)} %fusion.25, f32[512,4,128]{0,2,1:T(8,128)} %fusion.24, f32[4]{0:T(128)S(1)} %get-tuple-element.9, f32[1024,4]{0,1:T(4,128)S(1)} %fusion.77, f32[4]{0:T(128)S(1)} %get-tuple-element.10, f32[4,4,128,128]{3,2,1,0:T(8,128)} %all-gather.4.cloned.1.call-done, ...), kind=kOutput, calls=%fused_computation.30 | convolution fusion | flops 141361152 | bytes 7356460 | tf_op jit(solution)/shard_map/thd,hde->the/dot_general | solution.py:96
  99.8 0.0 copy-done.1
  99.8 8.1 %fusion.93 = f32[1024,4096]{1,0:T(8,128)} fusion(bf16[1024,512]{0,1:T(8,128)(2,1)S(1)} %bitcast.82, bf16[512,4096]{1,0:T(8,128)(2,1)S(1)} %copy-done.1), kind=kOutput, calls=%fused_computation.130 | convolution fusion | flops 4294967296 | bytes 22020096 | tf_op jit(solution)/shard_map/dot_general | solution.py:102
  107.9 0.0 reduce-scatter.2.cloned.1.call-update
  107.9 95.1 %reduce-scatter.2.cloned.1.call-done = f32[1024,512]{1,0:T(8,128)} async-done(((f32[1024,4096]{1,0:T(8,128)}), f32[1024,512]{1,0:T(8,128)}) %reduce-scatter.2.cloned.1.call-update) | async-done | bytes 2097168 | tf_op jit(solution)/shard_map/reduce_scatter | solution.py:103
  203.0 2.7 %convert_element_type.32 = bf16[1024,512]{1,0:T(8,128)(2,1)} convert(f32[1024,512]{1,0:T(8,128)} %reduce-scatter.2.cloned.1.call-done) | non-fusion elementwise | flops 524288 | bytes 3145728 | tf_op jit(solution)/shard_map/convert_element_type | solution.py:104
  (5 shorter events, 0.0 us)
Async XLA Ops:
  6.5 58.1 %all-gather.6.cloned.1.call-start = ((), (), s32[]{:S(2)}) async-start(), calls=%async_computation.3 | async-start | bytes 2359296 | tf_op jit(solution)/shard_map/all_gather | solution.py:27
  10.0 1.2 copy-start.4
  10.0 85.8 %all-gather.4.cloned.1.call-start = ((), (), s32[]{:S(2)}) async-start(), calls=%async_computation.1 | async-start | bytes 1310720 | tf_op jit(solution)/shard_map/all_gather | solution.py:27
  11.2 3.2 %slice-start = ((bf16[1024,512]{1,0:T(8,128)(2,1)}), bf16[512,512]{1,0:T(8,128)(2,1)S(1)}, s32[]{:S(2)}) async-start(bf16[1024,512]{1,0:T(8,128)(2,1)} %param.6), calls=%async_computation.4 | async-start | bytes 1048576 | tf_op jit(solution)/shard_map/slice | solution.py:57
  12.1 2.6 %slice-start.1 = ((bf16[1024,512]{1,0:T(8,128)(2,1)}), bf16[512,512]{1,0:T(8,128)(2,1)S(1)}, s32[]{:S(2)}) async-start(bf16[1024,512]{1,0:T(8,128)(2,1)} %param.7), calls=%async_computation.5 | async-start | bytes 1048576 | tf_op jit(solution)/shard_map/slice | solution.py:73
  12.1 2.8 %copy-start = (bf16[1024,512]{1,0:T(8,128)(2,1)S(1)}, bf16[1024,512]{1,0:T(8,128)(2,1)}, u32[]{:S(2)}) copy-start(bf16[1024,512]{1,0:T(8,128)(2,1)} %param.6) | copy-start | bytes 3145732
  49.0 2.3 %copy-start.6 = (bf16[512,512]{0,1:T(8,128)(2,1)S(1)}, bf16[512,512]{0,1:T(8,128)(2,1)}, u32[]{:S(2)}) copy-start(bf16[512,512]{0,1:T(8,128)(2,1)} %copy.70) | copy-start | bytes 1572868
  55.0 2.2 %copy-start.9 = (f32[4,512,512]{1,2,0:T(8,128)S(1)}, f32[4,512,512]{1,2,0:T(8,128)}, u32[]{:S(2)}) copy-start(f32[4,512,512]{1,2,0:T(8,128)} %get-tuple-element.16) | copy-start | bytes 12582916
  57.2 1.5 copy-start.7
  64.6 2.7 %copy-start.8 = (f32[4]{0:T(128)S(1)}, f32[4]{0:T(128)}, u32[]{:S(2)}) copy-start(f32[4]{0:T(128)} %param.8) | copy-start | bytes 52
  64.6 2.7 %copy-start.2 = (bf16[1024,512]{1,0:T(8,128)(2,1)S(1)}, bf16[1024,512]{1,0:T(8,128)(2,1)}, u32[]{:S(2)}) copy-start(bf16[1024,512]{1,0:T(8,128)(2,1)} %param.7) | copy-start | bytes 3145732
  67.1 136.0 %reduce-scatter.2.cloned.1.call-start = ((), (), s32[]{:S(2)}) async-start(), calls=%async_computation.2 | async-start | bytes 18874368 | tf_op jit(solution)/shard_map/reduce_scatter | solution.py:103
  67.3 28.4 %copy-start.3 = (f32[1,4,128,128]{3,2,1,0:T(8,128)S(1)}, f32[1,4,128,128]{3,2,1,0:T(8,128)}, u32[]{:S(2)}) copy-start(f32[1,4,128,128]{3,2,1,0:T(8,128)} %get-tuple-element.5) | copy-start | bytes 786436
  67.3 28.4 %copy-start.5 = (bf16[1024,512]{1,0:T(8,128)(2,1)S(1)}, bf16[1024,512]{1,0:T(8,128)(2,1)}, u32[]{:S(2)}) copy-start(bf16[1024,512]{1,0:T(8,128)(2,1)} %param.5) | copy-start | bytes 3145732
  95.7 4.0 %copy-start.1 = (bf16[512,4096]{1,0:T(8,128)(2,1)S(1)}, bf16[512,4096]{1,0:T(8,128)(2,1)}, u32[]{:S(2)}) copy-start(bf16[512,4096]{1,0:T(8,128)(2,1)} %param.9) | copy-start | bytes 12582916
Sparse Core Ops, SparseCore 0:
  10.1 41.3 all-gather.5
  67.2 28.5 all-gather.3
  108.0 94.9 reduce-scatter.1
where the time goes:
time: 213 us; the launch traced here: 212 us
  waiting for transfers between devices  118 us (55%)
  blocking collectives  31.9 us (15%)
  matrix products  30.3 us (14%)
  other arithmetic  13.3 us (6%)
  between operations  13.3 us (6%)
  local copies, waits for them, and re-layouts  5.71 us (3%)
    reduce_scatter x1, waiting for transfers between devices, local(): lax.psum_scatter(partial_terms, 'heads', scatter_dimension=1, tiled=True)  95.1 us
    all_gather x2, blocking collectives, entering(): pieces = jax.tree.map(lambda part: lax.all_gather(part, axis), subtotal)  31.9 us
    all_gather x2, waiting for transfers between devices, entering(): pieces = jax.tree.map(lambda part: lax.all_gather(part, axis), subtotal)  22.3 us
    dot_general x1, matrix products, local(): jnp.dot(attended, out_weight, preferred_element_type=jnp.float32)  8.11 us
    dot_general x2, matrix products, local_attention(): jnp.einsum('hqk,khd->qhd', probabilities, value_heads[:key_end], preferre...  7.52 us
    sub x1, other arithmetic, local_attention(): weights = jnp.exp(scores - row_max)  5.95 us
    unnamed x24, local copies, waits for them, and re-layouts  4.84 us
  transfers between devices with their start and end apart: 3, of which 2 were waited for; matrix products, arithmetic and copies ran while one was open for 13% of the time, Pallas kernels for 0%

commit v1 on v0

v1 whole, which is shorter than its diff:
```python
import functools
import math

import jax
import jax.numpy as jnp
from jax import lax
from jax.experimental import pallas as pl
from jax.experimental.pallas import tpu as pltpu
from jax.sharding import Mesh
from jax.sharding import PartitionSpec as P

HD = 128
PACK = 144
QB = 256
NT = (((1,), (1,)), ((), ()))
TN = (((0,), (0,)), ((), ()))
F32 = jnp.float32
BF16 = jnp.bfloat16


def features(v):
    return jnp.where(v > 0, v + 1.0, jnp.exp(jnp.minimum(v, 0.0)))


def delta_kernel(k_ref, v_ref, o_ref):
    feat = features(k_ref[...].astype(F32))
    o_ref[0, :HD, :] = lax.dot_general(
        v_ref[...], feat.astype(BF16), TN, preferred_element_type=F32
    )
    total = jnp.sum(feat, axis=0, keepdims=True)
    o_ref[0, HD:, :] = jnp.broadcast_to(total, (PACK - HD, HD))


def delta(keys, values):
    rows, cols = keys.shape
    heads = cols // HD
    spec = pl.BlockSpec((rows, HD), lambda h: (0, h))
    return pl.pallas_call(
        delta_kernel,
        grid=(heads,),
        in_specs=[spec, spec],
        out_specs=pl.BlockSpec((1, PACK, HD), lambda h: (h, 0, 0)),
        out_shape=jax.ShapeDtypeStruct((heads, PACK, HD), F32),
        name="delta",
    )(keys, values)


def attention_kernel(q_ref, k_ref, v_ref, o_ref):
    rows = q_ref.shape[0]
    c = math.log2(math.e) / math.sqrt(HD)
    causal = lax.broadcasted_iota(jnp.int32, (QB, QB), 1) <= lax.broadcasted_iota(
        jnp.int32, (QB, QB), 0
    )
    for i in range(rows // QB):
        lo, hi = i * QB, (i + 1) * QB
        q = q_ref[lo:hi, :]
        diag = lax.dot_general(q, k_ref[lo:hi, :], NT, preferred_element_type=F32)
        diag = jnp.where(causal, diag, -1e30)
        top = jnp.max(diag, axis=-1, keepdims=True)
        if lo:
            off = lax.dot_general(q, k_ref[:lo, :], NT, preferred_element_type=F32)
            top = jnp.maximum(top, jnp.max(off, axis=-1, keepdims=True))
        w = jnp.exp2((diag - top) * c)
        norm = jnp.sum(w, axis=-1, keepdims=True)
        out = jnp.dot(w.astype(BF16), v_ref[lo:hi, :], preferred_element_type=F32)
        if lo:
            w = jnp.exp2((off - top) * c)
            norm += jnp.sum(w, axis=-1, keepdims=True)
            out += jnp.dot(w.astype(BF16), v_ref[:lo, :], preferred_element_type=F32)
        o_ref[lo:hi, :] = out / norm


def attention(queries, keys, values, first, count):
    rows = queries.shape[0]
    spec = pl.BlockSpec((rows, HD), lambda h: (0, first + h))
    return pl.pallas_call(
        attention_kernel,
        grid=(count,),
        in_specs=[spec] * 3,
        out_specs=pl.BlockSpec((rows, HD), lambda h: (0, h)),
        out_shape=jax.ShapeDtypeStruct((rows, count * HD), F32),
        name="attention",
    )(queries, keys, values)


def retrieve_kernel(q_ref, la_ref, lb_ref, s_ref, g_ref, o_ref):
    heads = s_ref.shape[0]
    half = heads // 2
    for h in range(heads):
        cols = slice(h * HD, (h + 1) * HD)
        feat = features(q_ref[:, cols].astype(F32)).astype(BF16)
        got = lax.dot_general(feat, s_ref[h], NT, preferred_element_type=F32)
        denom = jnp.maximum(got[:, HD : HD + 1], 1.0)
        gate = g_ref[:, cols]
        src = la_ref if h < half else lb_ref
        at = h % half
        local = src[:, at * HD : (at + 1) * HD]
        mixed = gate * (got[:, :HD] / denom) + (1.0 - gate) * local
        o_ref[:, cols] = mixed.astype(BF16)


def retrieve(queries, local_a, local_b, state, gate):
    rows, cols = queries.shape
    heads = cols // HD
    block = 256
    return pl.pallas_call(
        retrieve_kernel,
        grid=(rows // block,),
        in_specs=[
            pl.BlockSpec((block, cols), lambda i: (i, 0)),
            pl.BlockSpec((block, cols // 2), lambda i: (i, 0)),
            pl.BlockSpec((block, cols // 2), lambda i: (i, 0)),
            pl.BlockSpec((heads, PACK, HD), lambda i: (0, 0, 0)),
            pl.BlockSpec((1, cols), lambda i: (0, 0)),
        ],
        out_specs=pl.BlockSpec((block, cols), lambda i: (i, 0)),
        out_shape=jax.ShapeDtypeStruct((rows, cols), BF16),
        name="retrieve",
    )(queries, local_a, local_b, state, gate)


def project_kernel(n_add, *refs):
    (ao1, as1, wo1, ws1, ao2, as2, wo2, ws2) = refs[:8]
    adds = refs[8 : 8 + 2 * n_add]
    outs = refs[8 + 2 * n_add :]
    for side, (ao, asb, wo, ws) in enumerate(((ao1, as1, wo1, ws1), (ao2, as2, wo2, ws2))):
        total = jnp.dot(ao[...], wo[0], preferred_element_type=F32)
        total += jnp.dot(asb[...], ws[0], preferred_element_type=F32)
        for j in range(n_add):
            total += adds[2 * j + side][...].astype(F32)
        outs[side][...] = total.astype(outs[side].dtype)


def project(a_own, a_sib, w_own, w_sib, pick, adds, dtype):
    rows, depth = a_own.shape
    width = w_own.shape[2]
    block = 256
    steps = rows // 2 // block
    half = pl.BlockSpec((block, width), lambda i: (i, 0))
    specs, args = [], []
    for side in range(2):
        a_spec = pl.BlockSpec((block, depth), functools.partial(lambda s, i: (s * steps + i, 0), side))
        w_spec = pl.BlockSpec((1, depth, width), functools.partial(lambda k, i: (k, 0, 0), pick[side]))
        specs += [a_spec, a_spec, w_spec, w_spec]
        args += [a_own, a_sib, w_own, w_sib]
    for pair in adds:
        specs += [half, half]
        args += list(pair)
    return pl.pallas_call(
        functools.partial(project_kernel, len(adds)),
        grid=(steps,),
        in_specs=specs,
        out_specs=[half, half],
        out_shape=[jax.ShapeDtypeStruct((rows // 2, width), dtype)] * 2,
        name="project",
    )(*args)


def finish_kernel(steps, p1, p2, r1, r2, o_ref):
    first = pl.program_id(0) < steps

    @pl.when(first)
    def _():
        o_ref[...] = (p1[...] + r1[...].astype(F32)).astype(o_ref.dtype)

    @pl.when(jnp.logical_not(first))
    def _():
        o_ref[...] = (p2[...] + r2[...].astype(F32)).astype(o_ref.dtype)


def finish(p1, p2, r1, r2):
    rows, width = p1.shape
    block = 256
    steps = rows // block
    one = pl.BlockSpec((block, width), lambda i: (jnp.minimum(i, steps - 1), 0))
    two = pl.BlockSpec((block, width), lambda i: (jnp.maximum(i - steps, 0), 0))
    return pl.pallas_call(
        functools.partial(finish_kernel, steps),
        grid=(2 * steps,),
        in_specs=[one, two, one, two],
        out_specs=pl.BlockSpec((block, width), lambda i: (i, 0)),
        out_shape=jax.ShapeDtypeStruct((2 * rows, width), BF16),
        name="finish",
    )(p1, p2, r1, r2)


def swap(array, axis, mask):
    size = lax.axis_size(axis)
    return lax.ppermute(array, axis, [(i, i ^ mask) for i in range(size)])


def entering(own):
    y, z = lax.axis_index("y"), lax.axis_index("z")
    total, before = own, jnp.zeros_like(own)
    for axis, mine, masks in (("z", z, (1, 2, 3)), ("z", z, (4,)), ("y", y, (1, 2, 3))):
        sent = total.astype(BF16)
        got = [swap(sent, axis, m).astype(F32) for m in masks]
        for m, g in zip(masks, got):
            before = before + jnp.where((mine ^ m) < mine, g, 0.0)
            total = total + g
    return before.astype(BF16)


def local(queries, keys, values, gate_bias, out_weight):
    x, c = lax.axis_index("x"), lax.axis_index("c")
    width = out_weight.shape[1] // 8
    own = delta(keys, values)
    state = entering(own)

    def columns(core):
        return jnp.stack(
            [
                lax.dynamic_slice_in_dim(out_weight, ((x ^ k) * 2 + core) * width, width, 1)
                for k in range(4)
            ]
        )

    w_own = columns(c)
    w_sib = swap(columns(1 - c), "c", 1)
    heads = gate_bias.shape[0]
    local_a = attention(queries, keys, values, 0, heads // 2)
    local_b = attention(queries, keys, values, heads // 2, heads // 2)
    gate = jnp.repeat(jax.nn.sigmoid(gate_bias), HD)[None, :]
    a_own = retrieve(queries, local_a, local_b, state, gate)
    a_sib = swap(a_own, "c", 1)

    mm = functools.partial(project, a_own, a_sib, w_own, w_sib)
    far1, far2 = mm((2, 2), (), BF16)
    far1, far2 = swap(far1, "x", 1), swap(far2, "x", 3)
    near1, near2 = mm((1, 3), (), BF16)
    near1, near2 = swap(near1, "x", 1), swap(near2, "x", 3)
    pass1, pass2 = mm((3, 1), ((far1, far2),), BF16)
    pass1, pass2 = swap(pass1, "x", 3), swap(pass2, "x", 1)
    mine1, mine2 = mm((0, 0), ((near1, near2),), F32)
    return finish(mine1, mine2, pass1, pass2)


def solution(mesh):
    finer = Mesh(mesh.devices.reshape(4, 8, 4, 2), ("y", "z", "x", "c"))
    rows, cols = ("y", "z"), ("x", "c")
    placed = (P(rows, cols), P(rows, cols), P(rows, cols), P(cols), P(cols, None))
    return jax.shard_map(
        local, mesh=finer, in_specs=placed, out_specs=P(rows, cols), check_vma=False
    )
```

time: 213 us -> 110 us (0.52)
  waiting for transfers between devices: 118 us -> 26.7 us
  Pallas kernels: 0 us -> 40.9 us
  blocking collectives: 31.9 us -> 0 us
  matrix products: 30.3 us -> 0 us
  starting transfers between devices: 0.27 us -> 26.3 us
  between operations: 13.3 us -> 0.05 us
  other arithmetic: 13.3 us -> 6.69 us
  local copies, waits for them, and re-layouts: 5.71 us -> 9.27 us
    reduce_scatter x1 -> x0, waiting for transfers between devices: 95.1 us -> none  [local(): lax.psum_scatter(partial_terms, 'heads', scatter_dimension=1, tiled=True)]
    pallas_call x0 -> x9, Pallas kernels: none -> 40.9 us  [the longest x4 17.4 us: project(): pl.pallas_call(functools.partial(project_kernel, len(adds)), grid=(steps,...]
    all_gather x2 -> x0, blocking collectives: 31.9 us -> none  [entering(): pieces = jax.tree.map(lambda part: lax.all_gather(part, axis), subtotal)]
    ppermute x0 -> x15, waiting for transfers between devices: none -> 26.7 us  [swap(): return lax.ppermute(array, axis, [(i, i ^ mask) for i in range(size)])]
    dot_general x7 -> x0, matrix products: 26.7 us -> none  [the longest x1 8.11 us: local(): jnp.dot(attended, out_weight, preferred_element_type=jnp.float32)]
    ppermute x0 -> x15, starting transfers between devices: none -> 26.3 us  [swap(): return lax.ppermute(array, axis, [(i, i ^ mask) for i in range(size)])]
    all_gather x2 -> x0, waiting for transfers between devices: 22.3 us -> none  [entering(): pieces = jax.tree.map(lambda part: lax.all_gather(part, axis), subtotal)]
    sub x2 -> x0, other arithmetic: 5.96 us -> none  [the longest x1 5.95 us: local_attention(): weights = jnp.exp(scores - row_max)]
  transfers between devices with their start and end apart: 3 -> 15, of which waited for: 2 -> 9; matrix products, arithmetic and copies ran while one was open for 13% -> 9% of each run, Pallas kernels for 0% -> 26%
where the time goes in v1:
time: 110 us
  Pallas kernels  40.9 us (37%)
  waiting for transfers between devices  26.7 us (24%)
  starting transfers between devices  26.3 us (24%)
  local copies, waits for them, and re-layouts  9.27 us (8%)
  other arithmetic  6.69 us (6%)
    ppermute x15, waiting for transfers between devices, swap(): return lax.ppermute(array, axis, [(i, i ^ mask) for i in range(size)])  26.7 us
    ppermute x15, starting transfers between devices, swap(): return lax.ppermute(array, axis, [(i, i ^ mask) for i in range(size)])  26.3 us
    pallas_call x4, Pallas kernels, project(): pl.pallas_call(functools.partial(project_kernel, len(adds)), grid=(steps,...  17.4 us
    pallas_call x2, Pallas kernels, attention(): pl.pallas_call(attention_kernel, grid=(count,), in_specs=[spec] * 3, out_...  10.8 us
    unnamed x20, local copies, waits for them, and re-layouts  4.87 us
    another operation x2, other arithmetic, columns(): jnp.stack([lax.dynamic_slice_in_dim(out_weight, ((x ^ k) * 2 + core) * wi...  4.68 us
    pallas_call x1, Pallas kernels, retrieve(): pl.pallas_call(retrieve_kernel, grid=(rows // block,), in_specs=[pl.Block...  4.61 us
    pallas_call x1, Pallas kernels, finish(): pl.pallas_call(functools.partial(finish_kernel, steps), grid=(2 * steps,)...  4.05 us
  transfers between devices with their start and end apart: 15, of which 9 were waited for; matrix products, arithmetic and copies ran while one was open for 9% of the time, Pallas kernels for 26%

profile of v1, /device:TPU:1, one launch (start us, length us, event | category | flops | bytes accessed | tf_op | source)
XLA Modules:
  0.0 109.9 jit_solution(15418197936796003358)
XLA Ops:
  0.0 4.0 %delta.1 = f32[4,144,128]{2,1,0:T(8,128)} custom-call(bf16[1024,512]{1,0:T(8,128)(2,1)} %k_ref.5, bf16[1024,512]{1,0:T(8,128)(2,1)} %v_ref.5), custom_call_target="tpu_custom_call" | custom-call | tf_op jit(solution)/shard_map/delta/pallas_call | solution.py:38
  4.0 1.0 convert_element_type.33
  5.0 5.3 %collective-permute-start.2 = (bf16[4,144,128]{2,1,0:T(8,128)(2,1)S(1)}, bf16[4,144,128]{2,1,0:T(8,128)(2,1)S(1)}, u32[]{:S(2)}, u32[]{:S(2)}) collective-permute-start(bf16[4,144,128]{2,1,0:T(8,128)(2,1)S(1)} %convert_element_type.33), channel_id=1, source_target_pairs={{0,24},{8,16},{16,8},{24,0},{32,56},{40,48},{48,40},{56,32},{1,25}... | collective-permute-start | bytes 442376 | tf_op jit(solution)/shard_map/ppermute | solution.py:189
  10.3 0.0 collective-permute-start.1
  10.3 0.4 collective-permute-start
  10.7 3.8 %dynamic-slice_bitcast_fusion.3 = (bf16[1,512,512]{2,1,0:T(8,128)(2,1)S(1)}, bf16[1,512,512]{2,1,0:T(8,128)(2,1)S(1)}, bf16[1,512,512]{2,1,0:T(8,128)(2,1)}, bf1...) fusion(bf16[512,4096]{1,0:T(8,128)(2,1)} %param.9, ...), kind=kLoop, calls=%fused_computation.5 | loop fusion | bytes 8388640 | tf_op jit(solution)/shard_map/stack | solution.py:211
  14.4 0.0 copy-start.2
  14.4 1.6 %pad_maximum_fusion.1 = bf16[4,512,512]{2,1,0:T(8,128)(2,1)} fusion(bf16[1,512,512]{2,1,0:T(8,128)(2,1)S(1)} %get-tuple-element.27, bf16[1,512,512]{2,1,0:T(8,128)(2,1)S(1)} %get-tuple-element.28, bf16[1,512,512]{2,1,0:T(8,128)(2,1)S(1)} %get-tuple-element.22, bf16[1,512,512]{2,1,0:T(8,128)(2,1)S(1)} %get-tuple-element.21), kind=kLoop, calls=%fused_computation.1 | loop fusion | flops 3145728 | bytes 4194304 | tf_op jit(solution)/shard_map/stack | solution.py:211
  16.0 2.1 %collective-permute-start.8 = (bf16[4,512,512]{2,1,0:T(8,128)(2,1)}, bf16[4,512,512]{2,1,0:T(8,128)(2,1)S(1)}, u32[]{:S(2)}, u32[]{:S(2)}) collective-permute-start(bf16[4,512,512]{2,1,0:T(8,128)(2,1)} %pad_maximum_fusion.1), channel_id=1, source_target_pairs={{0,1},{1,0},{2,3},{3,2},{4,5},{5,4},{6,7},{7,6},{8,9},{9,8},{10,11... | collective-permute-start | bytes 6291464 | tf_op jit(solution)/shard_map/ppermute | solution.py:189
  18.0 0.0 collective-permute-done.2
  18.1 3.8 %collective-permute-done.1 = bf16[4,144,128]{2,1,0:T(8,128)(2,1)S(1)} collective-permute-done((bf16[4,144,128]{2,1,0:T(8,128)(2,1)S(1)}, bf16[4,144,128]{2,1,0:T(8,128)(2,1)S(1)}, u32[]{:S(2)}, u32[]{:S(2)}) %collective-permute-start.1) | collective-permute-done | bytes 147488 | tf_op jit(solution)/shard_map/ppermute | solution.py:189
  21.9 0.0 collective-permute-done
  21.9 0.0 copy-done.2
  21.9 0.1 fusion.8
  22.0 5.7 %collective-permute-start.3 = (bf16[4,144,128]{2,1,0:T(8,128)(2,1)S(1)}, bf16[4,144,128]{2,1,0:T(8,128)(2,1)S(1)}, u32[]{:S(2)}, u32[]{:S(2)}) collective-permute-start(bf16[4,144,128]{2,1,0:T(8,128)(2,1)S(1)} %fusion.8), channel_id=1, source_target_pairs={{0,32},{8,40},{16,48},{24,56},{32,0},{40,8},{48,16},{56,24},{1,33}... | collective-permute-start | bytes 442376 | tf_op jit(solution)/shard_map/ppermute | solution.py:189
  27.7 5.4 %attention.2.la_ref = f32[1024,256]{1,0:T(8,128)} custom-call(bf16[1024,512]{1,0:T(8,128)(2,1)} %q_ref.5, bf16[1024,512]{1,0:T(8,128)(2,1)} %k_ref.5, bf16[1024,512]{1,0:T(8,128)(2,1)} %v_ref.5), custom_call_target="tpu_custom_call" | custom-call | tf_op jit(solution)/shard_map/attention/pallas_call | solution.py:76
  33.0 0.0 copy-start.9
  33.0 5.4 %attention.3.lb_ref = f32[1024,256]{1,0:T(8,128)} custom-call(bf16[1024,512]{1,0:T(8,128)(2,1)} %q_ref.5, bf16[1024,512]{1,0:T(8,128)(2,1)} %k_ref.5, bf16[1024,512]{1,0:T(8,128)(2,1)} %v_ref.5), custom_call_target="tpu_custom_call" | custom-call | tf_op jit(solution)/shard_map/attention/pallas_call | solution.py:76
  38.4 0.0 collective-permute-done.3
  38.4 0.1 fusion.7
  38.5 2.8 %collective-permute-start.6 = (bf16[4,144,128]{2,1,0:T(8,128)(2,1)S(1)}, bf16[4,144,128]{2,1,0:T(8,128)(2,1)S(1)}, u32[]{:S(2)}, u32[]{:S(2)}) collective-permute-start(bf16[4,144,128]{2,1,0:T(8,128)(2,1)S(1)} %fusion.7), channel_id=1, source_target_pairs={{0,192},{64,128},{128,64},{192,0},{1,193},{65,129},{129,65},{193,1... | collective-permute-start | bytes 442376 | tf_op jit(solution)/shard_map/ppermute | solution.py:189
  41.4 0.4 collective-permute-start.5
  41.7 0.3 collective-permute-start.4
  42.0 0.0 copy-done.9
  42.0 4.2 %collective-permute-done.6 = bf16[4,144,128]{2,1,0:T(8,128)(2,1)S(1)} collective-permute-done((bf16[4,144,128]{2,1,0:T(8,128)(2,1)S(1)}, bf16[4,144,128]{2,1,0:T(8,128)(2,1)S(1)}, u32[]{:S(2)}, u32[]{:S(2)}) %collective-permute-start.6) | collective-permute-done | bytes 147488 | tf_op jit(solution)/shard_map/ppermute | solution.py:189
  46.3 0.7 collective-permute-done.5
  47.0 0.2 collective-permute-done.4
  47.2 0.9 fusion.6.s_ref
  48.0 0.6 broadcast_in_dim.14
  48.7 4.6 %retrieve.1.refs_0_.refs_4_ = bf16[1024,512]{1,0:T(8,128)(2,1)} custom-call(bf16[1024,512]{1,0:T(8,128)(2,1)} %q_ref.5, f32[1024,256]{1,0:T(8,128)} %attention.2.la_ref, f32[1024,256]{1,0:T(8,128)} %attention.3.lb_ref, bf16[4,144,128]{2,1,0:T(8,128)(2,1)} %fusion.6.s_ref, f32[1,512]{1,0:T(1,128)} %bitcast.17), custom_call_target="tpu_custom_call" | custom-call | tf_op jit(solution)/shard_map/retrieve/pallas_call | solution.py:106
  53.3 3.6 %collective-permute-start.7 = (bf16[1024,512]{1,0:T(8,128)(2,1)}, bf16[1024,512]{1,0:T(8,128)(2,1)S(1)}, u32[]{:S(2)}, u32[]{:S(2)}) collective-permute-start(bf16[1024,512]{1,0:T(8,128)(2,1)} %retrieve.1.refs_0_.refs_4_), channel_id=1, source_target_pairs={{0,1},{1,0},{2,3},{3,2},{4,5},{5,4},{6,7},{7,6},{8,9},{9,8},{10,11... | collective-permute-start | bytes 3145736 | tf_op jit(solution)/shard_map/ppermute | solution.py:189
  56.9 3.1 %pad_maximum_fusion.refs_2_.refs_6_ = bf16[4,512,512]{2,1,0:T(8,128)(2,1)} fusion(bf16[1,512,512]{2,1,0:T(8,128)(2,1)} %get-tuple-element.23, bf16[1,512,512]{2,1,0:T(8,128)(2,1)} %get-tuple-element.24, bf16[1,512,512]{2,1,0:T(8,128)(2,1)} %get-tuple-element.25, bf16[1,512,512]{2,1,0:T(8,128)(2,1)} %get-tuple-element.26), kind=kLoop, calls=%fused_computation | loop fusion | flops 3145728 | bytes 4194304 | tf_op jit(solution)/shard_map/stack | solution.py:211
  60.0 0.0 collective-permute-done.7.refs_1_.refs_5_
  60.0 0.0 copy-start.1
  60.0 0.0 collective-permute-done.8.refs_3_.refs_7_
  60.0 1.0 copy-done.1
  61.0 0.0 copy-start
  61.0 1.3 %copy-done = bf16[4,512,512]{2,1,0:T(8,128)(2,1)} copy-done((bf16[4,512,512]{2,1,0:T(8,128)(2,1)}, bf16[4,512,512]{2,1,0:T(8,128)(2,1)S(1)}, u32[]{:S(2)}) %copy-start) | copy-done | bytes 2097176
  62.3 4.3 %project.6 = (bf16[512,512]{1,0:T(8,128)(2,1)}, bf16[512,512]{1,0:T(8,128)(2,1)}) custom-call(bf16[1024,512]{1,0:T(8,128)(2,1)} %retrieve.1.refs_0_.refs_4_, bf16[1024,512]{1,0:T(8,128)(2,1)} %copy-done.1, bf16[4,512,512]{2,1,0:T(8,128)(2,1)} %pad_maximum_fusion.refs_2_.refs_6_, bf16[4,512,512]{2,1,0:T(8,128)(2,1)} %copy-done, ...), custom_call_target="tpu_custom_call" | custom-call | tf_op jit(solution)/shard_map/project/pallas_call | solution.py:149
  66.6 1.2 %collective-permute-start.11 = (bf16[512,512]{1,0:T(8,128)(2,1)}, bf16[512,512]{1,0:T(8,128)(2,1)S(1)}, u32[]{:S(2)}, u32[]{:S(2)}) collective-permute-start(bf16[512,512]{1,0:T(8,128)(2,1)} %get-tuple-element.17), channel_id=1, source_target_pairs={{0,2},{2,0},{4,6},{6,4},{1,3},{3,1},{5,7},{7,5},{8,10},{10,8},{12,... | collective-permute-start | bytes 1572872 | tf_op jit(solution)/shard_map/ppermute | solution.py:189
  67.8 1.8 %collective-permute-start.12 = (bf16[512,512]{1,0:T(8,128)(2,1)}, bf16[512,512]{1,0:T(8,128)(2,1)S(1)}, u32[]{:S(2)}, u32[]{:S(2)}) collective-permute-start(bf16[512,512]{1,0:T(8,128)(2,1)} %get-tuple-element.18), channel_id=1, source_target_pairs={{0,6},{2,4},{4,2},{6,0},{1,7},{3,5},{5,3},{7,1},{8,14},{10,12},{12... | collective-permute-start | bytes 1572872 | tf_op jit(solution)/shard_map/ppermute | solution.py:189
  69.6 4.1 %project.4 = (bf16[512,512]{1,0:T(8,128)(2,1)}, bf16[512,512]{1,0:T(8,128)(2,1)}) custom-call(bf16[1024,512]{1,0:T(8,128)(2,1)} %retrieve.1.refs_0_.refs_4_, bf16[1024,512]{1,0:T(8,128)(2,1)} %copy-done.1, bf16[4,512,512]{2,1,0:T(8,128)(2,1)} %pad_maximum_fusion.refs_2_.refs_6_, bf16[4,512,512]{2,1,0:T(8,128)(2,1)} %copy-done, ...), custom_call_target="tpu_custom_call" | custom-call | tf_op jit(solution)/shard_map/project/pallas_call | solution.py:149
  73.7 0.3 collective-permute-start.9
  74.0 0.6 collective-permute-start.10
  74.7 5.7 %collective-permute-done.11.refs_8_ = bf16[512,512]{1,0:T(8,128)(2,1)S(1)} collective-permute-done((bf16[512,512]{1,0:T(8,128)(2,1)}, bf16[512,512]{1,0:T(8,128)(2,1)S(1)}, u32[]{:S(2)}, u32[]{:S(2)}) %collective-permute-start.11) | collective-permute-done | bytes 524320 | tf_op jit(solution)/shard_map/ppermute | solution.py:189
  80.3 0.0 copy-start.7
  80.3 2.1 %collective-permute-done.12.refs_9_ = bf16[512,512]{1,0:T(8,128)(2,1)S(1)} collective-permute-done((bf16[512,512]{1,0:T(8,128)(2,1)}, bf16[512,512]{1,0:T(8,128)(2,1)S(1)}, u32[]{:S(2)}, u32[]{:S(2)}) %collective-permute-start.12) | collective-permute-done | bytes 524320 | tf_op jit(solution)/shard_map/ppermute | solution.py:189
  82.4 0.0 copy-done.7
  82.4 0.0 copy-start.8
  82.4 0.8 copy-done.8
  83.2 4.4 %project.7 = (bf16[512,512]{1,0:T(8,128)(2,1)}, bf16[512,512]{1,0:T(8,128)(2,1)}) custom-call(bf16[1024,512]{1,0:T(8,128)(2,1)} %retrieve.1.refs_0_.refs_4_, bf16[1024,512]{1,0:T(8,128)(2,1)} %copy-done.1, bf16[4,512,512]{2,1,0:T(8,128)(2,1)} %pad_maximum_fusion.refs_2_.refs_6_, bf16[4,512,512]{2,1,0:T(8,128)(2,1)} %copy-done, ...), custom_call_target="tpu_custom_call" | custom-call | tf_op jit(solution)/shard_map/project/pallas_call | solution.py:149
  87.6 1.8 %collective-permute-start.13 = (bf16[512,512]{1,0:T(8,128)(2,1)}, bf16[512,512]{1,0:T(8,128)(2,1)S(1)}, u32[]{:S(2)}, u32[]{:S(2)}) collective-permute-start(bf16[512,512]{1,0:T(8,128)(2,1)} %get-tuple-element.19), channel_id=1, source_target_pairs={{0,6},{2,4},{4,2},{6,0},{1,7},{3,5},{5,3},{7,1},{8,14},{10,12},{12... | collective-permute-start | bytes 1572872 | tf_op jit(solution)/shard_map/ppermute | solution.py:189
  89.4 0.0 collective-permute-start.14
  89.5 2.1 %collective-permute-done.9.refs_8_ = bf16[512,512]{1,0:T(8,128)(2,1)S(1)} collective-permute-done((bf16[512,512]{1,0:T(8,128)(2,1)}, bf16[512,512]{1,0:T(8,128)(2,1)S(1)}, u32[]{:S(2)}, u32[]{:S(2)}) %collective-permute-start.9) | collective-permute-done | bytes 524320 | tf_op jit(solution)/shard_map/ppermute | solution.py:189
  91.6 0.0 copy-start.5
  91.6 2.1 %collective-permute-done.10.refs_9_ = bf16[512,512]{1,0:T(8,128)(2,1)S(1)} collective-permute-done((bf16[512,512]{1,0:T(8,128)(2,1)}, bf16[512,512]{1,0:T(8,128)(2,1)S(1)}, u32[]{:S(2)}, u32[]{:S(2)}) %collective-permute-start.10) | collective-permute-done | bytes 524320 | tf_op jit(solution)/shard_map/ppermute | solution.py:189
  93.7 0.0 copy-done.5
  93.7 0.8 copy-done.6
  94.5 4.7 %project.5 = (f32[512,512]{1,0:T(8,128)}, f32[512,512]{1,0:T(8,128)}) custom-call(bf16[1024,512]{1,0:T(8,128)(2,1)} %retrieve.1.refs_0_.refs_4_, bf16[1024,512]{1,0:T(8,128)(2,1)} %copy-done.1, bf16[4,512,512]{2,1,0:T(8,128)(2,1)} %pad_maximum_fusion.refs_2_.refs_6_, bf16[4,512,512]{2,1,0:T(8,128)(2,1)} %copy-done, ...), custom_call_target="tpu_custom_call" | custom-call | tf_op jit(solution)/shard_map/project/pallas_call | solution.py:149
  99.1 5.8 %collective-permute-done.13.r1 = bf16[512,512]{1,0:T(8,128)(2,1)S(1)} collective-permute-done((bf16[512,512]{1,0:T(8,128)(2,1)}, bf16[512,512]{1,0:T(8,128)(2,1)S(1)}, u32[]{:S(2)}, u32[]{:S(2)}) %collective-permute-start.13) | collective-permute-done | bytes 524320 | tf_op jit(solution)/shard_map/ppermute | solution.py:189
  104.9 0.0 collective-permute-done.14.r2
  104.9 0.8 copy-done.3
  105.7 0.2 copy-done.4
  105.9 4.0 %finish.1 = bf16[1024,512]{1,0:T(8,128)(2,1)} custom-call(f32[512,512]{1,0:T(8,128)} %get-tuple-element.15.p1, f32[512,512]{1,0:T(8,128)} %get-tuple-element.16.p2, bf16[512,512]{1,0:T(8,128)(2,1)} %copy-done.3, bf16[512,512]{1,0:T(8,128)(2,1)} %copy-done.4), custom_call_target="tpu_custom_call" | custom-call | tf_op jit(solution)/shard_map/finish/pallas_call | solution.py:177
  (4 shorter events, 0.0 us)
Async XLA Ops:
  5.0 13.0 %collective-permute-start.2 = (bf16[4,144,128]{2,1,0:T(8,128)(2,1)S(1)}, bf16[4,144,128]{2,1,0:T(8,128)(2,1)S(1)}, u32[]{:S(2)}, u32[]{:S(2)}) collective-permute-start(bf16[4,144,128]{2,1,0:T(8,128)(2,1)S(1)} %convert_element_type.33), channel_id=1, source_target_pairs={{0,24},{8,16},{16,8},{24,0},{32,56},{40,48},{48,40},{56,32},{1,25}... | collective-permute-start | bytes 442376 | tf_op jit(solution)/shard_map/ppermute | solution.py:189
  10.3 11.6 %collective-permute-start.1 = (bf16[4,144,128]{2,1,0:T(8,128)(2,1)S(1)}, bf16[4,144,128]{2,1,0:T(8,128)(2,1)S(1)}, u32[]{:S(2)}, u32[]{:S(2)}) collective-permute-start(bf16[4,144,128]{2,1,0:T(8,128)(2,1)S(1)} %convert_element_type.33), channel_id=1, source_target_pairs={{0,16},{8,24},{16,0},{24,8},{32,48},{40,56},{48,32},{56,40},{1,17}... | collective-permute-start | bytes 442376 | tf_op jit(solution)/shard_map/ppermute | solution.py:189
  10.3 11.6 %collective-permute-start = (bf16[4,144,128]{2,1,0:T(8,128)(2,1)S(1)}, bf16[4,144,128]{2,1,0:T(8,128)(2,1)S(1)}, u32[]{:S(2)}, u32[]{:S(2)}) collective-permute-start(bf16[4,144,128]{2,1,0:T(8,128)(2,1)S(1)} %convert_element_type.33), channel_id=1, source_target_pairs={{0,8},{8,0},{16,24},{24,16},{32,40},{40,32},{48,56},{56,48},{1,9},... | collective-permute-start | bytes 442376 | tf_op jit(solution)/shard_map/ppermute | solution.py:189
  14.4 7.5 %copy-start.2 = (f32[4,144,128]{2,1,0:T(8,128)S(1)}, f32[4,144,128]{2,1,0:T(8,128)}, u32[]{:S(2)}) copy-start(f32[4,144,128]{2,1,0:T(8,128)} %delta.1) | copy-start | bytes 884740
  16.0 44.0 %collective-permute-start.8 = (bf16[4,512,512]{2,1,0:T(8,128)(2,1)}, bf16[4,512,512]{2,1,0:T(8,128)(2,1)S(1)}, u32[]{:S(2)}, u32[]{:S(2)}) collective-permute-start(bf16[4,512,512]{2,1,0:T(8,128)(2,1)} %pad_maximum_fusion.1), channel_id=1, source_target_pairs={{0,1},{1,0},{2,3},{3,2},{4,5},{5,4},{6,7},{7,6},{8,9},{9,8},{10,11... | collective-permute-start | bytes 6291464 | tf_op jit(solution)/shard_map/ppermute | solution.py:189
  22.0 16.5 %collective-permute-start.3 = (bf16[4,144,128]{2,1,0:T(8,128)(2,1)S(1)}, bf16[4,144,128]{2,1,0:T(8,128)(2,1)S(1)}, u32[]{:S(2)}, u32[]{:S(2)}) collective-permute-start(bf16[4,144,128]{2,1,0:T(8,128)(2,1)S(1)} %fusion.8), channel_id=1, source_target_pairs={{0,32},{8,40},{16,48},{24,56},{32,0},{40,8},{48,16},{56,24},{1,33}... | collective-permute-start | bytes 442376 | tf_op jit(solution)/shard_map/ppermute | solution.py:189
  33.0 9.0 %copy-start.9 = (f32[4]{0:T(128)S(1)}, f32[4]{0:T(128)}, u32[]{:S(2)}) copy-start(f32[4]{0:T(128)} %param.8) | copy-start | bytes 52
  38.5 7.7 %collective-permute-start.6 = (bf16[4,144,128]{2,1,0:T(8,128)(2,1)S(1)}, bf16[4,144,128]{2,1,0:T(8,128)(2,1)S(1)}, u32[]{:S(2)}, u32[]{:S(2)}) collective-permute-start(bf16[4,144,128]{2,1,0:T(8,128)(2,1)S(1)} %fusion.7), channel_id=1, source_target_pairs={{0,192},{64,128},{128,64},{192,0},{1,193},{65,129},{129,65},{193,1... | collective-permute-start | bytes 442376 | tf_op jit(solution)/shard_map/ppermute | solution.py:189
  41.4 5.6 %collective-permute-start.5 = (bf16[4,144,128]{2,1,0:T(8,128)(2,1)S(1)}, bf16[4,144,128]{2,1,0:T(8,128)(2,1)S(1)}, u32[]{:S(2)}, u32[]{:S(2)}) collective-permute-start(bf16[4,144,128]{2,1,0:T(8,128)(2,1)S(1)} %fusion.7), channel_id=1, source_target_pairs={{0,128},{64,192},{128,0},{192,64},{1,129},{65,193},{129,1},{193,65... | collective-permute-start | bytes 442376 | tf_op jit(solution)/shard_map/ppermute | solution.py:189
  41.7 5.4 %collective-permute-start.4 = (bf16[4,144,128]{2,1,0:T(8,128)(2,1)S(1)}, bf16[4,144,128]{2,1,0:T(8,128)(2,1)S(1)}, u32[]{:S(2)}, u32[]{:S(2)}) collective-permute-start(bf16[4,144,128]{2,1,0:T(8,128)(2,1)S(1)} %fusion.7), channel_id=1, source_target_pairs={{0,64},{64,0},{128,192},{192,128},{1,65},{65,1},{129,193},{193,129... | collective-permute-start | bytes 442376 | tf_op jit(solution)/shard_map/ppermute | solution.py:189
  53.3 6.7 %collective-permute-start.7 = (bf16[1024,512]{1,0:T(8,128)(2,1)}, bf16[1024,512]{1,0:T(8,128)(2,1)S(1)}, u32[]{:S(2)}, u32[]{:S(2)}) collective-permute-start(bf16[1024,512]{1,0:T(8,128)(2,1)} %retrieve.1.refs_0_.refs_4_), channel_id=1, source_target_pairs={{0,1},{1,0},{2,3},{3,2},{4,5},{5,4},{6,7},{7,6},{8,9},{9,8},{10,11... | collective-permute-start | bytes 3145736 | tf_op jit(solution)/shard_map/ppermute | solution.py:189
  60.0 1.0 copy-start.1
  61.0 1.3 %copy-start = (bf16[4,512,512]{2,1,0:T(8,128)(2,1)}, bf16[4,512,512]{2,1,0:T(8,128)(2,1)S(1)}, u32[]{:S(2)}) copy-start(bf16[4,512,512]{2,1,0:T(8,128)(2,1)S(1)} %collective-permute-done.8.refs_3_.refs_7_) | copy-start | bytes 6291460
  66.6 13.8 %collective-permute-start.11 = (bf16[512,512]{1,0:T(8,128)(2,1)}, bf16[512,512]{1,0:T(8,128)(2,1)S(1)}, u32[]{:S(2)}, u32[]{:S(2)}) collective-permute-start(bf16[512,512]{1,0:T(8,128)(2,1)} %get-tuple-element.17), channel_id=1, source_target_pairs={{0,2},{2,0},{4,6},{6,4},{1,3},{3,1},{5,7},{7,5},{8,10},{10,8},{12,... | collective-permute-start | bytes 1572872 | tf_op jit(solution)/shard_map/ppermute | solution.py:189
  67.8 14.7 %collective-permute-start.12 = (bf16[512,512]{1,0:T(8,128)(2,1)}, bf16[512,512]{1,0:T(8,128)(2,1)S(1)}, u32[]{:S(2)}, u32[]{:S(2)}) collective-permute-start(bf16[512,512]{1,0:T(8,128)(2,1)} %get-tuple-element.18), channel_id=1, source_target_pairs={{0,6},{2,4},{4,2},{6,0},{1,7},{3,5},{5,3},{7,1},{8,14},{10,12},{12... | collective-permute-start | bytes 1572872 | tf_op jit(solution)/shard_map/ppermute | solution.py:189
  73.7 17.9 %collective-permute-start.9 = (bf16[512,512]{1,0:T(8,128)(2,1)}, bf16[512,512]{1,0:T(8,128)(2,1)S(1)}, u32[]{:S(2)}, u32[]{:S(2)}) collective-permute-start(bf16[512,512]{1,0:T(8,128)(2,1)} %get-tuple-element.13), channel_id=1, source_target_pairs={{0,2},{2,0},{4,6},{6,4},{1,3},{3,1},{5,7},{7,5},{8,10},{10,8},{12,... | collective-permute-start | bytes 1572872 | tf_op jit(solution)/shard_map/ppermute | solution.py:189
  74.0 19.6 %collective-permute-start.10 = (bf16[512,512]{1,0:T(8,128)(2,1)}, bf16[512,512]{1,0:T(8,128)(2,1)S(1)}, u32[]{:S(2)}, u32[]{:S(2)}) collective-permute-start(bf16[512,512]{1,0:T(8,128)(2,1)} %get-tuple-element.14), channel_id=1, source_target_pairs={{0,6},{2,4},{4,2},{6,0},{1,7},{3,5},{5,3},{7,1},{8,14},{10,12},{12... | collective-permute-start | bytes 1572872 | tf_op jit(solution)/shard_map/ppermute | solution.py:189
  80.3 2.1 %copy-start.7 = (bf16[512,512]{1,0:T(8,128)(2,1)}, bf16[512,512]{1,0:T(8,128)(2,1)S(1)}, u32[]{:S(2)}) copy-start(bf16[512,512]{1,0:T(8,128)(2,1)S(1)} %collective-permute-done.11.refs_8_) | copy-start | bytes 1572868
  82.4 0.8 copy-start.8
  87.6 17.3 %collective-permute-start.13 = (bf16[512,512]{1,0:T(8,128)(2,1)}, bf16[512,512]{1,0:T(8,128)(2,1)S(1)}, u32[]{:S(2)}, u32[]{:S(2)}) collective-permute-start(bf16[512,512]{1,0:T(8,128)(2,1)} %get-tuple-element.19), channel_id=1, source_target_pairs={{0,6},{2,4},{4,2},{6,0},{1,7},{3,5},{5,3},{7,1},{8,14},{10,12},{12... | collective-permute-start | bytes 1572872 | tf_op jit(solution)/shard_map/ppermute | solution.py:189
  89.4 15.5 %collective-permute-start.14 = (bf16[512,512]{1,0:T(8,128)(2,1)}, bf16[512,512]{1,0:T(8,128)(2,1)S(1)}, u32[]{:S(2)}, u32[]{:S(2)}) collective-permute-start(bf16[512,512]{1,0:T(8,128)(2,1)} %get-tuple-element.20), channel_id=1, source_target_pairs={{0,2},{2,0},{4,6},{6,4},{1,3},{3,1},{5,7},{7,5},{8,10},{10,8},{12,... | collective-permute-start | bytes 1572872 | tf_op jit(solution)/shard_map/ppermute | solution.py:189
  91.6 2.1 %copy-start.5 = (bf16[512,512]{1,0:T(8,128)(2,1)}, bf16[512,512]{1,0:T(8,128)(2,1)S(1)}, u32[]{:S(2)}) copy-start(bf16[512,512]{1,0:T(8,128)(2,1)S(1)} %collective-permute-done.9.refs_8_) | copy-start | bytes 1572868
  93.7 0.8 copy-start.6
  104.9 0.8 copy-start.3
  104.9 1.0 copy-start.4

commit v2 on v1

v2 whole, which is shorter than its diff:
```python
import functools
import math

import jax
import jax.numpy as jnp
from jax import lax
from jax.experimental import pallas as pl
from jax.experimental.pallas import tpu as pltpu
from jax.sharding import Mesh
from jax.sharding import PartitionSpec as P

HD = 128
PAD = 16
QB = 256
NT = (((1,), (1,)), ((), ()))
TN = (((0,), (0,)), ((), ()))
F32 = jnp.float32
BF16 = jnp.bfloat16
VMEM = pl.BlockSpec(memory_space=pltpu.VMEM)
SMEM = pl.BlockSpec(memory_space=pltpu.SMEM)
PARAMS = pltpu.CompilerParams(vmem_limit_bytes=8 * 2**20)


def near_core(array):
    return pltpu.with_memory_space_constraint(array, pltpu.VMEM)


def far_memory(array):
    return pltpu.with_memory_space_constraint(array, pltpu.HBM)


def features(v):
    return jnp.where(v > 0, v + 1.0, jnp.exp(jnp.minimum(v, 0.0)))


def delta_kernel(k_ref, v_ref, o_ref, total_ref, norm_ref):
    step = pl.program_id(0)
    heads = total_ref.shape[0] // HD

    @pl.when(step == 0)
    def _():
        total_ref[...] = jnp.zeros_like(total_ref)
        norm_ref[...] = jnp.zeros_like(norm_ref)

    feat = features(k_ref[...].astype(F32))
    norm_ref[...] += jnp.sum(feat, axis=0, keepdims=True)
    feat = feat.astype(BF16)
    for h in range(heads):
        cols = slice(h * HD, (h + 1) * HD)
        total_ref[cols, :] += lax.dot_general(
            v_ref[:, cols], feat[:, cols], TN, preferred_element_type=F32
        )

    @pl.when(step == pl.num_programs(0) - 1)
    def _():
        o_ref[: heads * HD, :] = total_ref[...].astype(BF16)
        row = lax.broadcasted_iota(jnp.int32, (PAD, HD), 0)
        norms = jnp.zeros((PAD, HD), F32)
        for h in range(heads):
            mine = jnp.broadcast_to(norm_ref[:, h * HD : (h + 1) * HD], (PAD, HD))
            norms = jnp.where(row == h, mine, norms)
        o_ref[heads * HD :, :] = norms.astype(BF16)


def delta(keys, values):
    rows, cols = keys.shape
    block = 256
    spec = pl.BlockSpec((block, cols), lambda i: (i, 0))
    return pl.pallas_call(
        delta_kernel,
        grid=(rows // block,),
        in_specs=[spec, spec],
        out_specs=VMEM,
        out_shape=pltpu.VMEM((cols + PAD, HD), BF16),
        scratch_shapes=[pltpu.VMEM((cols, HD), F32), pltpu.VMEM((1, cols), F32)],
        compiler_params=PARAMS,
        name="delta",
    )(far_memory(keys), far_memory(values))


def attention_kernel(first, g_ref, q_ref, k_ref, v_ref, o_ref, f_ref):
    h = pl.program_id(0)
    rows = q_ref.shape[0]
    c = math.log2(math.e) / math.sqrt(HD)
    keep = 1.0 - g_ref[first + h]
    causal = lax.broadcasted_iota(jnp.int32, (QB, QB), 1) <= lax.broadcasted_iota(
        jnp.int32, (QB, QB), 0
    )
    for i in range(rows // QB):
        lo, hi = i * QB, (i + 1) * QB
        q = q_ref[lo:hi, :]
        f_ref[lo:hi, :] = features(q.astype(F32)).astype(BF16)
        diag = lax.dot_general(q, k_ref[lo:hi, :], NT, preferred_element_type=F32)
        diag = jnp.where(causal, diag, -1e30)
        top = jnp.max(diag, axis=-1, keepdims=True)
        if lo:
            off = lax.dot_general(q, k_ref[:lo, :], NT, preferred_element_type=F32)
            top = jnp.maximum(top, jnp.max(off, axis=-1, keepdims=True))
        w = jnp.exp2((diag - top) * c)
        norm = jnp.sum(w, axis=-1, keepdims=True)
        out = jnp.dot(w.astype(BF16), v_ref[lo:hi, :], preferred_element_type=F32)
        if lo:
            w = jnp.exp2((off - top) * c)
            norm += jnp.sum(w, axis=-1, keepdims=True)
            out += jnp.dot(w.astype(BF16), v_ref[:lo, :], preferred_element_type=F32)
        o_ref[lo:hi, :] = out * (keep / norm)


def attention(gate, queries, keys, values, first, count):
    rows = queries.shape[0]
    spec = pl.BlockSpec((rows, HD), lambda h: (0, first + h))
    return pl.pallas_call(
        functools.partial(attention_kernel, first),
        grid=(count,),
        in_specs=[SMEM] + [spec] * 3,
        out_specs=[pl.BlockSpec((rows, HD), lambda h: (0, h))] * 2,
        out_shape=[pltpu.HBM((rows, count * HD), F32), pltpu.HBM((rows, count * HD), BF16)],
        compiler_params=PARAMS,
        name="attention",
    )(gate, queries, keys, values)


def retrieve_kernel(g_ref, *refs):
    *groups, s_ref, o_ref = refs
    base = s_ref.shape[0] - PAD
    block = groups[0].shape[0]
    out_rows = pl.ds(pl.multiple_of(pl.program_id(0) * block, block), block)
    h = 0
    for group in range(0, len(groups), 2):
        local, feat = groups[group], groups[group + 1]
        for at in range(local.shape[1] // HD):
            cols = slice(at * HD, (at + 1) * HD)
            f = feat[:, cols]
            numer = lax.dot_general(
                f, s_ref[h * HD : (h + 1) * HD, :], NT, preferred_element_type=F32
            )
            denom = lax.dot_general(f, s_ref[base:, :], NT, preferred_element_type=F32)
            scale = g_ref[h] / jnp.maximum(denom[:, h : h + 1], 1.0)
            mixed = numer * scale + local[:, cols]
            o_ref[out_rows, h * HD : (h + 1) * HD] = mixed.astype(BF16)
            h += 1


def retrieve(gate, groups, state, start, rows):
    flat = [array for group in groups for array in group]
    cols = state.shape[0] - PAD
    block = 128
    first = start // block
    specs = [pl.BlockSpec((block, a.shape[1]), lambda i: (first + i, 0)) for a in flat]
    return pl.pallas_call(
        retrieve_kernel,
        grid=(rows // block,),
        in_specs=[SMEM] + specs + [VMEM],
        out_specs=VMEM,
        out_shape=pltpu.VMEM((rows, cols), BF16),
        compiler_params=PARAMS,
        name="retrieve",
    )(gate, *[far_memory(a) for a in flat], near_core(state))


def sibling_kernel(at_ref, w_ref, o_ref):
    o_ref[0] = w_ref[...]


def sibling_columns(at, weight):
    depth, cols = weight.shape
    width = cols // 8
    return pl.pallas_call(
        sibling_kernel,
        grid_spec=pltpu.PrefetchScalarGridSpec(
            num_scalar_prefetch=1,
            grid=(4,),
            in_specs=[pl.BlockSpec((depth, width), lambda k, at: (0, 2 * k + 1 - at[1]))],
            out_specs=pl.BlockSpec((1, depth, width), lambda k, at: (k, 0, 0)),
        ),
        out_shape=pltpu.HBM((4, depth, width), BF16),
        compiler_params=PARAMS,
        name="sibling_columns",
    )(at, far_memory(weight))


def project_kernel(k, at_ref, a_own, a_sib, w_own, w_sib, *refs):
    *adds, o_ref = refs
    rows, width = o_ref.shape
    to = lax.bitwise_xor(at_ref[0], k)
    cols = pl.ds(pl.multiple_of((to * 2 + at_ref[1]) * width, width), width)
    block = 256
    for lo in range(0, rows, block):
        part = slice(lo, lo + block)
        total = jnp.dot(a_own[part, :], w_own[:, cols], preferred_element_type=F32)
        total += jnp.dot(a_sib[part, :], w_sib[to], preferred_element_type=F32)
        for add in adds:
            total += add[part, :].astype(F32)
        o_ref[part, :] = total.astype(o_ref.dtype)


def project(at, a_own, a_sib, w_own, w_sib, k, adds, dtype):
    rows, width = a_own.shape[0], w_sib.shape[2]
    return pl.pallas_call(
        functools.partial(project_kernel, k),
        in_specs=[SMEM] + [VMEM] * (4 + len(adds)),
        out_specs=VMEM,
        out_shape=pltpu.VMEM((rows, width), dtype),
        compiler_params=PARAMS,
        name="project",
    )(at, *[near_core(a) for a in (a_own, a_sib, w_own, w_sib, *adds)])


def finish_kernel(steps, p1, p2, r1, r2, o_ref):
    i = pl.program_id(0)
    block = o_ref.shape[0]

    def write(p, r, step):
        part = pl.ds(pl.multiple_of(step * block, block), block)
        o_ref[...] = (p[part, :] + r[part, :].astype(F32)).astype(o_ref.dtype)

    @pl.when(i < steps)
    def _():
        write(p1, r1, i)

    @pl.when(i >= steps)
    def _():
        write(p2, r2, i - steps)


def finish(p1, p2, r1, r2):
    rows, width = p1.shape
    block = 256
    steps = rows // block
    return pl.pallas_call(
        functools.partial(finish_kernel, steps),
        grid=(2 * steps,),
        in_specs=[VMEM] * 4,
        out_specs=pl.BlockSpec((block, width), lambda i: (i, 0)),
        out_shape=jax.ShapeDtypeStruct((2 * rows, width), BF16),
        compiler_params=PARAMS,
        name="finish",
    )(*[near_core(a) for a in (p1, p2, r1, r2)])


def swap(array, axis, mask):
    size = lax.axis_size(axis)
    return lax.ppermute(array, axis, [(i, i ^ mask) for i in range(size)])


def local(queries, keys, values, gate_bias, out_weight):
    y, z = lax.axis_index("y"), lax.axis_index("z")
    at = jnp.stack([lax.axis_index("x"), lax.axis_index("c")])
    heads = gate_bias.shape[0]
    gate = jax.nn.sigmoid(gate_bias)
    own = delta(keys, values)
    total, before = own.astype(F32), 0.0
    groups = []

    def fold(axis, mine, masks, beside):
        nonlocal total, before
        got = [swap(total.astype(BF16), axis, m) for m in masks]
        got, beside = lax.optimization_barrier((got, beside))
        for m, g in zip(masks, got):
            g = g.astype(F32)
            before = before + jnp.where((mine ^ m) < mine, g, 0.0)
            total = total + g
        return beside

    first = attention(gate, queries, keys, values, 0, heads // 2)
    first = fold("z", z, (1, 2, 3), first)
    held, total = lax.optimization_barrier(((queries, keys, values), total))
    second = attention(gate, *held, heads // 2, heads // 2)
    second = fold("z", z, (4,), second)
    weight, total = lax.optimization_barrier((out_weight, total))
    w_out = sibling_columns(at, weight)
    w_out = fold("y", y, (1, 2, 3), w_out)
    w_own, w_sib = out_weight, swap(w_out, "c", 1)
    state = before.astype(BF16)

    half = queries.shape[0] // 2
    halves = []
    for start in (0, half):
        a_own = retrieve(gate, (first, second), state, start, half)
        halves.append((a_own, swap(a_own, "c", 1)))

    def mm(i, k, adds, dtype):
        return project(at, *halves[i], w_own, w_sib, k, adds, dtype)

    hops = ((1, 3), (3, 1))
    far = [swap(mm(i, 2, (), BF16), "x", hops[i][0]) for i in range(2)]
    near = [swap(mm(i, hops[i][0], (), BF16), "x", hops[i][0]) for i in range(2)]
    passed = [swap(mm(i, hops[i][1], (far[i],), BF16), "x", hops[i][1]) for i in range(2)]
    mine = [mm(i, 0, (near[i],), F32) for i in range(2)]
    return finish(*mine, *passed)


def solution(mesh):
    finer = Mesh(mesh.devices.reshape(4, 8, 4, 2), ("y", "z", "x", "c"))
    rows, cols = ("y", "z"), ("x", "c")
    placed = (P(rows, cols), P(rows, cols), P(rows, cols), P(cols), P(cols, None))
    return jax.shard_map(
        local, mesh=finer, in_specs=placed, out_specs=P(rows, cols), check_vma=False
    )
```

time: 110 us -> 92.6 us (0.84)
  local copies, waits for them, and re-layouts: 9.27 us -> 1.24 us
  other arithmetic: 6.69 us -> 0.4 us
  Pallas kernels: 40.9 us -> 35.7 us
  waiting for transfers between devices: 26.7 us -> 29.2 us
    another operation x2 -> x1, other arithmetic: 4.68 us -> 0.07 us  [local(): at = jnp.stack([lax.axis_index('x'), lax.axis_index('c')])]
    another operation x1 -> x0, local copies, waits for them, and re-layouts: 3.75 us -> none  [columns(): jnp.stack([lax.dynamic_slice_in_dim(out_weight, ((x ^ k) * 2 + core) * wi...]
    unnamed x20 -> x12, local copies, waits for them, and re-layouts: 4.87 us -> 1.24 us
    pallas_call x8 -> x14, Pallas kernels: 36.8 us -> 34.1 us  [the longest x8 10 us: project(): pl.pallas_call(functools.partial(project_kernel, k), in_specs=[SMEM] + [V...]
    ppermute x15 -> x16, waiting for transfers between devices: 26.7 us -> 29.2 us  [swap(): return lax.ppermute(array, axis, [(i, i ^ mask) for i in range(size)])]
    pallas_call x1, Pallas kernels: 4.05 us -> 1.6 us  [finish(): pl.pallas_call(functools.partial(finish_kernel, steps), grid=(2 * steps,)...]
    convert_element_type x4 -> x2, other arithmetic: 2 us -> 0.21 us  [the longest x1 0.19 us: local(): state = before.astype(BF16)]
    ppermute x15 -> x16, starting transfers between devices: 26.3 us -> 25.6 us  [swap(): return lax.ppermute(array, axis, [(i, i ^ mask) for i in range(size)])]
  transfers between devices with their start and end apart: 15 -> 16, of which waited for: 9 -> 6; matrix products, arithmetic and copies ran while one was open for 9% -> 0% of each run, Pallas kernels for 26% -> 33%
where the time goes in v2:
time: 92.6 us; the launch traced here: 92.3 us
  Pallas kernels  35.7 us (39%)
  waiting for transfers between devices  29.2 us (32%)
  starting transfers between devices  25.6 us (28%)
  local copies, waits for them, and re-layouts  1.24 us (1%)
    ppermute x16, waiting for transfers between devices, swap(): return lax.ppermute(array, axis, [(i, i ^ mask) for i in range(size)])  29.2 us
    ppermute x16, starting transfers between devices, swap(): return lax.ppermute(array, axis, [(i, i ^ mask) for i in range(size)])  25.6 us
    pallas_call x8, Pallas kernels, project(): pl.pallas_call(functools.partial(project_kernel, k), in_specs=[SMEM] + [V...  10 us
    pallas_call x2, Pallas kernels, attention(): pl.pallas_call(functools.partial(attention_kernel, first), grid=(count,),...  9.96 us
    pallas_call x2, Pallas kernels, retrieve(): pl.pallas_call(retrieve_kernel, grid=(rows // block,), in_specs=[SMEM] +...  6.4 us
    pallas_call x1, Pallas kernels, sibling_columns(): pl.pallas_call(sibling_kernel, grid_spec=pltpu.PrefetchScalarGridSpec(num...  4.35 us
    pallas_call x1, Pallas kernels, delta(): pl.pallas_call(delta_kernel, grid=(rows // block,), in_specs=[spec, spec]...  3.4 us
  transfers between devices with their start and end apart: 16, of which 6 were waited for; matrix products, arithmetic and copies ran while one was open for 0% of the time, Pallas kernels for 33%

profile of v2, /device:TPU:1, one launch (start us, length us, event | category | flops | bytes accessed | tf_op | source)
XLA Modules:
  0.0 92.3 jit_solution(11529315927676969036)
XLA Ops:
  0.0 0.0 copy-start.2
  0.0 0.0 copy-start.1
  0.0 0.0 copy-start.5
  0.0 3.4 %delta.1 = bf16[528,128]{1,0:T(8,128)(2,1)S(1)} custom-call(bf16[1024,512]{1,0:T(8,128)(2,1)} %k_ref.4, bf16[1024,512]{1,0:T(8,128)(2,1)} %v_ref.4), custom_call_target="tpu_custom_call" | custom-call | tf_op jit(solution)/shard_map/delta/pallas_call | solution.py:69
  3.4 5.3 %collective-permute-start.2 = (bf16[528,128]{1,0:T(8,128)(2,1)S(1)}, bf16[528,128]{1,0:T(8,128)(2,1)S(1)}, u32[]{:S(2)}, u32[]{:S(2)}) collective-permute-start(bf16[528,128]{1,0:T(8,128)(2,1)S(1)} %delta.1), channel_id=1, source_target_pairs={{0,24},{8,16},{16,8},{24,0},{32,56},{40,48},{48,40},{56,32},{1,25}... | collective-permute-start | bytes 405512 | tf_op jit(solution)/shard_map/ppermute | solution.py:243
  8.7 0.0 collective-permute-start.1
  8.7 0.4 collective-permute-start
  9.1 0.0 copy-done.5
  9.1 0.0 copy-done.2
  9.1 0.0 copy-done.1
  9.1 0.0 copy-start.3
  9.1 1.2 %copy-done.3 = bf16[1024,512]{1,0:T(8,128)(2,1)S(1)} copy-done((bf16[1024,512]{1,0:T(8,128)(2,1)S(1)}, bf16[1024,512]{1,0:T(8,128)(2,1)}, u32[]{:S(2)}) %copy-start.3) | copy-done | bytes 1048600
  10.3 0.0 copy-start.4
  10.3 5.0 %attention.2 = (f32[1024,256]{1,0:T(8,128)}, bf16[1024,256]{1,0:T(8,128)(2,1)}) custom-call(f32[4]{0:T(128)S(1)} %add_divide_fusion.g_ref, bf16[1024,512]{1,0:T(8,128)(2,1)S(1)} %copy-done.3, bf16[1024,512]{1,0:T(8,128)(2,1)S(1)} %copy-done.1, bf16[1024,512]{1,0:T(8,128)(2,1)S(1)} %copy-done.2), custom_call_target="tpu_custom_call" | custom-call | tf_op jit(solution)/shard_map/attention/pallas_call | solution.py:112
  15.3 0.0 collective-permute-done.2
  15.3 3.9 %collective-permute-done.1 = bf16[528,128]{1,0:T(8,128)(2,1)S(1)} collective-permute-done((bf16[528,128]{1,0:T(8,128)(2,1)S(1)}, bf16[528,128]{1,0:T(8,128)(2,1)S(1)}, u32[]{:S(2)}, u32[]{:S(2)}) %collective-permute-start.1) | collective-permute-done | bytes 135200 | tf_op jit(solution)/shard_map/ppermute | solution.py:243
  19.2 0.0 collective-permute-done
  19.2 0.1 convert_add_fusion.1
  19.3 5.7 %collective-permute-start.3 = (bf16[528,128]{1,0:T(8,128)(2,1)S(1)}, bf16[528,128]{1,0:T(8,128)(2,1)S(1)}, u32[]{:S(2)}, u32[]{:S(2)}) collective-permute-start(bf16[528,128]{1,0:T(8,128)(2,1)S(1)} %convert_element_type.42), channel_id=1, source_target_pairs={{0,32},{8,40},{16,48},{24,56},{32,0},{40,8},{48,16},{56,24},{1,33}... | collective-permute-start | bytes 405512 | tf_op jit(solution)/shard_map/ppermute | solution.py:243
  25.0 0.0 copy-done.4
  25.0 5.0 %attention.3 = (f32[1024,256]{1,0:T(8,128)}, bf16[1024,256]{1,0:T(8,128)(2,1)}) custom-call(f32[4]{0:T(128)S(1)} %add_divide_fusion.g_ref, bf16[1024,512]{1,0:T(8,128)(2,1)S(1)} %copy-done.4, bf16[1024,512]{1,0:T(8,128)(2,1)S(1)} %copy-done.1, bf16[1024,512]{1,0:T(8,128)(2,1)S(1)} %copy-done.2), custom_call_target="tpu_custom_call" | custom-call | tf_op jit(solution)/shard_map/attention/pallas_call | solution.py:112
  30.0 0.0 collective-permute-done.3
  30.1 3.0 %collective-permute-start.5 = (bf16[528,128]{1,0:T(8,128)(2,1)S(1)}, bf16[528,128]{1,0:T(8,128)(2,1)S(1)}, u32[]{:S(2)}, u32[]{:S(2)}) collective-permute-start(bf16[528,128]{1,0:T(8,128)(2,1)S(1)} %convert_add_fusion), channel_id=1, source_target_pairs={{0,128},{64,192},{128,0},{192,64},{1,129},{65,193},{129,1},{193,65... | collective-permute-start | bytes 405512 | tf_op jit(solution)/shard_map/ppermute | solution.py:243
  33.1 0.4 collective-permute-start.4
  33.5 0.4 collective-permute-start.6
  33.9 0.1 pad_add_fusion.at_ref
  33.9 4.4 %sibling_columns.1 = bf16[4,512,512]{2,1,0:T(8,128)(2,1)} custom-call(s32[2]{0:T(128)S(1)} %pad_add_fusion.at_ref, bf16[512,4096]{1,0:T(8,128)(2,1)} %w_own.15), custom_call_target="tpu_custom_call" | custom-call | tf_op jit(solution)/shard_map/sibling_columns/pallas_call | solution.py:168
  38.3 0.0 collective-permute-done.5
  38.3 0.0 collective-permute-done.4
  38.3 1.5 %collective-permute-done.6 = bf16[528,128]{1,0:T(8,128)(2,1)S(1)} collective-permute-done((bf16[528,128]{1,0:T(8,128)(2,1)S(1)}, bf16[528,128]{1,0:T(8,128)(2,1)S(1)}, u32[]{:S(2)}, u32[]{:S(2)}) %collective-permute-start.6) | collective-permute-done | bytes 135200 | tf_op jit(solution)/shard_map/ppermute | solution.py:243
  39.8 2.6 %collective-permute-start.8 = (bf16[4,512,512]{2,1,0:T(8,128)(2,1)}, bf16[4,512,512]{2,1,0:T(8,128)(2,1)S(1)}, u32[]{:S(2)}, u32[]{:S(2)}) collective-permute-start(bf16[4,512,512]{2,1,0:T(8,128)(2,1)} %sibling_columns.1), channel_id=1, source_target_pairs={{0,1},{1,0},{2,3},{3,2},{4,5},{5,4},{6,7},{7,6},{8,9},{9,8},{10,11... | collective-permute-start | bytes 6291464 | tf_op jit(solution)/shard_map/ppermute | solution.py:243
  42.4 0.2 fusion.6.refs_4_
  42.6 0.0 copy-start
  42.6 3.3 %retrieve.2.a_own = bf16[512,512]{1,0:T(8,128)(2,1)S(1)} custom-call(f32[4]{0:T(128)S(1)} %add_divide_fusion.g_ref, f32[1024,256]{1,0:T(8,128)} %get-tuple-element.29.refs_0_, bf16[1024,256]{1,0:T(8,128)(2,1)} %get-tuple-element.30.refs_1_, f32[1024,256]{1,0:T(8,128)} %get-tuple-element.40.refs_2_, bf16[1024,256]{1,0:T(8,128)(2,1)} %get-tuple-element.41.refs_3_, ...), custom_call_target="tpu_custom_call" | custom-call | tf_op jit(solution)/shard_map/retrieve/pallas_call | solution.py:150
  45.9 0.1 collective-permute-start.7
  46.0 3.1 %retrieve.3.a_own = bf16[512,512]{1,0:T(8,128)(2,1)S(1)} custom-call(f32[4]{0:T(128)S(1)} %add_divide_fusion.g_ref, f32[1024,256]{1,0:T(8,128)} %get-tuple-element.29.refs_0_, bf16[1024,256]{1,0:T(8,128)(2,1)} %get-tuple-element.30.refs_1_, f32[1024,256]{1,0:T(8,128)} %get-tuple-element.40.refs_2_, bf16[1024,256]{1,0:T(8,128)(2,1)} %get-tuple-element.41.refs_3_, ...), custom_call_target="tpu_custom_call" | custom-call | tf_op jit(solution)/shard_map/retrieve/pallas_call | solution.py:150
  49.2 0.6 collective-permute-start.10
  49.7 0.0 collective-permute-done.7.a_sib
  49.7 0.0 collective-permute-done.8.w_sib
  49.7 0.0 copy-done
  49.7 1.3 %project.12 = bf16[512,512]{1,0:T(8,128)(2,1)S(1)} custom-call(s32[2]{0:T(128)S(1)} %pad_add_fusion.at_ref, bf16[512,512]{1,0:T(8,128)(2,1)S(1)} %retrieve.2.a_own, bf16[512,512]{1,0:T(8,128)(2,1)S(1)} %collective-permute-done.7.a_sib, bf16[512,4096]{1,0:T(8,128)(2,1)S(1)} %copy-done, bf16[4,512,512]{2,1,0:T(8,128)(2,1)S(1)} %collective-permute-done.8.w_sib), custom_call_target="tpu_custom_call" | custom-call | tf_op jit(solution)/shard_map/project/pallas_call | solution.py:199
  51.0 1.3 %collective-permute-start.12 = (bf16[512,512]{1,0:T(8,128)(2,1)S(1)}, bf16[512,512]{1,0:T(8,128)(2,1)S(1)}, u32[]{:S(2)}, u32[]{:S(2)}) collective-permute-start(bf16[512,512]{1,0:T(8,128)(2,1)S(1)} %project.12), channel_id=1, source_target_pairs={{0,2},{2,0},{4,6},{6,4},{1,3},{3,1},{5,7},{7,5},{8,10},{10,8},{12,... | collective-permute-start | bytes 1572872 | tf_op jit(solution)/shard_map/ppermute | solution.py:243
  52.3 0.0 collective-permute-done.10.a_sib
  52.3 1.2 %project.14 = bf16[512,512]{1,0:T(8,128)(2,1)S(1)} custom-call(s32[2]{0:T(128)S(1)} %pad_add_fusion.at_ref, bf16[512,512]{1,0:T(8,128)(2,1)S(1)} %retrieve.3.a_own, bf16[512,512]{1,0:T(8,128)(2,1)S(1)} %collective-permute-done.10.a_sib, bf16[512,4096]{1,0:T(8,128)(2,1)S(1)} %copy-done, bf16[4,512,512]{2,1,0:T(8,128)(2,1)S(1)} %collective-permute-done.8.w_sib), custom_call_target="tpu_custom_call" | custom-call | tf_op jit(solution)/shard_map/project/pallas_call | solution.py:199
  53.6 2.1 %collective-permute-start.14 = (bf16[512,512]{1,0:T(8,128)(2,1)S(1)}, bf16[512,512]{1,0:T(8,128)(2,1)S(1)}, u32[]{:S(2)}, u32[]{:S(2)}) collective-permute-start(bf16[512,512]{1,0:T(8,128)(2,1)S(1)} %project.14), channel_id=1, source_target_pairs={{0,6},{2,4},{4,2},{6,0},{1,7},{3,5},{5,3},{7,1},{8,14},{10,12},{12... | collective-permute-start | bytes 1572872 | tf_op jit(solution)/shard_map/ppermute | solution.py:243
  55.6 1.2 %project.8 = bf16[512,512]{1,0:T(8,128)(2,1)S(1)} custom-call(s32[2]{0:T(128)S(1)} %pad_add_fusion.at_ref, bf16[512,512]{1,0:T(8,128)(2,1)S(1)} %retrieve.2.a_own, bf16[512,512]{1,0:T(8,128)(2,1)S(1)} %collective-permute-done.7.a_sib, bf16[512,4096]{1,0:T(8,128)(2,1)S(1)} %copy-done, bf16[4,512,512]{2,1,0:T(8,128)(2,1)S(1)} %collective-permute-done.8.w_sib), custom_call_target="tpu_custom_call" | custom-call | tf_op jit(solution)/shard_map/project/pallas_call | solution.py:199
  56.9 0.4 collective-permute-start.9
  57.3 1.2 %project.10 = bf16[512,512]{1,0:T(8,128)(2,1)S(1)} custom-call(s32[2]{0:T(128)S(1)} %pad_add_fusion.at_ref, bf16[512,512]{1,0:T(8,128)(2,1)S(1)} %retrieve.3.a_own, bf16[512,512]{1,0:T(8,128)(2,1)S(1)} %collective-permute-done.10.a_sib, bf16[512,4096]{1,0:T(8,128)(2,1)S(1)} %copy-done, bf16[4,512,512]{2,1,0:T(8,128)(2,1)S(1)} %collective-permute-done.8.w_sib), custom_call_target="tpu_custom_call" | custom-call | tf_op jit(solution)/shard_map/project/pallas_call | solution.py:199
  58.6 0.7 collective-permute-start.11
  59.3 5.3 %collective-permute-done.12.refs_0_ = bf16[512,512]{1,0:T(8,128)(2,1)S(1)} collective-permute-done((bf16[512,512]{1,0:T(8,128)(2,1)S(1)}, bf16[512,512]{1,0:T(8,128)(2,1)S(1)}, u32[]{:S(2)}, u32[]{:S(2)}) %collective-permute-start.12) | collective-permute-done | bytes 524320 | tf_op jit(solution)/shard_map/ppermute | solution.py:243
  64.6 1.3 %project.13 = bf16[512,512]{1,0:T(8,128)(2,1)S(1)} custom-call(s32[2]{0:T(128)S(1)} %pad_add_fusion.at_ref, bf16[512,512]{1,0:T(8,128)(2,1)S(1)} %retrieve.2.a_own, bf16[512,512]{1,0:T(8,128)(2,1)S(1)} %collective-permute-done.7.a_sib, bf16[512,4096]{1,0:T(8,128)(2,1)S(1)} %copy-done, bf16[4,512,512]{2,1,0:T(8,128)(2,1)S(1)} %collective-permute-done.8.w_sib, ...), custom_call_target="tpu_custom_call" | custom-call | tf_op jit(solution)/shard_map/project/pallas_call | solution.py:199
  65.9 2.6 %collective-permute-start.13 = (bf16[512,512]{1,0:T(8,128)(2,1)S(1)}, bf16[512,512]{1,0:T(8,128)(2,1)S(1)}, u32[]{:S(2)}, u32[]{:S(2)}) collective-permute-start(bf16[512,512]{1,0:T(8,128)(2,1)S(1)} %project.13), channel_id=1, source_target_pairs={{0,6},{2,4},{4,2},{6,0},{1,7},{3,5},{5,3},{7,1},{8,14},{10,12},{12... | collective-permute-start | bytes 1572872 | tf_op jit(solution)/shard_map/ppermute | solution.py:243
  68.4 0.0 collective-permute-done.14.refs_0_
  68.4 1.3 %project.15 = bf16[512,512]{1,0:T(8,128)(2,1)S(1)} custom-call(s32[2]{0:T(128)S(1)} %pad_add_fusion.at_ref, bf16[512,512]{1,0:T(8,128)(2,1)S(1)} %retrieve.3.a_own, bf16[512,512]{1,0:T(8,128)(2,1)S(1)} %collective-permute-done.10.a_sib, bf16[512,4096]{1,0:T(8,128)(2,1)S(1)} %copy-done, bf16[4,512,512]{2,1,0:T(8,128)(2,1)S(1)} %collective-permute-done.8.w_sib, ...), custom_call_target="tpu_custom_call" | custom-call | tf_op jit(solution)/shard_map/project/pallas_call | solution.py:199
  69.7 0.1 collective-permute-start.15
  69.8 6.0 %collective-permute-done.9.refs_0_ = bf16[512,512]{1,0:T(8,128)(2,1)S(1)} collective-permute-done((bf16[512,512]{1,0:T(8,128)(2,1)S(1)}, bf16[512,512]{1,0:T(8,128)(2,1)S(1)}, u32[]{:S(2)}, u32[]{:S(2)}) %collective-permute-start.9) | collective-permute-done | bytes 524320 | tf_op jit(solution)/shard_map/ppermute | solution.py:243
  75.8 1.3 %project.9.p1 = f32[512,512]{1,0:T(8,128)S(1)} custom-call(s32[2]{0:T(128)S(1)} %pad_add_fusion.at_ref, bf16[512,512]{1,0:T(8,128)(2,1)S(1)} %retrieve.2.a_own, bf16[512,512]{1,0:T(8,128)(2,1)S(1)} %collective-permute-done.7.a_sib, bf16[512,4096]{1,0:T(8,128)(2,1)S(1)} %copy-done, bf16[4,512,512]{2,1,0:T(8,128)(2,1)S(1)} %collective-permute-done.8.w_sib, ...), custom_call_target="tpu_custom_call" | custom-call | tf_op jit(solution)/shard_map/project/pallas_call | solution.py:199
  77.1 2.4 %collective-permute-done.11.refs_0_ = bf16[512,512]{1,0:T(8,128)(2,1)S(1)} collective-permute-done((bf16[512,512]{1,0:T(8,128)(2,1)S(1)}, bf16[512,512]{1,0:T(8,128)(2,1)S(1)}, u32[]{:S(2)}, u32[]{:S(2)}) %collective-permute-start.11) | collective-permute-done | bytes 524320 | tf_op jit(solution)/shard_map/ppermute | solution.py:243
  79.5 1.3 %project.11.p2 = f32[512,512]{1,0:T(8,128)S(1)} custom-call(s32[2]{0:T(128)S(1)} %pad_add_fusion.at_ref, bf16[512,512]{1,0:T(8,128)(2,1)S(1)} %retrieve.3.a_own, bf16[512,512]{1,0:T(8,128)(2,1)S(1)} %collective-permute-done.10.a_sib, bf16[512,4096]{1,0:T(8,128)(2,1)S(1)} %copy-done, bf16[4,512,512]{2,1,0:T(8,128)(2,1)S(1)} %collective-permute-done.8.w_sib, ...), custom_call_target="tpu_custom_call" | custom-call | tf_op jit(solution)/shard_map/project/pallas_call | solution.py:199
  80.7 10.0 %collective-permute-done.13.r1 = bf16[512,512]{1,0:T(8,128)(2,1)S(1)} collective-permute-done((bf16[512,512]{1,0:T(8,128)(2,1)S(1)}, bf16[512,512]{1,0:T(8,128)(2,1)S(1)}, u32[]{:S(2)}, u32[]{:S(2)}) %collective-permute-start.13) | collective-permute-done | bytes 524320 | tf_op jit(solution)/shard_map/ppermute | solution.py:243
  90.7 0.0 collective-permute-done.15.r2
  90.7 1.6 %finish.1 = bf16[1024,512]{1,0:T(8,128)(2,1)} custom-call(f32[512,512]{1,0:T(8,128)S(1)} %project.9.p1, f32[512,512]{1,0:T(8,128)S(1)} %project.11.p2, bf16[512,512]{1,0:T(8,128)(2,1)S(1)} %collective-permute-done.13.r1, bf16[512,512]{1,0:T(8,128)(2,1)S(1)} %collective-permute-done.15.r2), custom_call_target="tpu_custom_call" | custom-call | tf_op jit(solution)/shard_map/finish/pallas_call | solution.py:230
  (3 shorter events, 0.1 us)
Async XLA Ops:
  0.0 9.1 %copy-start.2 = (bf16[1024,512]{1,0:T(8,128)(2,1)S(1)}, bf16[1024,512]{1,0:T(8,128)(2,1)}, u32[]{:S(2)}) copy-start(bf16[1024,512]{1,0:T(8,128)(2,1)} %v_ref.4) | copy-start | bytes 3145732
  0.0 9.1 %copy-start.1 = (bf16[1024,512]{1,0:T(8,128)(2,1)S(1)}, bf16[1024,512]{1,0:T(8,128)(2,1)}, u32[]{:S(2)}) copy-start(bf16[1024,512]{1,0:T(8,128)(2,1)} %k_ref.4) | copy-start | bytes 3145732
  0.0 9.1 %copy-start.5 = (f32[4]{0:T(128)S(1)}, f32[4]{0:T(128)}, u32[]{:S(2)}) copy-start(f32[4]{0:T(128)} %param.8) | copy-start | bytes 52
  3.4 11.9 %collective-permute-start.2 = (bf16[528,128]{1,0:T(8,128)(2,1)S(1)}, bf16[528,128]{1,0:T(8,128)(2,1)S(1)}, u32[]{:S(2)}, u32[]{:S(2)}) collective-permute-start(bf16[528,128]{1,0:T(8,128)(2,1)S(1)} %delta.1), channel_id=1, source_target_pairs={{0,24},{8,16},{16,8},{24,0},{32,56},{40,48},{48,40},{56,32},{1,25}... | collective-permute-start | bytes 405512 | tf_op jit(solution)/shard_map/ppermute | solution.py:243
  8.7 10.5 %collective-permute-start.1 = (bf16[528,128]{1,0:T(8,128)(2,1)S(1)}, bf16[528,128]{1,0:T(8,128)(2,1)S(1)}, u32[]{:S(2)}, u32[]{:S(2)}) collective-permute-start(bf16[528,128]{1,0:T(8,128)(2,1)S(1)} %delta.1), channel_id=1, source_target_pairs={{0,16},{8,24},{16,0},{24,8},{32,48},{40,56},{48,32},{56,40},{1,17}... | collective-permute-start | bytes 405512 | tf_op jit(solution)/shard_map/ppermute | solution.py:243
  8.7 10.5 %collective-permute-start = (bf16[528,128]{1,0:T(8,128)(2,1)S(1)}, bf16[528,128]{1,0:T(8,128)(2,1)S(1)}, u32[]{:S(2)}, u32[]{:S(2)}) collective-permute-start(bf16[528,128]{1,0:T(8,128)(2,1)S(1)} %delta.1), channel_id=1, source_target_pairs={{0,8},{8,0},{16,24},{24,16},{32,40},{40,32},{48,56},{56,48},{1,9},... | collective-permute-start | bytes 405512 | tf_op jit(solution)/shard_map/ppermute | solution.py:243
  9.1 1.2 %copy-start.3 = (bf16[1024,512]{1,0:T(8,128)(2,1)S(1)}, bf16[1024,512]{1,0:T(8,128)(2,1)}, u32[]{:S(2)}) copy-start(bf16[1024,512]{1,0:T(8,128)(2,1)} %q_ref.2) | copy-start | bytes 3145732
  10.3 14.7 %copy-start.4 = (bf16[1024,512]{1,0:T(8,128)(2,1)S(1)}, bf16[1024,512]{1,0:T(8,128)(2,1)}, u32[]{:S(2)}) copy-start(bf16[1024,512]{1,0:T(8,128)(2,1)} %q_ref.2) | copy-start | bytes 3145732
  19.3 10.7 %collective-permute-start.3 = (bf16[528,128]{1,0:T(8,128)(2,1)S(1)}, bf16[528,128]{1,0:T(8,128)(2,1)S(1)}, u32[]{:S(2)}, u32[]{:S(2)}) collective-permute-start(bf16[528,128]{1,0:T(8,128)(2,1)S(1)} %convert_element_type.42), channel_id=1, source_target_pairs={{0,32},{8,40},{16,48},{24,56},{32,0},{40,8},{48,16},{56,24},{1,33}... | collective-permute-start | bytes 405512 | tf_op jit(solution)/shard_map/ppermute | solution.py:243
  30.1 8.2 %collective-permute-start.5 = (bf16[528,128]{1,0:T(8,128)(2,1)S(1)}, bf16[528,128]{1,0:T(8,128)(2,1)S(1)}, u32[]{:S(2)}, u32[]{:S(2)}) collective-permute-start(bf16[528,128]{1,0:T(8,128)(2,1)S(1)} %convert_add_fusion), channel_id=1, source_target_pairs={{0,128},{64,192},{128,0},{192,64},{1,129},{65,193},{129,1},{193,65... | collective-permute-start | bytes 405512 | tf_op jit(solution)/shard_map/ppermute | solution.py:243
  33.1 5.2 %collective-permute-start.4 = (bf16[528,128]{1,0:T(8,128)(2,1)S(1)}, bf16[528,128]{1,0:T(8,128)(2,1)S(1)}, u32[]{:S(2)}, u32[]{:S(2)}) collective-permute-start(bf16[528,128]{1,0:T(8,128)(2,1)S(1)} %convert_add_fusion), channel_id=1, source_target_pairs={{0,64},{64,0},{128,192},{192,128},{1,65},{65,1},{129,193},{193,129... | collective-permute-start | bytes 405512 | tf_op jit(solution)/shard_map/ppermute | solution.py:243
  33.5 6.3 %collective-permute-start.6 = (bf16[528,128]{1,0:T(8,128)(2,1)S(1)}, bf16[528,128]{1,0:T(8,128)(2,1)S(1)}, u32[]{:S(2)}, u32[]{:S(2)}) collective-permute-start(bf16[528,128]{1,0:T(8,128)(2,1)S(1)} %convert_add_fusion), channel_id=1, source_target_pairs={{0,192},{64,128},{128,64},{192,0},{1,193},{65,129},{129,65},{193,1... | collective-permute-start | bytes 405512 | tf_op jit(solution)/shard_map/ppermute | solution.py:243
  39.8 9.9 %collective-permute-start.8 = (bf16[4,512,512]{2,1,0:T(8,128)(2,1)}, bf16[4,512,512]{2,1,0:T(8,128)(2,1)S(1)}, u32[]{:S(2)}, u32[]{:S(2)}) collective-permute-start(bf16[4,512,512]{2,1,0:T(8,128)(2,1)} %sibling_columns.1), channel_id=1, source_target_pairs={{0,1},{1,0},{2,3},{3,2},{4,5},{5,4},{6,7},{7,6},{8,9},{9,8},{10,11... | collective-permute-start | bytes 6291464 | tf_op jit(solution)/shard_map/ppermute | solution.py:243
  42.6 7.1 %copy-start = (bf16[512,4096]{1,0:T(8,128)(2,1)S(1)}, bf16[512,4096]{1,0:T(8,128)(2,1)}, u32[]{:S(2)}) copy-start(bf16[512,4096]{1,0:T(8,128)(2,1)} %w_own.15) | copy-start | bytes 12582916
  45.9 3.8 %collective-permute-start.7 = (bf16[512,512]{1,0:T(8,128)(2,1)S(1)}, bf16[512,512]{1,0:T(8,128)(2,1)S(1)}, u32[]{:S(2)}, u32[]{:S(2)}) collective-permute-start(bf16[512,512]{1,0:T(8,128)(2,1)S(1)} %retrieve.2.a_own), channel_id=1, source_target_pairs={{0,1},{1,0},{2,3},{3,2},{4,5},{5,4},{6,7},{7,6},{8,9},{9,8},{10,11... | collective-permute-start | bytes 1572872 | tf_op jit(solution)/shard_map/ppermute | solution.py:243
  49.2 3.1 %collective-permute-start.10 = (bf16[512,512]{1,0:T(8,128)(2,1)S(1)}, bf16[512,512]{1,0:T(8,128)(2,1)S(1)}, u32[]{:S(2)}, u32[]{:S(2)}) collective-permute-start(bf16[512,512]{1,0:T(8,128)(2,1)S(1)} %retrieve.3.a_own), channel_id=1, source_target_pairs={{0,1},{1,0},{2,3},{3,2},{4,5},{5,4},{6,7},{7,6},{8,9},{9,8},{10,11... | collective-permute-start | bytes 1572872 | tf_op jit(solution)/shard_map/ppermute | solution.py:243
  51.0 13.6 %collective-permute-start.12 = (bf16[512,512]{1,0:T(8,128)(2,1)S(1)}, bf16[512,512]{1,0:T(8,128)(2,1)S(1)}, u32[]{:S(2)}, u32[]{:S(2)}) collective-permute-start(bf16[512,512]{1,0:T(8,128)(2,1)S(1)} %project.12), channel_id=1, source_target_pairs={{0,2},{2,0},{4,6},{6,4},{1,3},{3,1},{5,7},{7,5},{8,10},{10,8},{12,... | collective-permute-start | bytes 1572872 | tf_op jit(solution)/shard_map/ppermute | solution.py:243
  53.6 14.9 %collective-permute-start.14 = (bf16[512,512]{1,0:T(8,128)(2,1)S(1)}, bf16[512,512]{1,0:T(8,128)(2,1)S(1)}, u32[]{:S(2)}, u32[]{:S(2)}) collective-permute-start(bf16[512,512]{1,0:T(8,128)(2,1)S(1)} %project.14), channel_id=1, source_target_pairs={{0,6},{2,4},{4,2},{6,0},{1,7},{3,5},{5,3},{7,1},{8,14},{10,12},{12... | collective-permute-start | bytes 1572872 | tf_op jit(solution)/shard_map/ppermute | solution.py:243
  56.9 19.0 %collective-permute-start.9 = (bf16[512,512]{1,0:T(8,128)(2,1)S(1)}, bf16[512,512]{1,0:T(8,128)(2,1)S(1)}, u32[]{:S(2)}, u32[]{:S(2)}) collective-permute-start(bf16[512,512]{1,0:T(8,128)(2,1)S(1)} %project.8), channel_id=1, source_target_pairs={{0,2},{2,0},{4,6},{6,4},{1,3},{3,1},{5,7},{7,5},{8,10},{10,8},{12,... | collective-permute-start | bytes 1572872 | tf_op jit(solution)/shard_map/ppermute | solution.py:243
  58.6 20.9 %collective-permute-start.11 = (bf16[512,512]{1,0:T(8,128)(2,1)S(1)}, bf16[512,512]{1,0:T(8,128)(2,1)S(1)}, u32[]{:S(2)}, u32[]{:S(2)}) collective-permute-start(bf16[512,512]{1,0:T(8,128)(2,1)S(1)} %project.10), channel_id=1, source_target_pairs={{0,6},{2,4},{4,2},{6,0},{1,7},{3,5},{5,3},{7,1},{8,14},{10,12},{12... | collective-permute-start | bytes 1572872 | tf_op jit(solution)/shard_map/ppermute | solution.py:243
  65.9 24.8 %collective-permute-start.13 = (bf16[512,512]{1,0:T(8,128)(2,1)S(1)}, bf16[512,512]{1,0:T(8,128)(2,1)S(1)}, u32[]{:S(2)}, u32[]{:S(2)}) collective-permute-start(bf16[512,512]{1,0:T(8,128)(2,1)S(1)} %project.13), channel_id=1, source_target_pairs={{0,6},{2,4},{4,2},{6,0},{1,7},{3,5},{5,3},{7,1},{8,14},{10,12},{12... | collective-permute-start | bytes 1572872 | tf_op jit(solution)/shard_map/ppermute | solution.py:243
  69.7 21.0 %collective-permute-start.15 = (bf16[512,512]{1,0:T(8,128)(2,1)S(1)}, bf16[512,512]{1,0:T(8,128)(2,1)S(1)}, u32[]{:S(2)}, u32[]{:S(2)}) collective-permute-start(bf16[512,512]{1,0:T(8,128)(2,1)S(1)} %project.15), channel_id=1, source_target_pairs={{0,2},{2,0},{4,6},{6,4},{1,3},{3,1},{5,7},{7,5},{8,10},{10,8},{12,... | collective-permute-start | bytes 1572872 | tf_op jit(solution)/shard_map/ppermute | solution.py:243

commit v3 on v2

--- a/solution.py
+++ b/solution.py
@@ -64,7 +64,7 @@
 
 def delta(keys, values):
     rows, cols = keys.shape
-    block = 256
+    block = 512
     spec = pl.BlockSpec((block, cols), lambda i: (i, 0))
     return pl.pallas_call(
         delta_kernel,
@@ -89,7 +89,7 @@
     for i in range(rows // QB):
         lo, hi = i * QB, (i + 1) * QB
         q = q_ref[lo:hi, :]
-        f_ref[lo:hi, :] = features(q.astype(F32)).astype(BF16)
+        f_ref[0, lo:hi, :] = features(q.astype(F32)).astype(BF16)
         diag = lax.dot_general(q, k_ref[lo:hi, :], NT, preferred_element_type=F32)
         diag = jnp.where(causal, diag, -1e30)
         top = jnp.max(diag, axis=-1, keepdims=True)
@@ -103,7 +103,7 @@
             w = jnp.exp2((off - top) * c)
             norm += jnp.sum(w, axis=-1, keepdims=True)
             out += jnp.dot(w.astype(BF16), v_ref[:lo, :], preferred_element_type=F32)
-        o_ref[lo:hi, :] = out * (keep / norm)
+        o_ref[0, lo:hi, :] = out * (keep / norm)
 
 
 def attention(gate, queries, keys, values, first, count):
@@ -113,97 +113,147 @@
         functools.partial(attention_kernel, first),
         grid=(count,),
         in_specs=[SMEM] + [spec] * 3,
-        out_specs=[pl.BlockSpec((rows, HD), lambda h: (0, h))] * 2,
-        out_shape=[pltpu.HBM((rows, count * HD), F32), pltpu.HBM((rows, count * HD), BF16)],
+        out_specs=[pl.BlockSpec((1, rows, HD), lambda h: (h, 0, 0))] * 2,
+        out_shape=[pltpu.HBM((count, rows, HD), F32), pltpu.HBM((count, rows, HD), BF16)],
         compiler_params=PARAMS,
         name="attention",
-    )(gate, queries, keys, values)
-
-
-def retrieve_kernel(g_ref, *refs):
+    )(gate, far_memory(queries), far_memory(keys), far_memory(values))
+
+
+def preload_kernel(*refs):
+    half = len(refs) // 2
+    sems = refs[-1]
+    copies = [
+        pltpu.make_async_copy(refs[i], refs[half + i], sems.at[i]) for i in range(half)
+    ]
+    for copy in copies:
+        copy.start()
+    for copy in copies:
+        copy.wait()
+
+
+def preload(arrays):
+    return pl.pallas_call(
+        preload_kernel,
+        in_specs=[pl.BlockSpec(memory_space=pltpu.HBM)] * len(arrays),
+        out_specs=[VMEM] * len(arrays),
+        out_shape=[pltpu.VMEM(a.shape, a.dtype) for a in arrays],
+        scratch_shapes=[pltpu.SemaphoreType.DMA((len(arrays),))],
+        compiler_params=PARAMS,
+        name="preload",
+    )(*[far_memory(a) for a in arrays])
+
+
+def retrieve_kernel(starts, g_ref, *refs):
     *groups, s_ref, o_ref = refs
     base = s_ref.shape[0] - PAD
-    block = groups[0].shape[0]
-    out_rows = pl.ds(pl.multiple_of(pl.program_id(0) * block, block), block)
+    block = o_ref.shape[0] // len(starts)
     h = 0
     for group in range(0, len(groups), 2):
         local, feat = groups[group], groups[group + 1]
-        for at in range(local.shape[1] // HD):
-            cols = slice(at * HD, (at + 1) * HD)
-            f = feat[:, cols]
-            numer = lax.dot_general(
-                f, s_ref[h * HD : (h + 1) * HD, :], NT, preferred_element_type=F32
-            )
-            denom = lax.dot_general(f, s_ref[base:, :], NT, preferred_element_type=F32)
-            scale = g_ref[h] / jnp.maximum(denom[:, h : h + 1], 1.0)
-            mixed = numer * scale + local[:, cols]
-            o_ref[out_rows, h * HD : (h + 1) * HD] = mixed.astype(BF16)
+        for at in range(local.shape[0]):
+            for i, lo in enumerate(starts):
+                f = feat[at, lo : lo + block, :]
+                numer = lax.dot_general(
+                    f, s_ref[h * HD : (h + 1) * HD, :], NT, preferred_element_type=F32
+                )
+                denom = lax.dot_general(f, s_ref[base:, :], NT, preferred_element_type=F32)
+                scale = g_ref[h] / jnp.maximum(denom[:, h : h + 1], 1.0)
+                mixed = numer * scale + local[at, lo : lo + block, :]
+                o_ref[i * block : (i + 1) * block, h * HD : (h + 1) * HD] = mixed.astype(BF16)
             h += 1
 
 
-def retrieve(gate, groups, state, start, rows):
-    flat = [array for group in groups for array in group]
+def retrieve(gate, arrays, state, starts, rows):
     cols = state.shape[0] - PAD
-    block = 128
-    first = start // block
-    specs = [pl.BlockSpec((block, a.shape[1]), lambda i: (first + i, 0)) for a in flat]
-    return pl.pallas_call(
-        retrieve_kernel,
-        grid=(rows // block,),
-        in_specs=[SMEM] + specs + [VMEM],
+    return pl.pallas_call(
+        functools.partial(retrieve_kernel, starts),
+        in_specs=[SMEM] + [VMEM] * (len(arrays) + 1),
         out_specs=VMEM,
         out_shape=pltpu.VMEM((rows, cols), BF16),
         compiler_params=PARAMS,
         name="retrieve",
-    )(gate, *[far_memory(a) for a in flat], near_core(state))
-
-
-def sibling_kernel(at_ref, w_ref, o_ref):
-    o_ref[0] = w_ref[...]
+    )(gate, *[near_core(a) for a in arrays], near_core(state))
+
+
+def sibling_kernel(at_ref, w_ref, o_ref, sems):
+    width = o_ref.shape[2]
+    copies = []
+    for k in range(o_ref.shape[0]):
+        cols = pl.ds(pl.multiple_of((2 * k + 1 - at_ref[1]) * width, width), width)
+        copies.append(pltpu.make_async_copy(w_ref.at[:, cols], o_ref.at[k], sems.at[k]))
+    for copy in copies:
+        copy.start()
+    for copy in copies:
+        copy.wait()
 
 
 def sibling_columns(at, weight):
     depth, cols = weight.shape
-    width = cols // 8
     return pl.pallas_call(
         sibling_kernel,
-        grid_spec=pltpu.PrefetchScalarGridSpec(
-            num_scalar_prefetch=1,
-            grid=(4,),
-            in_specs=[pl.BlockSpec((depth, width), lambda k, at: (0, 2 * k + 1 - at[1]))],
-            out_specs=pl.BlockSpec((1, depth, width), lambda k, at: (k, 0, 0)),
-        ),
-        out_shape=pltpu.HBM((4, depth, width), BF16),
+        in_specs=[SMEM, pl.BlockSpec(memory_space=pltpu.HBM)],
+        out_specs=VMEM,
+        out_shape=pltpu.VMEM((4, depth, cols // 8), BF16),
+        scratch_shapes=[pltpu.SemaphoreType.DMA((4,))],
         compiler_params=PARAMS,
         name="sibling_columns",
     )(at, far_memory(weight))
 
 
-def project_kernel(k, at_ref, a_own, a_sib, w_own, w_sib, *refs):
-    *adds, o_ref = refs
-    rows, width = o_ref.shape
+def block_product(k, at_ref, a_own, a_sib, part, w_own, w_sib, width):
     to = lax.bitwise_xor(at_ref[0], k)
     cols = pl.ds(pl.multiple_of((to * 2 + at_ref[1]) * width, width), width)
-    block = 256
-    for lo in range(0, rows, block):
-        part = slice(lo, lo + block)
-        total = jnp.dot(a_own[part, :], w_own[:, cols], preferred_element_type=F32)
-        total += jnp.dot(a_sib[part, :], w_sib[to], preferred_element_type=F32)
-        for add in adds:
-            total += add[part, :].astype(F32)
-        o_ref[part, :] = total.astype(o_ref.dtype)
-
-
-def project(at, a_own, a_sib, w_own, w_sib, k, adds, dtype):
-    rows, width = a_own.shape[0], w_sib.shape[2]
-    return pl.pallas_call(
-        functools.partial(project_kernel, k),
-        in_specs=[SMEM] + [VMEM] * (4 + len(adds)),
+    total = jnp.dot(a_own[part, :], w_own[:, cols], preferred_element_type=F32)
+    return total + jnp.dot(a_sib[part, :], w_sib[to], preferred_element_type=F32)
+
+
+def far_kernel(at_ref, a_own, a_sib, w_own, w_sib, *outs):
+    block, width = outs[0].shape
+    for i, o_ref in enumerate(outs):
+        part = slice(i * block, (i + 1) * block)
+        total = block_product(2, at_ref, a_own, a_sib, part, w_own, w_sib, width)
+        o_ref[...] = total.astype(o_ref.dtype)
+
+
+def project_far(at, piece, w_own, w_sib):
+    rows, width = piece[0].shape[0], w_sib.shape[2]
+    return pl.pallas_call(
+        far_kernel,
+        in_specs=[SMEM] + [VMEM] * 4,
+        out_specs=[VMEM, VMEM],
+        out_shape=[pltpu.VMEM((rows // 2, width), BF16)] * 2,
+        compiler_params=PARAMS,
+        name="project_far",
+    )(at, *[near_core(a) for a in (*piece, w_own, w_sib)])
+
+
+def project_kernel(k, side, at_ref, a_own1, a_sib1, a_own2, a_sib2, w_own, w_sib, *refs):
+    *adds, o_ref = refs
+    width = o_ref.shape[1]
+    block = o_ref.shape[0] // 2
+    part = slice(side * block, (side + 1) * block)
+    for i, (own, sib) in enumerate(((a_own1, a_sib1), (a_own2, a_sib2))):
+        out = slice(i * block, (i + 1) * block)
+        total = block_product(k, at_ref, own, sib, part, w_own, w_sib, width)
+        if len(adds) == 2:
+            total += adds[i][...].astype(F32)
+        elif adds:
+            total += adds[0][out, :].astype(F32)
+        o_ref[out, :] = total.astype(o_ref.dtype)
+
+
+def project(at, pieces, w_own, w_sib, side, k, adds, dtype):
+    rows, width = pieces[0][0].shape[0], w_sib.shape[2]
+    flat = [array for piece in pieces for array in piece]
+    return pl.pallas_call(
+        functools.partial(project_kernel, k, side),
+        in_specs=[SMEM] + [VMEM] * (6 + len(adds)),
         out_specs=VMEM,
         out_shape=pltpu.VMEM((rows, width), dtype),
         compiler_params=PARAMS,
         name="project",
-    )(at, *[near_core(a) for a in (a_own, a_sib, w_own, w_sib, *adds)])
+    )(at, *[near_core(a) for a in (*flat, w_own, w_sib, *adds)])
 
 
 def finish_kernel(steps, p1, p2, r1, r2, o_ref):
@@ -250,7 +300,6 @@
     gate = jax.nn.sigmoid(gate_bias)
     own = delta(keys, values)
     total, before = own.astype(F32), 0.0
-    groups = []
 
     def fold(axis, mine, masks, beside):
         nonlocal total, before
@@ -260,32 +309,41 @@
             g = g.astype(F32)
             before = before + jnp.where((mine ^ m) < mine, g, 0.0)
             total = total + g
+        total, before = lax.optimization_barrier((total, before))
         return beside
 
-    first = attention(gate, queries, keys, values, 0, heads // 2)
-    first = fold("z", z, (1, 2, 3), first)
-    held, total = lax.optimization_barrier(((queries, keys, values), total))
-    second = attention(gate, *held, heads // 2, heads // 2)
-    second = fold("z", z, (4,), second)
-    weight, total = lax.optimization_barrier((out_weight, total))
-    w_out = sibling_columns(at, weight)
-    w_out = fold("y", y, (1, 2, 3), w_out)
+    weight, _ = lax.optimization_barrier((out_weight, own))
+    w_out = fold("z", z, (1,), sibling_columns(at, weight))
+
     w_own, w_sib = out_weight, swap(w_out, "c", 1)
+
+    def heads_after(done, start):
+        held, _ = lax.optimization_barrier(((queries, keys, values), done))
+        return attention(gate, *held, start, heads // 2)
+
+    first = fold("z", z, (2,), heads_after(total, 0))
+    second = fold("z", z, (7,), heads_after(total, heads // 2))
+    waiting = (*first, *second)
+    waiting, _ = lax.optimization_barrier((waiting, total))
+    arrays = fold("y", y, (1, 2, 3), preload(waiting))
     state = before.astype(BF16)
 
     half = queries.shape[0] // 2
-    halves = []
-    for start in (0, half):
-        a_own = retrieve(gate, (first, second), state, start, half)
-        halves.append((a_own, swap(a_own, "c", 1)))
-
-    def mm(i, k, adds, dtype):
-        return project(at, *halves[i], w_own, w_sib, k, adds, dtype)
+    pieces = []
+    for start in (0, half // 2):
+        a_own = retrieve(gate, arrays, state, (start, start + half), half)
+        pieces.append((a_own, swap(a_own, "c", 1)))
+
+    def mm(side, k, adds, dtype):
+        return project(at, pieces, w_own, w_sib, side, k, adds, dtype)
 
     hops = ((1, 3), (3, 1))
-    far = [swap(mm(i, 2, (), BF16), "x", hops[i][0]) for i in range(2)]
+    far = [[], []]
+    for piece in pieces:
+        for side, part in enumerate(project_far(at, piece, w_own, w_sib)):
+            far[side].append(swap(part, "x", hops[side][0]))
     near = [swap(mm(i, hops[i][0], (), BF16), "x", hops[i][0]) for i in range(2)]
-    passed = [swap(mm(i, hops[i][1], (far[i],), BF16), "x", hops[i][1]) for i in range(2)]
+    passed = [swap(mm(i, hops[i][1], far[i], BF16), "x", hops[i][1]) for i in range(2)]
     mine = [mm(i, 0, (near[i],), F32) for i in range(2)]
     return finish(*mine, *passed)
 

time: 92.6 us -> 89.6 us (0.968)
  Pallas kernels: 35.7 us -> 32.2 us
  waiting for transfers between devices: 29.2 us -> 30.7 us
  local copies, waits for them, and re-layouts: 1.24 us -> 0.01 us
    pallas_call x11 -> x12, Pallas kernels: 20.8 us -> 17.4 us  [the longest x6 7.52 us: project(): pl.pallas_call(functools.partial(project_kernel, k, side), in_specs=[SMEM...]
    ppermute x16 -> x17, waiting for transfers between devices: 29.2 us -> 30.7 us  [swap(): return lax.ppermute(array, axis, [(i, i ^ mask) for i in range(size)])]
    unnamed x12 -> x4, local copies, waits for them, and re-layouts: 1.24 us -> 0.01 us
    pallas_call x1, Pallas kernels: 3.4 us -> 2.37 us  [delta(): pl.pallas_call(delta_kernel, grid=(rows // block,), in_specs=[spec, spec]...]
    ppermute x16 -> x17, starting transfers between devices: 25.6 us -> 25.7 us  [swap(): return lax.ppermute(array, axis, [(i, i ^ mask) for i in range(size)])]
  transfers between devices with their start and end apart: 16 -> 17, of which waited for: 6 -> 10; matrix products, arithmetic and copies ran while one was open for 0% -> 0% of each run, Pallas kernels for 33% -> 32%
where the time goes in v3:
time: 89.6 us; the launch traced here: 89.2 us
  Pallas kernels  32.2 us (36%)
  waiting for transfers between devices  30.7 us (34%)
  starting transfers between devices  25.7 us (29%)
    ppermute x17, waiting for transfers between devices, swap(): return lax.ppermute(array, axis, [(i, i ^ mask) for i in range(size)])  30.7 us
    ppermute x17, starting transfers between devices, swap(): return lax.ppermute(array, axis, [(i, i ^ mask) for i in range(size)])  25.7 us
    pallas_call x2, Pallas kernels, attention(): pl.pallas_call(functools.partial(attention_kernel, first), grid=(count,),...  10.8 us
    pallas_call x6, Pallas kernels, project(): pl.pallas_call(functools.partial(project_kernel, k, side), in_specs=[SMEM...  7.52 us
    pallas_call x1, Pallas kernels, sibling_columns(): pl.pallas_call(sibling_kernel, in_specs=[SMEM, pl.BlockSpec(memory_space=...  3.44 us
    pallas_call x2, Pallas kernels, project_far(): pl.pallas_call(far_kernel, in_specs=[SMEM] + [VMEM] * 4, out_specs=[VMEM,...  2.5 us
    pallas_call x1, Pallas kernels, delta(): pl.pallas_call(delta_kernel, grid=(rows // block,), in_specs=[spec, spec]...  2.37 us
    pallas_call x2, Pallas kernels, retrieve(): pl.pallas_call(functools.partial(retrieve_kernel, starts), in_specs=[SMEM...  2.11 us
  transfers between devices with their start and end apart: 17, of which 10 were waited for; matrix products, arithmetic and copies ran while one was open for 0% of the time, Pallas kernels for 32%

profile of v3, /device:TPU:1, one launch (start us, length us, event | category | flops | bytes accessed | tf_op | source)
XLA Modules:
  0.0 89.2 jit_solution(5783067121198436996)
XLA Ops:
  0.0 2.4 %delta.1 = bf16[528,128]{1,0:T(8,128)(2,1)S(1)} custom-call(bf16[1024,512]{1,0:T(8,128)(2,1)} %k_ref.3, bf16[1024,512]{1,0:T(8,128)(2,1)} %v_ref.3), custom_call_target="tpu_custom_call" | custom-call | tf_op jit(solution)/shard_map/delta/pallas_call | solution.py:69
  2.4 2.5 %collective-permute-start = (bf16[528,128]{1,0:T(8,128)(2,1)S(1)}, bf16[528,128]{1,0:T(8,128)(2,1)S(1)}, u32[]{:S(2)}, u32[]{:S(2)}) collective-permute-start(bf16[528,128]{1,0:T(8,128)(2,1)S(1)} %delta.1), channel_id=1, source_target_pairs={{0,8},{8,0},{16,24},{24,16},{32,40},{40,32},{48,56},{56,48},{1,9},... | collective-permute-start | bytes 405512 | tf_op jit(solution)/shard_map/ppermute | solution.py:293
  4.9 0.1 pad_add_fusion.at_ref
  5.0 0.0 copy-start.1
  5.0 3.4 %sibling_columns.1 = bf16[4,512,512]{2,1,0:T(8,128)(2,1)} custom-call(s32[2]{0:T(128)S(1)} %pad_add_fusion.at_ref, bf16[512,4096]{1,0:T(8,128)(2,1)} %w_own.15), custom_call_target="tpu_custom_call" | custom-call | tf_op jit(solution)/shard_map/sibling_columns/pallas_call | solution.py:193
  8.5 0.0 collective-permute-done
  8.5 2.3 %collective-permute-start.8 = (bf16[4,512,512]{2,1,0:T(8,128)(2,1)}, bf16[4,512,512]{2,1,0:T(8,128)(2,1)S(1)}, u32[]{:S(2)}, u32[]{:S(2)}) collective-permute-start(bf16[4,512,512]{2,1,0:T(8,128)(2,1)} %sibling_columns.1), channel_id=1, source_target_pairs={{0,1},{1,0},{2,3},{3,2},{4,5},{5,4},{6,7},{7,6},{8,9},{9,8},{10,11... | collective-permute-start | bytes 6291464 | tf_op jit(solution)/shard_map/ppermute | solution.py:293
  10.8 1.9 %collective-permute-start.1 = (bf16[528,128]{1,0:T(8,128)(2,1)S(1)}, bf16[528,128]{1,0:T(8,128)(2,1)S(1)}, u32[]{:S(2)}, u32[]{:S(2)}) collective-permute-start(bf16[528,128]{1,0:T(8,128)(2,1)S(1)} %convert_element_type.38), channel_id=1, source_target_pairs={{0,16},{8,24},{16,0},{24,8},{32,48},{40,56},{48,32},{56,40},{1,17}... | collective-permute-start | bytes 405512 | tf_op jit(solution)/shard_map/ppermute | solution.py:293
  12.6 0.0 copy-done.1
  12.7 5.4 %attention.2 = (f32[2,1024,128]{2,1,0:T(8,128)}, bf16[2,1024,128]{2,1,0:T(8,128)(2,1)}) custom-call(f32[4]{0:T(128)S(1)} %add_divide_fusion.g_ref, bf16[1024,512]{1,0:T(8,128)(2,1)} %q_ref.1, bf16[1024,512]{1,0:T(8,128)(2,1)} %k_ref.3, bf16[1024,512]{1,0:T(8,128)(2,1)} %v_ref.3), custom_call_target="tpu_custom_call" | custom-call | tf_op jit(solution)/shard_map/attention/pallas_call | solution.py:112
  18.1 1.8 %collective-permute-done.1 = bf16[528,128]{1,0:T(8,128)(2,1)S(1)} collective-permute-done((bf16[528,128]{1,0:T(8,128)(2,1)S(1)}, bf16[528,128]{1,0:T(8,128)(2,1)S(1)}, u32[]{:S(2)}, u32[]{:S(2)}) %collective-permute-start.1) | collective-permute-done | bytes 135200 | tf_op jit(solution)/shard_map/ppermute | solution.py:293
  20.0 4.2 %collective-permute-start.2 = (bf16[528,128]{1,0:T(8,128)(2,1)S(1)}, bf16[528,128]{1,0:T(8,128)(2,1)S(1)}, u32[]{:S(2)}, u32[]{:S(2)}) collective-permute-start(bf16[528,128]{1,0:T(8,128)(2,1)S(1)} %convert_element_type.40), channel_id=1, source_target_pairs={{0,56},{8,48},{16,40},{24,32},{32,24},{40,16},{48,8},{56,0},{1,57}... | collective-permute-start | bytes 405512 | tf_op jit(solution)/shard_map/ppermute | solution.py:293
  24.2 5.4 %attention.3 = (f32[2,1024,128]{2,1,0:T(8,128)}, bf16[2,1024,128]{2,1,0:T(8,128)(2,1)}) custom-call(f32[4]{0:T(128)S(1)} %add_divide_fusion.g_ref, bf16[1024,512]{1,0:T(8,128)(2,1)} %q_ref.1, bf16[1024,512]{1,0:T(8,128)(2,1)} %k_ref.3, bf16[1024,512]{1,0:T(8,128)(2,1)} %v_ref.3), custom_call_target="tpu_custom_call" | custom-call | tf_op jit(solution)/shard_map/attention/pallas_call | solution.py:112
  29.6 0.9 collective-permute-done.2
  30.6 1.4 %collective-permute-start.3 = (bf16[528,128]{1,0:T(8,128)(2,1)S(1)}, bf16[528,128]{1,0:T(8,128)(2,1)S(1)}, u32[]{:S(2)}, u32[]{:S(2)}) collective-permute-start(bf16[528,128]{1,0:T(8,128)(2,1)S(1)} %convert_add_fusion), channel_id=1, source_target_pairs={{0,64},{64,0},{128,192},{192,128},{1,65},{65,1},{129,193},{193,129... | collective-permute-start | bytes 405512 | tf_op jit(solution)/shard_map/ppermute | solution.py:293
  31.9 2.6 %collective-permute-start.4 = (bf16[528,128]{1,0:T(8,128)(2,1)S(1)}, bf16[528,128]{1,0:T(8,128)(2,1)S(1)}, u32[]{:S(2)}, u32[]{:S(2)}) collective-permute-start(bf16[528,128]{1,0:T(8,128)(2,1)S(1)} %convert_add_fusion), channel_id=1, source_target_pairs={{0,128},{64,192},{128,0},{192,64},{1,129},{65,193},{129,1},{193,65... | collective-permute-start | bytes 405512 | tf_op jit(solution)/shard_map/ppermute | solution.py:293
  34.6 0.0 collective-permute-start.5
  34.6 1.9 %preload.1 = (f32[2,1024,128]{2,1,0:T(8,128)S(1)}, bf16[2,1024,128]{2,1,0:T(8,128)(2,1)S(1)}, f32[2,1024,128]{2,1,0:T(8,128)S(1)}, bf16[2,1024,128]{2,1,0:T(8,128)(2,1)S(1)}) custom-call(f32[2,1024,128]{2,1,0:T(8,128)} %get-tuple-element.72.refs_0_, bf16[2,1024,128]{2,1,0:T(8,128)(2,1)} %get-tuple-element.73.refs_1_, ...), custom_call_target="tpu_custom_call" | custom-call | tf_op jit(solution)/shard_map/preload/pallas_call | solution.py:136
  36.4 0.0 collective-permute-done.3
  36.5 4.3 %collective-permute-done.4 = bf16[528,128]{1,0:T(8,128)(2,1)S(1)} collective-permute-done((bf16[528,128]{1,0:T(8,128)(2,1)S(1)}, bf16[528,128]{1,0:T(8,128)(2,1)S(1)}, u32[]{:S(2)}, u32[]{:S(2)}) %collective-permute-start.4) | collective-permute-done | bytes 135200 | tf_op jit(solution)/shard_map/ppermute | solution.py:293
  40.7 2.5 %collective-permute-done.5 = bf16[528,128]{1,0:T(8,128)(2,1)S(1)} collective-permute-done((bf16[528,128]{1,0:T(8,128)(2,1)S(1)}, bf16[528,128]{1,0:T(8,128)(2,1)S(1)}, u32[]{:S(2)}, u32[]{:S(2)}) %collective-permute-start.5) | collective-permute-done | bytes 135200 | tf_op jit(solution)/shard_map/ppermute | solution.py:293
  43.2 0.1 select_add_fusion.refs_4_
  43.3 0.0 copy-start
  43.3 1.1 %retrieve.3.a_own2.a_own = bf16[512,512]{1,0:T(8,128)(2,1)S(1)} custom-call(f32[4]{0:T(128)S(1)} %add_divide_fusion.g_ref, f32[2,1024,128]{2,1,0:T(8,128)S(1)} %get-tuple-element.80.refs_0_, bf16[2,1024,128]{2,1,0:T(8,128)(2,1)S(1)} %get-tuple-element.81.refs_1_, f32[2,1024,128]{2,1,0:T(8,128)S(1)} %get-tuple-element.82.refs_2_, ...), custom_call_target="tpu_custom_call" | custom-call | tf_op jit(solution)/shard_map/retrieve/pallas_call | solution.py:169
  44.4 1.2 %collective-permute-start.7 = (bf16[512,512]{1,0:T(8,128)(2,1)S(1)}, bf16[512,512]{1,0:T(8,128)(2,1)S(1)}, u32[]{:S(2)}, u32[]{:S(2)}) collective-permute-start(bf16[512,512]{1,0:T(8,128)(2,1)S(1)} %retrieve.3.a_own2.a_own), channel_id=1, source_target_pairs={{0,1},{1,0},{2,3},{3,2},{4,5},{5,4},{6,7},{7,6},{8,9},{9,8},{10,11... | collective-permute-start | bytes 1572872 | tf_op jit(solution)/shard_map/ppermute | solution.py:293
  45.6 1.1 %retrieve.2.a_own1.a_own = bf16[512,512]{1,0:T(8,128)(2,1)S(1)} custom-call(f32[4]{0:T(128)S(1)} %add_divide_fusion.g_ref, f32[2,1024,128]{2,1,0:T(8,128)S(1)} %get-tuple-element.80.refs_0_, bf16[2,1024,128]{2,1,0:T(8,128)(2,1)S(1)} %get-tuple-element.81.refs_1_, f32[2,1024,128]{2,1,0:T(8,128)S(1)} %get-tuple-element.82.refs_2_, ...), custom_call_target="tpu_custom_call" | custom-call | tf_op jit(solution)/shard_map/retrieve/pallas_call | solution.py:169
  46.6 0.1 collective-permute-start.6
  46.7 0.4 collective-permute-done.7.a_sib2.a_sib
  47.1 0.0 collective-permute-done.8.w_sib
  47.1 0.0 copy-done
  47.1 1.2 %project_far.3 = (bf16[256,512]{1,0:T(8,128)(2,1)S(1)}, bf16[256,512]{1,0:T(8,128)(2,1)S(1)}) custom-call(s32[2]{0:T(128)S(1)} %pad_add_fusion.at_ref, bf16[512,512]{1,0:T(8,128)(2,1)S(1)} %retrieve.3.a_own2.a_own, bf16[512,512]{1,0:T(8,128)(2,1)S(1)} %collective-permute-done.7.a_sib2.a_sib, bf16[512,4096]{1,0:T(8,128)(2,1)S(1)} %copy-done, ...), custom_call_target="tpu_custom_call" | custom-call | tf_op jit(solution)/shard_map/project_far/pallas_call | solution.py:221
  48.4 2.6 %collective-permute-start.15 = (bf16[256,512]{1,0:T(8,128)(2,1)S(1)}, bf16[256,512]{1,0:T(8,128)(2,1)S(1)}, u32[]{:S(2)}, u32[]{:S(2)}) collective-permute-start(bf16[256,512]{1,0:T(8,128)(2,1)S(1)} %get-tuple-element.92), channel_id=1, source_target_pairs={{0,6},{2,4},{4,2},{6,0},{1,7},{3,5},{5,3},{7,1},{8,14},{10,12},{12... | collective-permute-start | bytes 786440 | tf_op jit(solution)/shard_map/ppermute | solution.py:293
  50.9 0.0 collective-permute-done.6.a_sib1.a_sib
  51.0 1.3 %project_far.2 = (bf16[256,512]{1,0:T(8,128)(2,1)S(1)}, bf16[256,512]{1,0:T(8,128)(2,1)S(1)}) custom-call(s32[2]{0:T(128)S(1)} %pad_add_fusion.at_ref, bf16[512,512]{1,0:T(8,128)(2,1)S(1)} %retrieve.2.a_own1.a_own, bf16[512,512]{1,0:T(8,128)(2,1)S(1)} %collective-permute-done.6.a_sib1.a_sib, bf16[512,4096]{1,0:T(8,128)(2,1)S(1)} %copy-done, ...), custom_call_target="tpu_custom_call" | custom-call | tf_op jit(solution)/shard_map/project_far/pallas_call | solution.py:221
  52.2 0.3 collective-permute-start.14
  52.5 0.1 collective-permute-start.12
  52.6 1.5 %collective-permute-start.11 = (bf16[256,512]{1,0:T(8,128)(2,1)S(1)}, bf16[256,512]{1,0:T(8,128)(2,1)S(1)}, u32[]{:S(2)}, u32[]{:S(2)}) collective-permute-start(bf16[256,512]{1,0:T(8,128)(2,1)S(1)} %get-tuple-element.89), channel_id=1, source_target_pairs={{0,2},{2,0},{4,6},{6,4},{1,3},{3,1},{5,7},{7,5},{8,10},{10,8},{12,... | collective-permute-start | bytes 786440 | tf_op jit(solution)/shard_map/ppermute | solution.py:293
  54.0 1.2 %project.8 = bf16[512,512]{1,0:T(8,128)(2,1)S(1)} custom-call(s32[2]{0:T(128)S(1)} %pad_add_fusion.at_ref, bf16[512,512]{1,0:T(8,128)(2,1)S(1)} %retrieve.2.a_own1.a_own, bf16[512,512]{1,0:T(8,128)(2,1)S(1)} %collective-permute-done.6.a_sib1.a_sib, bf16[512,512]{1,0:T(8,128)(2,1)S(1)} %retrieve.3.a_own2.a_own, ...), custom_call_target="tpu_custom_call" | custom-call | tf_op jit(solution)/shard_map/project/pallas_call | solution.py:249
  55.3 2.5 %collective-permute-start.10 = (bf16[512,512]{1,0:T(8,128)(2,1)S(1)}, bf16[512,512]{1,0:T(8,128)(2,1)S(1)}, u32[]{:S(2)}, u32[]{:S(2)}) collective-permute-start(bf16[512,512]{1,0:T(8,128)(2,1)S(1)} %project.8), channel_id=1, source_target_pairs={{0,6},{2,4},{4,2},{6,0},{1,7},{3,5},{5,3},{7,1},{8,14},{10,12},{12... | collective-permute-start | bytes 1572872 | tf_op jit(solution)/shard_map/ppermute | solution.py:293
  57.8 1.2 %project.6 = bf16[512,512]{1,0:T(8,128)(2,1)S(1)} custom-call(s32[2]{0:T(128)S(1)} %pad_add_fusion.at_ref, bf16[512,512]{1,0:T(8,128)(2,1)S(1)} %retrieve.2.a_own1.a_own, bf16[512,512]{1,0:T(8,128)(2,1)S(1)} %collective-permute-done.6.a_sib1.a_sib, bf16[512,512]{1,0:T(8,128)(2,1)S(1)} %retrieve.3.a_own2.a_own, ...), custom_call_target="tpu_custom_call" | custom-call | tf_op jit(solution)/shard_map/project/pallas_call | solution.py:249
  59.0 0.0 collective-permute-done.15.refs_1_
  59.1 0.1 collective-permute-start.9
  59.2 3.7 %collective-permute-done.14.refs_0_ = bf16[256,512]{1,0:T(8,128)(2,1)S(1)} collective-permute-done((bf16[256,512]{1,0:T(8,128)(2,1)S(1)}, bf16[256,512]{1,0:T(8,128)(2,1)S(1)}, u32[]{:S(2)}, u32[]{:S(2)}) %collective-permute-start.14) | collective-permute-done | bytes 262176 | tf_op jit(solution)/shard_map/ppermute | solution.py:293
  62.8 1.3 %project.11 = bf16[512,512]{1,0:T(8,128)(2,1)S(1)} custom-call(s32[2]{0:T(128)S(1)} %pad_add_fusion.at_ref, bf16[512,512]{1,0:T(8,128)(2,1)S(1)} %retrieve.2.a_own1.a_own, bf16[512,512]{1,0:T(8,128)(2,1)S(1)} %collective-permute-done.6.a_sib1.a_sib, bf16[512,512]{1,0:T(8,128)(2,1)S(1)} %retrieve.3.a_own2.a_own, ...), custom_call_target="tpu_custom_call" | custom-call | tf_op jit(solution)/shard_map/project/pallas_call | solution.py:249
  64.1 0.1 collective-permute-start.16
  64.2 0.0 collective-permute-done.12.refs_1_
  64.2 1.0 %collective-permute-done.11.refs_0_ = bf16[256,512]{1,0:T(8,128)(2,1)S(1)} collective-permute-done((bf16[256,512]{1,0:T(8,128)(2,1)S(1)}, bf16[256,512]{1,0:T(8,128)(2,1)S(1)}, u32[]{:S(2)}, u32[]{:S(2)}) %collective-permute-start.11) | collective-permute-done | bytes 262176 | tf_op jit(solution)/shard_map/ppermute | solution.py:293
  65.2 1.3 %project.10 = bf16[512,512]{1,0:T(8,128)(2,1)S(1)} custom-call(s32[2]{0:T(128)S(1)} %pad_add_fusion.at_ref, bf16[512,512]{1,0:T(8,128)(2,1)S(1)} %retrieve.2.a_own1.a_own, bf16[512,512]{1,0:T(8,128)(2,1)S(1)} %collective-permute-done.6.a_sib1.a_sib, bf16[512,512]{1,0:T(8,128)(2,1)S(1)} %retrieve.3.a_own2.a_own, ...), custom_call_target="tpu_custom_call" | custom-call | tf_op jit(solution)/shard_map/project/pallas_call | solution.py:249
  66.4 2.4 %collective-permute-start.13 = (bf16[512,512]{1,0:T(8,128)(2,1)S(1)}, bf16[512,512]{1,0:T(8,128)(2,1)S(1)}, u32[]{:S(2)}, u32[]{:S(2)}) collective-permute-start(bf16[512,512]{1,0:T(8,128)(2,1)S(1)} %project.10), channel_id=1, source_target_pairs={{0,6},{2,4},{4,2},{6,0},{1,7},{3,5},{5,3},{7,1},{8,14},{10,12},{12... | collective-permute-start | bytes 1572872 | tf_op jit(solution)/shard_map/ppermute | solution.py:293
  68.8 5.2 %collective-permute-done.10.refs_0_ = bf16[512,512]{1,0:T(8,128)(2,1)S(1)} collective-permute-done((bf16[512,512]{1,0:T(8,128)(2,1)S(1)}, bf16[512,512]{1,0:T(8,128)(2,1)S(1)}, u32[]{:S(2)}, u32[]{:S(2)}) %collective-permute-start.10) | collective-permute-done | bytes 524320 | tf_op jit(solution)/shard_map/ppermute | solution.py:293
  74.1 1.3 %project.9.p2 = f32[512,512]{1,0:T(8,128)S(1)} custom-call(s32[2]{0:T(128)S(1)} %pad_add_fusion.at_ref, bf16[512,512]{1,0:T(8,128)(2,1)S(1)} %retrieve.2.a_own1.a_own, bf16[512,512]{1,0:T(8,128)(2,1)S(1)} %collective-permute-done.6.a_sib1.a_sib, bf16[512,512]{1,0:T(8,128)(2,1)S(1)} %retrieve.3.a_own2.a_own, ...), custom_call_target="tpu_custom_call" | custom-call | tf_op jit(solution)/shard_map/project/pallas_call | solution.py:249
  75.3 1.1 %collective-permute-done.9.refs_0_ = bf16[512,512]{1,0:T(8,128)(2,1)S(1)} collective-permute-done((bf16[512,512]{1,0:T(8,128)(2,1)S(1)}, bf16[512,512]{1,0:T(8,128)(2,1)S(1)}, u32[]{:S(2)}, u32[]{:S(2)}) %collective-permute-start.9) | collective-permute-done | bytes 524320 | tf_op jit(solution)/shard_map/ppermute | solution.py:293
  76.4 1.3 %project.7.p1 = f32[512,512]{1,0:T(8,128)S(1)} custom-call(s32[2]{0:T(128)S(1)} %pad_add_fusion.at_ref, bf16[512,512]{1,0:T(8,128)(2,1)S(1)} %retrieve.2.a_own1.a_own, bf16[512,512]{1,0:T(8,128)(2,1)S(1)} %collective-permute-done.6.a_sib1.a_sib, bf16[512,512]{1,0:T(8,128)(2,1)S(1)} %retrieve.3.a_own2.a_own, ...), custom_call_target="tpu_custom_call" | custom-call | tf_op jit(solution)/shard_map/project/pallas_call | solution.py:249
  77.7 10.0 %collective-permute-done.16.r2 = bf16[512,512]{1,0:T(8,128)(2,1)S(1)} collective-permute-done((bf16[512,512]{1,0:T(8,128)(2,1)S(1)}, bf16[512,512]{1,0:T(8,128)(2,1)S(1)}, u32[]{:S(2)}, u32[]{:S(2)}) %collective-permute-start.16) | collective-permute-done | bytes 524320 | tf_op jit(solution)/shard_map/ppermute | solution.py:293
  87.6 0.0 collective-permute-done.13.r1
  87.6 1.6 %finish.1 = bf16[1024,512]{1,0:T(8,128)(2,1)} custom-call(f32[512,512]{1,0:T(8,128)S(1)} %project.7.p1, f32[512,512]{1,0:T(8,128)S(1)} %project.9.p2, bf16[512,512]{1,0:T(8,128)(2,1)S(1)} %collective-permute-done.13.r1, bf16[512,512]{1,0:T(8,128)(2,1)S(1)} %collective-permute-done.16.r2), custom_call_target="tpu_custom_call" | custom-call | tf_op jit(solution)/shard_map/finish/pallas_call | solution.py:280
  (7 shorter events, 0.2 us)
Async XLA Ops:
  2.4 6.1 %collective-permute-start = (bf16[528,128]{1,0:T(8,128)(2,1)S(1)}, bf16[528,128]{1,0:T(8,128)(2,1)S(1)}, u32[]{:S(2)}, u32[]{:S(2)}) collective-permute-start(bf16[528,128]{1,0:T(8,128)(2,1)S(1)} %delta.1), channel_id=1, source_target_pairs={{0,8},{8,0},{16,24},{24,16},{32,40},{40,32},{48,56},{56,48},{1,9},... | collective-permute-start | bytes 405512 | tf_op jit(solution)/shard_map/ppermute | solution.py:293
  5.0 7.6 %copy-start.1 = (f32[4]{0:T(128)S(1)}, f32[4]{0:T(128)}, u32[]{:S(2)}) copy-start(f32[4]{0:T(128)} %param.8) | copy-start | bytes 52
  8.5 38.7 %collective-permute-start.8 = (bf16[4,512,512]{2,1,0:T(8,128)(2,1)}, bf16[4,512,512]{2,1,0:T(8,128)(2,1)S(1)}, u32[]{:S(2)}, u32[]{:S(2)}) collective-permute-start(bf16[4,512,512]{2,1,0:T(8,128)(2,1)} %sibling_columns.1), channel_id=1, source_target_pairs={{0,1},{1,0},{2,3},{3,2},{4,5},{5,4},{6,7},{7,6},{8,9},{9,8},{10,11... | collective-permute-start | bytes 6291464 | tf_op jit(solution)/shard_map/ppermute | solution.py:293
  10.8 9.1 %collective-permute-start.1 = (bf16[528,128]{1,0:T(8,128)(2,1)S(1)}, bf16[528,128]{1,0:T(8,128)(2,1)S(1)}, u32[]{:S(2)}, u32[]{:S(2)}) collective-permute-start(bf16[528,128]{1,0:T(8,128)(2,1)S(1)} %convert_element_type.38), channel_id=1, source_target_pairs={{0,16},{8,24},{16,0},{24,8},{32,48},{40,56},{48,32},{56,40},{1,17}... | collective-permute-start | bytes 405512 | tf_op jit(solution)/shard_map/ppermute | solution.py:293
  20.0 10.5 %collective-permute-start.2 = (bf16[528,128]{1,0:T(8,128)(2,1)S(1)}, bf16[528,128]{1,0:T(8,128)(2,1)S(1)}, u32[]{:S(2)}, u32[]{:S(2)}) collective-permute-start(bf16[528,128]{1,0:T(8,128)(2,1)S(1)} %convert_element_type.40), channel_id=1, source_target_pairs={{0,56},{8,48},{16,40},{24,32},{32,24},{40,16},{48,8},{56,0},{1,57}... | collective-permute-start | bytes 405512 | tf_op jit(solution)/shard_map/ppermute | solution.py:293
  30.6 5.9 %collective-permute-start.3 = (bf16[528,128]{1,0:T(8,128)(2,1)S(1)}, bf16[528,128]{1,0:T(8,128)(2,1)S(1)}, u32[]{:S(2)}, u32[]{:S(2)}) collective-permute-start(bf16[528,128]{1,0:T(8,128)(2,1)S(1)} %convert_add_fusion), channel_id=1, source_target_pairs={{0,64},{64,0},{128,192},{192,128},{1,65},{65,1},{129,193},{193,129... | collective-permute-start | bytes 405512 | tf_op jit(solution)/shard_map/ppermute | solution.py:293
  31.9 8.8 %collective-permute-start.4 = (bf16[528,128]{1,0:T(8,128)(2,1)S(1)}, bf16[528,128]{1,0:T(8,128)(2,1)S(1)}, u32[]{:S(2)}, u32[]{:S(2)}) collective-permute-start(bf16[528,128]{1,0:T(8,128)(2,1)S(1)} %convert_add_fusion), channel_id=1, source_target_pairs={{0,128},{64,192},{128,0},{192,64},{1,129},{65,193},{129,1},{193,65... | collective-permute-start | bytes 405512 | tf_op jit(solution)/shard_map/ppermute | solution.py:293
  34.6 8.6 %collective-permute-start.5 = (bf16[528,128]{1,0:T(8,128)(2,1)S(1)}, bf16[528,128]{1,0:T(8,128)(2,1)S(1)}, u32[]{:S(2)}, u32[]{:S(2)}) collective-permute-start(bf16[528,128]{1,0:T(8,128)(2,1)S(1)} %convert_add_fusion), channel_id=1, source_target_pairs={{0,192},{64,128},{128,64},{192,0},{1,193},{65,129},{129,65},{193,1... | collective-permute-start | bytes 405512 | tf_op jit(solution)/shard_map/ppermute | solution.py:293
  43.3 3.8 %copy-start = (bf16[512,4096]{1,0:T(8,128)(2,1)S(1)}, bf16[512,4096]{1,0:T(8,128)(2,1)}, u32[]{:S(2)}) copy-start(bf16[512,4096]{1,0:T(8,128)(2,1)} %w_own.15) | copy-start | bytes 12582916
  44.4 2.8 %collective-permute-start.7 = (bf16[512,512]{1,0:T(8,128)(2,1)S(1)}, bf16[512,512]{1,0:T(8,128)(2,1)S(1)}, u32[]{:S(2)}, u32[]{:S(2)}) collective-permute-start(bf16[512,512]{1,0:T(8,128)(2,1)S(1)} %retrieve.3.a_own2.a_own), channel_id=1, source_target_pairs={{0,1},{1,0},{2,3},{3,2},{4,5},{5,4},{6,7},{7,6},{8,9},{9,8},{10,11... | collective-permute-start | bytes 1572872 | tf_op jit(solution)/shard_map/ppermute | solution.py:293
  46.6 4.3 %collective-permute-start.6 = (bf16[512,512]{1,0:T(8,128)(2,1)S(1)}, bf16[512,512]{1,0:T(8,128)(2,1)S(1)}, u32[]{:S(2)}, u32[]{:S(2)}) collective-permute-start(bf16[512,512]{1,0:T(8,128)(2,1)S(1)} %retrieve.2.a_own1.a_own), channel_id=1, source_target_pairs={{0,1},{1,0},{2,3},{3,2},{4,5},{5,4},{6,7},{7,6},{8,9},{9,8},{10,11... | collective-permute-start | bytes 1572872 | tf_op jit(solution)/shard_map/ppermute | solution.py:293
  48.4 10.7 %collective-permute-start.15 = (bf16[256,512]{1,0:T(8,128)(2,1)S(1)}, bf16[256,512]{1,0:T(8,128)(2,1)S(1)}, u32[]{:S(2)}, u32[]{:S(2)}) collective-permute-start(bf16[256,512]{1,0:T(8,128)(2,1)S(1)} %get-tuple-element.92), channel_id=1, source_target_pairs={{0,6},{2,4},{4,2},{6,0},{1,7},{3,5},{5,3},{7,1},{8,14},{10,12},{12... | collective-permute-start | bytes 786440 | tf_op jit(solution)/shard_map/ppermute | solution.py:293
  52.2 10.6 %collective-permute-start.14 = (bf16[256,512]{1,0:T(8,128)(2,1)S(1)}, bf16[256,512]{1,0:T(8,128)(2,1)S(1)}, u32[]{:S(2)}, u32[]{:S(2)}) collective-permute-start(bf16[256,512]{1,0:T(8,128)(2,1)S(1)} %get-tuple-element.91), channel_id=1, source_target_pairs={{0,6},{2,4},{4,2},{6,0},{1,7},{3,5},{5,3},{7,1},{8,14},{10,12},{12... | collective-permute-start | bytes 786440 | tf_op jit(solution)/shard_map/ppermute | solution.py:293
  52.5 11.7 %collective-permute-start.12 = (bf16[256,512]{1,0:T(8,128)(2,1)S(1)}, bf16[256,512]{1,0:T(8,128)(2,1)S(1)}, u32[]{:S(2)}, u32[]{:S(2)}) collective-permute-start(bf16[256,512]{1,0:T(8,128)(2,1)S(1)} %get-tuple-element.90), channel_id=1, source_target_pairs={{0,2},{2,0},{4,6},{6,4},{1,3},{3,1},{5,7},{7,5},{8,10},{10,8},{12,... | collective-permute-start | bytes 786440 | tf_op jit(solution)/shard_map/ppermute | solution.py:293
  52.6 12.6 %collective-permute-start.11 = (bf16[256,512]{1,0:T(8,128)(2,1)S(1)}, bf16[256,512]{1,0:T(8,128)(2,1)S(1)}, u32[]{:S(2)}, u32[]{:S(2)}) collective-permute-start(bf16[256,512]{1,0:T(8,128)(2,1)S(1)} %get-tuple-element.89), channel_id=1, source_target_pairs={{0,2},{2,0},{4,6},{6,4},{1,3},{3,1},{5,7},{7,5},{8,10},{10,8},{12,... | collective-permute-start | bytes 786440 | tf_op jit(solution)/shard_map/ppermute | solution.py:293
  55.3 18.7 %collective-permute-start.10 = (bf16[512,512]{1,0:T(8,128)(2,1)S(1)}, bf16[512,512]{1,0:T(8,128)(2,1)S(1)}, u32[]{:S(2)}, u32[]{:S(2)}) collective-permute-start(bf16[512,512]{1,0:T(8,128)(2,1)S(1)} %project.8), channel_id=1, source_target_pairs={{0,6},{2,4},{4,2},{6,0},{1,7},{3,5},{5,3},{7,1},{8,14},{10,12},{12... | collective-permute-start | bytes 1572872 | tf_op jit(solution)/shard_map/ppermute | solution.py:293
  59.1 17.4 %collective-permute-start.9 = (bf16[512,512]{1,0:T(8,128)(2,1)S(1)}, bf16[512,512]{1,0:T(8,128)(2,1)S(1)}, u32[]{:S(2)}, u32[]{:S(2)}) collective-permute-start(bf16[512,512]{1,0:T(8,128)(2,1)S(1)} %project.6), channel_id=1, source_target_pairs={{0,2},{2,0},{4,6},{6,4},{1,3},{3,1},{5,7},{7,5},{8,10},{10,8},{12,... | collective-permute-start | bytes 1572872 | tf_op jit(solution)/shard_map/ppermute | solution.py:293
  64.1 23.6 %collective-permute-start.16 = (bf16[512,512]{1,0:T(8,128)(2,1)S(1)}, bf16[512,512]{1,0:T(8,128)(2,1)S(1)}, u32[]{:S(2)}, u32[]{:S(2)}) collective-permute-start(bf16[512,512]{1,0:T(8,128)(2,1)S(1)} %project.11), channel_id=1, source_target_pairs={{0,2},{2,0},{4,6},{6,4},{1,3},{3,1},{5,7},{7,5},{8,10},{10,8},{12,... | collective-permute-start | bytes 1572872 | tf_op jit(solution)/shard_map/ppermute | solution.py:293
  66.4 21.2 %collective-permute-start.13 = (bf16[512,512]{1,0:T(8,128)(2,1)S(1)}, bf16[512,512]{1,0:T(8,128)(2,1)S(1)}, u32[]{:S(2)}, u32[]{:S(2)}) collective-permute-start(bf16[512,512]{1,0:T(8,128)(2,1)S(1)} %project.10), channel_id=1, source_target_pairs={{0,6},{2,4},{4,2},{6,0},{1,7},{3,5},{5,3},{7,1},{8,14},{10,12},{12... | collective-permute-start | bytes 1572872 | tf_op jit(solution)/shard_map/ppermute | solution.py:293

commit v4 on v3

--- a/solution.py
+++ b/solution.py
@@ -10,6 +10,7 @@
 from jax.sharding import PartitionSpec as P
 
 HD = 128
+REST = {0: 0, 1: 1, 3: 2}
 PAD = 16
 QB = 256
 NT = (((1,), (1,)), ((), ()))
@@ -86,15 +87,25 @@
     causal = lax.broadcasted_iota(jnp.int32, (QB, QB), 1) <= lax.broadcasted_iota(
         jnp.int32, (QB, QB), 0
     )
-    for i in range(rows // QB):
+    def scores(i):
         lo, hi = i * QB, (i + 1) * QB
         q = q_ref[lo:hi, :]
-        f_ref[0, lo:hi, :] = features(q.astype(F32)).astype(BF16)
         diag = lax.dot_general(q, k_ref[lo:hi, :], NT, preferred_element_type=F32)
         diag = jnp.where(causal, diag, -1e30)
+        if not lo:
+            return diag, None
+        return diag, lax.dot_general(q, k_ref[:lo, :], NT, preferred_element_type=F32)
+
+    blocks = rows // QB
+    ahead = scores(0)
+    for i in range(blocks):
+        lo, hi = i * QB, (i + 1) * QB
+        diag, off = ahead
+        if i + 1 < blocks:
+            ahead = scores(i + 1)
+        f_ref[0, lo:hi, :] = features(q_ref[lo:hi, :].astype(F32)).astype(BF16)
         top = jnp.max(diag, axis=-1, keepdims=True)
         if lo:
-            off = lax.dot_general(q, k_ref[:lo, :], NT, preferred_element_type=F32)
             top = jnp.maximum(top, jnp.max(off, axis=-1, keepdims=True))
         w = jnp.exp2((diag - top) * c)
         norm = jnp.sum(w, axis=-1, keepdims=True)
@@ -176,12 +187,14 @@
     )(gate, *[near_core(a) for a in arrays], near_core(state))
 
 
-def sibling_kernel(at_ref, w_ref, o_ref, sems):
-    width = o_ref.shape[2]
+def sibling_kernel(at_ref, w_ref, far_ref, rest_ref, sems):
+    width = far_ref.shape[1]
     copies = []
-    for k in range(o_ref.shape[0]):
-        cols = pl.ds(pl.multiple_of((2 * k + 1 - at_ref[1]) * width, width), width)
-        copies.append(pltpu.make_async_copy(w_ref.at[:, cols], o_ref.at[k], sems.at[k]))
+    for k in range(4):
+        to = lax.bitwise_xor(at_ref[0], k)
+        cols = pl.ds(pl.multiple_of((2 * to + 1 - at_ref[1]) * width, width), width)
+        target = far_ref if k == 2 else rest_ref.at[REST[k]]
+        copies.append(pltpu.make_async_copy(w_ref.at[:, cols], target, sems.at[k]))
     for copy in copies:
         copy.start()
     for copy in copies:
@@ -193,99 +206,104 @@
     return pl.pallas_call(
         sibling_kernel,
         in_specs=[SMEM, pl.BlockSpec(memory_space=pltpu.HBM)],
-        out_specs=VMEM,
-        out_shape=pltpu.VMEM((4, depth, cols // 8), BF16),
+        out_specs=[VMEM, VMEM],
+        out_shape=[
+            pltpu.VMEM((depth, cols // 8), BF16),
+            pltpu.VMEM((3, depth, cols // 8), BF16),
+        ],
         scratch_shapes=[pltpu.SemaphoreType.DMA((4,))],
         compiler_params=PARAMS,
         name="sibling_columns",
     )(at, far_memory(weight))
 
 
-def block_product(k, at_ref, a_own, a_sib, part, w_own, w_sib, width):
+def own_columns(at_ref, k, width):
     to = lax.bitwise_xor(at_ref[0], k)
-    cols = pl.ds(pl.multiple_of((to * 2 + at_ref[1]) * width, width), width)
-    total = jnp.dot(a_own[part, :], w_own[:, cols], preferred_element_type=F32)
-    return total + jnp.dot(a_sib[part, :], w_sib[to], preferred_element_type=F32)
-
-
-def far_kernel(at_ref, a_own, a_sib, w_own, w_sib, *outs):
-    block, width = outs[0].shape
-    for i, o_ref in enumerate(outs):
-        part = slice(i * block, (i + 1) * block)
-        total = block_product(2, at_ref, a_own, a_sib, part, w_own, w_sib, width)
+    return pl.ds(pl.multiple_of((to * 2 + at_ref[1]) * width, width), width)
+
+
+def far_own_kernel(at_ref, a1, a2, w_own, o1, o2):
+    w = w_own[:, own_columns(at_ref, 2, o1.shape[1])]
+    for a, o_ref in ((a1, o1), (a2, o2)):
+        o_ref[...] = jnp.dot(a[...], w, preferred_element_type=F32)
+
+
+def far_sibling_kernel(a1, a2, w_sib, p1, p2, o1, o2):
+    w = w_sib[...]
+    for a, p, o_ref in ((a1, p1, o1), (a2, p2, o2)):
+        total = p[...] + jnp.dot(a[...], w, preferred_element_type=F32)
         o_ref[...] = total.astype(o_ref.dtype)
 
 
-def project_far(at, piece, w_own, w_sib):
-    rows, width = piece[0].shape[0], w_sib.shape[2]
-    return pl.pallas_call(
-        far_kernel,
-        in_specs=[SMEM] + [VMEM] * 4,
+def project_far(at, halves, w_own, w_sib):
+    rows, width = halves[0][0].shape[0], w_sib.shape[1]
+    (own1, sib1), (own2, sib2) = halves
+    partial = pl.pallas_call(
+        far_own_kernel,
+        in_specs=[SMEM] + [VMEM] * 3,
         out_specs=[VMEM, VMEM],
-        out_shape=[pltpu.VMEM((rows // 2, width), BF16)] * 2,
+        out_shape=[pltpu.VMEM((rows, width), F32)] * 2,
+        compiler_params=PARAMS,
+        name="project_far_own",
+    )(at, *[near_core(a) for a in (own1, own2, w_own)])
+    return pl.pallas_call(
+        far_sibling_kernel,
+        in_specs=[VMEM] * 5,
+        out_specs=[VMEM, VMEM],
+        out_shape=[pltpu.VMEM((rows, width), BF16)] * 2,
         compiler_params=PARAMS,
         name="project_far",
-    )(at, *[near_core(a) for a in (*piece, w_own, w_sib)])
-
-
-def project_kernel(k, side, at_ref, a_own1, a_sib1, a_own2, a_sib2, w_own, w_sib, *refs):
+    )(*[near_core(a) for a in (sib1, sib2, w_sib, *partial)])
+
+
+def project_kernel(k, at_ref, a_own, a_sib, w_own, w_sib, *refs):
     *adds, o_ref = refs
-    width = o_ref.shape[1]
-    block = o_ref.shape[0] // 2
-    part = slice(side * block, (side + 1) * block)
-    for i, (own, sib) in enumerate(((a_own1, a_sib1), (a_own2, a_sib2))):
-        out = slice(i * block, (i + 1) * block)
-        total = block_product(k, at_ref, own, sib, part, w_own, w_sib, width)
-        if len(adds) == 2:
-            total += adds[i][...].astype(F32)
-        elif adds:
-            total += adds[0][out, :].astype(F32)
-        o_ref[out, :] = total.astype(o_ref.dtype)
-
-
-def project(at, pieces, w_own, w_sib, side, k, adds, dtype):
-    rows, width = pieces[0][0].shape[0], w_sib.shape[2]
-    flat = [array for piece in pieces for array in piece]
-    return pl.pallas_call(
-        functools.partial(project_kernel, k, side),
-        in_specs=[SMEM] + [VMEM] * (6 + len(adds)),
+    rows, width = o_ref.shape
+    cols = own_columns(at_ref, k, width)
+    block = 256
+    for lo in range(0, rows, block):
+        part = slice(lo, lo + block)
+        total = jnp.dot(a_own[part, :], w_own[:, cols], preferred_element_type=F32)
+        total += jnp.dot(a_sib[part, :], w_sib[REST[k]], preferred_element_type=F32)
+        for add in adds:
+            total += add[part, :].astype(F32)
+        o_ref[part, :] = total.astype(o_ref.dtype)
+
+
+def project(at, half, w_own, w_sib, k, adds, dtype):
+    rows, width = half[0].shape[0], w_sib.shape[2]
+    return pl.pallas_call(
+        functools.partial(project_kernel, k),
+        in_specs=[SMEM] + [VMEM] * (4 + len(adds)),
         out_specs=VMEM,
         out_shape=pltpu.VMEM((rows, width), dtype),
         compiler_params=PARAMS,
         name="project",
-    )(at, *[near_core(a) for a in (*flat, w_own, w_sib, *adds)])
-
-
-def finish_kernel(steps, p1, p2, r1, r2, o_ref):
-    i = pl.program_id(0)
+    )(at, *[near_core(a) for a in (*half, w_own, w_sib, *adds)])
+
+
+def finish_kernel(p_ref, r_ref, *refs):
+    o_ref = refs[-1]
     block = o_ref.shape[0]
-
-    def write(p, r, step):
-        part = pl.ds(pl.multiple_of(step * block, block), block)
-        o_ref[...] = (p[part, :] + r[part, :].astype(F32)).astype(o_ref.dtype)
-
-    @pl.when(i < steps)
-    def _():
-        write(p1, r1, i)
-
-    @pl.when(i >= steps)
-    def _():
-        write(p2, r2, i - steps)
-
-
-def finish(p1, p2, r1, r2):
-    rows, width = p1.shape
+    part = pl.ds(pl.multiple_of(pl.program_id(0) * block, block), block)
+    o_ref[...] = (p_ref[part, :] + r_ref[part, :].astype(F32)).astype(o_ref.dtype)
+
+
+def finish(total, received, side, before):
+    rows, width = total.shape
     block = 256
     steps = rows // block
-    return pl.pallas_call(
-        functools.partial(finish_kernel, steps),
-        grid=(2 * steps,),
-        in_specs=[VMEM] * 4,
-        out_specs=pl.BlockSpec((block, width), lambda i: (i, 0)),
+    rest = [] if before is None else [before]
+    return pl.pallas_call(
+        finish_kernel,
+        grid=(steps,),
+        in_specs=[VMEM, VMEM] + [pl.BlockSpec(memory_space=pl.ANY)] * len(rest),
+        out_specs=pl.BlockSpec((block, width), lambda i: (side * steps + i, 0)),
         out_shape=jax.ShapeDtypeStruct((2 * rows, width), BF16),
+        input_output_aliases={2: 0} if rest else {},
         compiler_params=PARAMS,
         name="finish",
-    )(*[near_core(a) for a in (p1, p2, r1, r2)])
+    )(near_core(total), near_core(received), *rest)
 
 
 def swap(array, axis, mask):
@@ -315,37 +333,36 @@
     weight, _ = lax.optimization_barrier((out_weight, own))
     w_out = fold("z", z, (1,), sibling_columns(at, weight))
 
-    w_own, w_sib = out_weight, swap(w_out, "c", 1)
-
-    def heads_after(done, start):
+    w_own, w_far = out_weight, swap(w_out[0], "c", 1)
+
+    def heads_after(done):
         held, _ = lax.optimization_barrier(((queries, keys, values), done))
-        return attention(gate, *held, start, heads // 2)
-
-    first = fold("z", z, (2,), heads_after(total, 0))
-    second = fold("z", z, (7,), heads_after(total, heads // 2))
-    waiting = (*first, *second)
+        return attention(gate, *held, 0, heads)
+
+    waiting = fold("z", z, (2, 5, 6), heads_after(total))
     waiting, _ = lax.optimization_barrier((waiting, total))
-    arrays = fold("y", y, (1, 2, 3), preload(waiting))
+    arrays, w_far = fold("y", y, (1, 2, 3), (preload(waiting), w_far))
     state = before.astype(BF16)
+    w_rest, state = lax.optimization_barrier((w_out[1], state))
+    w_sib = swap(w_rest, "c", 1)
 
     half = queries.shape[0] // 2
-    pieces = []
-    for start in (0, half // 2):
-        a_own = retrieve(gate, arrays, state, (start, start + half), half)
-        pieces.append((a_own, swap(a_own, "c", 1)))
+    halves = []
+    for start in (0, half):
+        a_own = retrieve(gate, arrays, state, (start,), half)
+        halves.append((a_own, swap(a_own, "c", 1)))
 
     def mm(side, k, adds, dtype):
-        return project(at, pieces, w_own, w_sib, side, k, adds, dtype)
+        return project(at, halves[side], w_own, w_sib, k, adds, dtype)
 
     hops = ((1, 3), (3, 1))
-    far = [[], []]
-    for piece in pieces:
-        for side, part in enumerate(project_far(at, piece, w_own, w_sib)):
-            far[side].append(swap(part, "x", hops[side][0]))
+    far = project_far(at, halves, w_own, w_far)
+    far = [swap(far[i], "x", hops[i][0]) for i in range(2)]
     near = [swap(mm(i, hops[i][0], (), BF16), "x", hops[i][0]) for i in range(2)]
-    passed = [swap(mm(i, hops[i][1], far[i], BF16), "x", hops[i][1]) for i in range(2)]
+    passed = [swap(mm(i, hops[i][1], (far[i],), BF16), "x", hops[i][1]) for i in range(2)]
     mine = [mm(i, 0, (near[i],), F32) for i in range(2)]
-    return finish(*mine, *passed)
+    out = finish(mine[0], passed[0], 0, None)
+    return finish(mine[1], passed[1], 1, out)
 
 
 def solution(mesh):

time: 89.6 us -> 87.1 us (0.972)
  Pallas kernels: 32.2 us -> 26.5 us
  waiting for transfers between devices: 30.7 us -> 33.7 us
    pallas_call x2 -> x1, Pallas kernels: 10.8 us -> 6.9 us  [attention(): pl.pallas_call(functools.partial(attention_kernel, first), grid=(count,),...]
    ppermute x17, waiting for transfers between devices: 30.7 us -> 33.7 us  [swap(): return lax.ppermute(array, axis, [(i, i ^ mask) for i in range(size)])]
    pallas_call x1, Pallas kernels: 3.44 us -> 2.11 us  [sibling_columns(): pl.pallas_call(sibling_kernel, in_specs=[SMEM, pl.BlockSpec(memory_space=...]
    pallas_call x9 -> x10, Pallas kernels: 11.6 us -> 11.2 us  [the longest x6 7.5 us: project(): pl.pallas_call(functools.partial(project_kernel, k), in_specs=[SMEM] + [V...]
  transfers between devices with their start and end apart: 17 -> 17, of which waited for: 10 -> 10; matrix products, arithmetic and copies ran while one was open for 0% -> 0% of each run, Pallas kernels for 32% -> 27%
where the time goes in v4:
time: 87.1 us; the launch traced here: 86.9 us
  waiting for transfers between devices  33.7 us (39%)
  Pallas kernels  26.5 us (30%)
  starting transfers between devices  26.1 us (30%)
    ppermute x17, waiting for transfers between devices, swap(): return lax.ppermute(array, axis, [(i, i ^ mask) for i in range(size)])  33.7 us
    ppermute x17, starting transfers between devices, swap(): return lax.ppermute(array, axis, [(i, i ^ mask) for i in range(size)])  26.1 us
    pallas_call x6, Pallas kernels, project(): pl.pallas_call(functools.partial(project_kernel, k), in_specs=[SMEM] + [V...  7.5 us
    pallas_call x1, Pallas kernels, attention(): pl.pallas_call(functools.partial(attention_kernel, first), grid=(count,),...  6.9 us
    pallas_call x1, Pallas kernels, delta(): pl.pallas_call(delta_kernel, grid=(rows // block,), in_specs=[spec, spec]...  2.37 us
    pallas_call x1, Pallas kernels, sibling_columns(): pl.pallas_call(sibling_kernel, in_specs=[SMEM, pl.BlockSpec(memory_space=...  2.11 us
    pallas_call x2, Pallas kernels, retrieve(): pl.pallas_call(functools.partial(retrieve_kernel, starts), in_specs=[SMEM...  2.1 us
    pallas_call x1, Pallas kernels, preload(): pl.pallas_call(preload_kernel, in_specs=[pl.BlockSpec(memory_space=pltpu....  1.87 us
  transfers between devices with their start and end apart: 17, of which 10 were waited for; matrix products, arithmetic and copies ran while one was open for 0% of the time, Pallas kernels for 27%

profile of v4, /device:TPU:1, one launch (start us, length us, event | category | flops | bytes accessed | tf_op | source)
XLA Modules:
  0.0 86.9 jit_solution(8289061231735320252)
XLA Ops:
  0.0 2.4 %delta.1 = bf16[528,128]{1,0:T(8,128)(2,1)S(1)} custom-call(bf16[1024,512]{1,0:T(8,128)(2,1)} %k_ref.2, bf16[1024,512]{1,0:T(8,128)(2,1)} %v_ref.2), custom_call_target="tpu_custom_call" | custom-call | tf_op jit(solution)/shard_map/delta/pallas_call | solution.py:70
  2.4 2.5 %collective-permute-start = (bf16[528,128]{1,0:T(8,128)(2,1)S(1)}, bf16[528,128]{1,0:T(8,128)(2,1)S(1)}, u32[]{:S(2)}, u32[]{:S(2)}) collective-permute-start(bf16[528,128]{1,0:T(8,128)(2,1)S(1)} %delta.1), channel_id=1, source_target_pairs={{0,8},{8,0},{16,24},{24,16},{32,40},{40,32},{48,56},{56,48},{1,9},... | collective-permute-start | bytes 405512 | tf_op jit(solution)/shard_map/ppermute | solution.py:311
  4.9 0.1 pad_add_fusion.at_ref
  5.0 0.0 copy-start.1
  5.0 2.1 %sibling_columns.1 = (bf16[512,512]{1,0:T(8,128)(2,1)S(1)}, bf16[3,512,512]{2,1,0:T(8,128)(2,1)S(1)}) custom-call(s32[2]{0:T(128)S(1)} %pad_add_fusion.at_ref, bf16[512,4096]{1,0:T(8,128)(2,1)} %w_own.13), custom_call_target="tpu_custom_call" | custom-call | tf_op jit(solution)/shard_map/sibling_columns/pallas_call | solution.py:206
  7.1 0.2 collective-permute-done
  7.4 3.9 %collective-permute-start.1 = (bf16[528,128]{1,0:T(8,128)(2,1)S(1)}, bf16[528,128]{1,0:T(8,128)(2,1)S(1)}, u32[]{:S(2)}, u32[]{:S(2)}) collective-permute-start(bf16[528,128]{1,0:T(8,128)(2,1)S(1)} %convert_element_type.40), channel_id=1, source_target_pairs={{0,16},{8,24},{16,0},{24,8},{32,48},{40,56},{48,32},{56,40},{1,17}... | collective-permute-start | bytes 405512 | tf_op jit(solution)/shard_map/ppermute | solution.py:311
  11.3 4.3 %collective-permute-start.2 = (bf16[528,128]{1,0:T(8,128)(2,1)S(1)}, bf16[528,128]{1,0:T(8,128)(2,1)S(1)}, u32[]{:S(2)}, u32[]{:S(2)}) collective-permute-start(bf16[528,128]{1,0:T(8,128)(2,1)S(1)} %convert_element_type.40), channel_id=1, source_target_pairs={{0,40},{8,32},{16,56},{24,48},{32,8},{40,0},{48,24},{56,16},{1,41}... | collective-permute-start | bytes 405512 | tf_op jit(solution)/shard_map/ppermute | solution.py:311
  15.6 0.0 collective-permute-start.3
  15.6 0.0 copy-done.1
  15.6 2.2 %collective-permute-start.7 = (bf16[512,512]{1,0:T(8,128)(2,1)S(1)}, bf16[512,512]{1,0:T(8,128)(2,1)S(1)}, u32[]{:S(2)}, u32[]{:S(2)}) collective-permute-start(bf16[512,512]{1,0:T(8,128)(2,1)S(1)} %get-tuple-element.62), channel_id=1, source_target_pairs={{0,1},{1,0},{2,3},{3,2},{4,5},{5,4},{6,7},{7,6},{8,9},{9,8},{10,11... | collective-permute-start | bytes 1572872 | tf_op jit(solution)/shard_map/ppermute | solution.py:311
  17.8 6.9 %attention.1 = (f32[4,1024,128]{2,1,0:T(8,128)}, bf16[4,1024,128]{2,1,0:T(8,128)(2,1)}) custom-call(f32[4]{0:T(128)S(1)} %add_divide_fusion.g_ref, bf16[1024,512]{1,0:T(8,128)(2,1)} %q_ref, bf16[1024,512]{1,0:T(8,128)(2,1)} %k_ref.2, bf16[1024,512]{1,0:T(8,128)(2,1)} %v_ref.2), custom_call_target="tpu_custom_call" | custom-call | tf_op jit(solution)/shard_map/attention/pallas_call | solution.py:123
  24.7 0.0 collective-permute-done.1
  24.7 3.1 %collective-permute-done.2 = bf16[528,128]{1,0:T(8,128)(2,1)S(1)} collective-permute-done((bf16[528,128]{1,0:T(8,128)(2,1)S(1)}, bf16[528,128]{1,0:T(8,128)(2,1)S(1)}, u32[]{:S(2)}, u32[]{:S(2)}) %collective-permute-start.2) | collective-permute-done | bytes 135200 | tf_op jit(solution)/shard_map/ppermute | solution.py:311
  27.7 0.0 collective-permute-done.3
  27.7 0.1 convert_add_fusion
  27.8 0.1 fusion.2
  27.9 1.4 %collective-permute-start.4 = (bf16[528,128]{1,0:T(8,128)(2,1)S(1)}, bf16[528,128]{1,0:T(8,128)(2,1)S(1)}, u32[]{:S(2)}, u32[]{:S(2)}) collective-permute-start(bf16[528,128]{1,0:T(8,128)(2,1)S(1)} %convert_add_fusion), channel_id=1, source_target_pairs={{0,64},{64,0},{128,192},{192,128},{1,65},{65,1},{129,193},{193,129... | collective-permute-start | bytes 405512 | tf_op jit(solution)/shard_map/ppermute | solution.py:311
  29.3 2.6 %collective-permute-start.5 = (bf16[528,128]{1,0:T(8,128)(2,1)S(1)}, bf16[528,128]{1,0:T(8,128)(2,1)S(1)}, u32[]{:S(2)}, u32[]{:S(2)}) collective-permute-start(bf16[528,128]{1,0:T(8,128)(2,1)S(1)} %convert_add_fusion), channel_id=1, source_target_pairs={{0,128},{64,192},{128,0},{192,64},{1,129},{65,193},{129,1},{193,65... | collective-permute-start | bytes 405512 | tf_op jit(solution)/shard_map/ppermute | solution.py:311
  31.9 0.0 collective-permute-start.6
  31.9 1.9 %preload.1 = (f32[4,1024,128]{2,1,0:T(8,128)S(1)}, bf16[4,1024,128]{2,1,0:T(8,128)(2,1)S(1)}) custom-call(f32[4,1024,128]{2,1,0:T(8,128)} %get-tuple-element.58.refs_0_, bf16[4,1024,128]{2,1,0:T(8,128)(2,1)} %get-tuple-element.59.refs_1_), custom_call_target="tpu_custom_call" | custom-call | tf_op jit(solution)/shard_map/preload/pallas_call | solution.py:147
  33.8 0.0 collective-permute-done.4
  33.8 3.3 %collective-permute-done.5 = bf16[528,128]{1,0:T(8,128)(2,1)S(1)} collective-permute-done((bf16[528,128]{1,0:T(8,128)(2,1)S(1)}, bf16[528,128]{1,0:T(8,128)(2,1)S(1)}, u32[]{:S(2)}, u32[]{:S(2)}) %collective-permute-start.5) | collective-permute-done | bytes 135200 | tf_op jit(solution)/shard_map/ppermute | solution.py:311
  37.1 2.8 %collective-permute-done.6 = bf16[528,128]{1,0:T(8,128)(2,1)S(1)} collective-permute-done((bf16[528,128]{1,0:T(8,128)(2,1)S(1)}, bf16[528,128]{1,0:T(8,128)(2,1)S(1)}, u32[]{:S(2)}, u32[]{:S(2)}) %collective-permute-start.6) | collective-permute-done | bytes 135200 | tf_op jit(solution)/shard_map/ppermute | solution.py:311
  39.9 0.0 collective-permute-done.7.w_sib
  39.9 0.1 select_add_fusion.refs_2_
  40.0 1.5 %collective-permute-start.9 = (bf16[3,512,512]{2,1,0:T(8,128)(2,1)S(1)}, bf16[3,512,512]{2,1,0:T(8,128)(2,1)S(1)}, u32[]{:S(2)}, u32[]{:S(2)}) collective-permute-start(bf16[3,512,512]{2,1,0:T(8,128)(2,1)S(1)} %get-tuple-element.71), channel_id=1, source_target_pairs={{0,1},{1,0},{2,3},{3,2},{4,5},{5,4},{6,7},{7,6},{8,9},{9,8},{10,11... | collective-permute-start | bytes 4718600 | tf_op jit(solution)/shard_map/ppermute | solution.py:311
  41.6 0.0 copy-start
  41.6 1.0 %retrieve.3.a1.a_own = bf16[512,512]{1,0:T(8,128)(2,1)S(1)} custom-call(f32[4]{0:T(128)S(1)} %add_divide_fusion.g_ref, f32[4,1024,128]{2,1,0:T(8,128)S(1)} %get-tuple-element.63.refs_0_, bf16[4,1024,128]{2,1,0:T(8,128)(2,1)S(1)} %get-tuple-element.64.refs_1_, bf16[528,128]{1,0:T(8,128)(2,1)S(1)} %select_add_fusion.refs_2_), custom_call_target="tpu_custom_call" | custom-call | tf_op jit(solution)/shard_map/retrieve/pallas_call | solution.py:180
  42.6 1.0 %retrieve.2.a_own.a2 = bf16[512,512]{1,0:T(8,128)(2,1)S(1)} custom-call(f32[4]{0:T(128)S(1)} %add_divide_fusion.g_ref, f32[4,1024,128]{2,1,0:T(8,128)S(1)} %get-tuple-element.63.refs_0_, bf16[4,1024,128]{2,1,0:T(8,128)(2,1)S(1)} %get-tuple-element.64.refs_1_, bf16[528,128]{1,0:T(8,128)(2,1)S(1)} %select_add_fusion.refs_2_), custom_call_target="tpu_custom_call" | custom-call | tf_op jit(solution)/shard_map/retrieve/pallas_call | solution.py:180
  43.7 0.1 collective-permute-start.11
  43.8 0.5 collective-permute-start.8
  44.3 0.0 copy-done
  44.3 1.3 %project_far_own.1 = (f32[512,512]{1,0:T(8,128)S(1)}, f32[512,512]{1,0:T(8,128)S(1)}) custom-call(s32[2]{0:T(128)S(1)} %pad_add_fusion.at_ref, bf16[512,512]{1,0:T(8,128)(2,1)S(1)} %retrieve.3.a1.a_own, bf16[512,512]{1,0:T(8,128)(2,1)S(1)} %retrieve.2.a_own.a2, bf16[512,4096]{1,0:T(8,128)(2,1)S(1)} %copy-done), custom_call_target="tpu_custom_call" | custom-call | tf_op jit(solution)/shard_map/project_far_own/pallas_call | solution.py:241
  45.5 0.1 collective-permute-done.11.a1.a_sib
  45.7 0.7 collective-permute-done.8.a_sib.a2
  46.4 0.7 project_far.1
  47.1 1.3 %collective-permute-start.15 = (bf16[512,512]{1,0:T(8,128)(2,1)S(1)}, bf16[512,512]{1,0:T(8,128)(2,1)S(1)}, u32[]{:S(2)}, u32[]{:S(2)}) collective-permute-start(bf16[512,512]{1,0:T(8,128)(2,1)S(1)} %get-tuple-element.76), channel_id=1, source_target_pairs={{0,2},{2,0},{4,6},{6,4},{1,3},{3,1},{5,7},{7,5},{8,10},{10,8},{12,... | collective-permute-start | bytes 1572872 | tf_op jit(solution)/shard_map/ppermute | solution.py:311
  48.4 1.8 %collective-permute-start.12 = (bf16[512,512]{1,0:T(8,128)(2,1)S(1)}, bf16[512,512]{1,0:T(8,128)(2,1)S(1)}, u32[]{:S(2)}, u32[]{:S(2)}) collective-permute-start(bf16[512,512]{1,0:T(8,128)(2,1)S(1)} %get-tuple-element.75), channel_id=1, source_target_pairs={{0,6},{2,4},{4,2},{6,0},{1,7},{3,5},{5,3},{7,1},{8,14},{10,12},{12... | collective-permute-start | bytes 1572872 | tf_op jit(solution)/shard_map/ppermute | solution.py:311
  50.2 0.0 collective-permute-done.9.w_sib
  50.2 1.2 %project.9 = bf16[512,512]{1,0:T(8,128)(2,1)S(1)} custom-call(s32[2]{0:T(128)S(1)} %pad_add_fusion.at_ref, bf16[512,512]{1,0:T(8,128)(2,1)S(1)} %retrieve.3.a1.a_own, bf16[512,512]{1,0:T(8,128)(2,1)S(1)} %collective-permute-done.11.a1.a_sib, bf16[512,4096]{1,0:T(8,128)(2,1)S(1)} %copy-done, bf16[3,512,512]{2,1,0:T(8,128)(2,1)S(1)} %collective-permute-done.9.w_sib), custom_call_target="tpu_custom_call" | custom-call | tf_op jit(solution)/shard_map/project/pallas_call | solution.py:275
  51.5 0.6 collective-permute-start.14
  52.1 1.2 %project.6 = bf16[512,512]{1,0:T(8,128)(2,1)S(1)} custom-call(s32[2]{0:T(128)S(1)} %pad_add_fusion.at_ref, bf16[512,512]{1,0:T(8,128)(2,1)S(1)} %retrieve.2.a_own.a2, bf16[512,512]{1,0:T(8,128)(2,1)S(1)} %collective-permute-done.8.a_sib.a2, bf16[512,4096]{1,0:T(8,128)(2,1)S(1)} %copy-done, bf16[3,512,512]{2,1,0:T(8,128)(2,1)S(1)} %collective-permute-done.9.w_sib), custom_call_target="tpu_custom_call" | custom-call | tf_op jit(solution)/shard_map/project/pallas_call | solution.py:275
  53.3 0.7 collective-permute-start.10
  54.0 6.6 %collective-permute-done.15.refs_0_ = bf16[512,512]{1,0:T(8,128)(2,1)S(1)} collective-permute-done((bf16[512,512]{1,0:T(8,128)(2,1)S(1)}, bf16[512,512]{1,0:T(8,128)(2,1)S(1)}, u32[]{:S(2)}, u32[]{:S(2)}) %collective-permute-start.15) | collective-permute-done | bytes 524320 | tf_op jit(solution)/shard_map/ppermute | solution.py:311
  60.6 1.3 %project.11 = bf16[512,512]{1,0:T(8,128)(2,1)S(1)} custom-call(s32[2]{0:T(128)S(1)} %pad_add_fusion.at_ref, bf16[512,512]{1,0:T(8,128)(2,1)S(1)} %retrieve.3.a1.a_own, bf16[512,512]{1,0:T(8,128)(2,1)S(1)} %collective-permute-done.11.a1.a_sib, bf16[512,4096]{1,0:T(8,128)(2,1)S(1)} %copy-done, bf16[3,512,512]{2,1,0:T(8,128)(2,1)S(1)} %collective-permute-done.9.w_sib, ...), custom_call_target="tpu_custom_call" | custom-call | tf_op jit(solution)/shard_map/project/pallas_call | solution.py:275
  61.9 2.6 %collective-permute-start.16 = (bf16[512,512]{1,0:T(8,128)(2,1)S(1)}, bf16[512,512]{1,0:T(8,128)(2,1)S(1)}, u32[]{:S(2)}, u32[]{:S(2)}) collective-permute-start(bf16[512,512]{1,0:T(8,128)(2,1)S(1)} %project.11), channel_id=1, source_target_pairs={{0,6},{2,4},{4,2},{6,0},{1,7},{3,5},{5,3},{7,1},{8,14},{10,12},{12... | collective-permute-start | bytes 1572872 | tf_op jit(solution)/shard_map/ppermute | solution.py:311
  64.4 0.0 collective-permute-done.12.refs_0_
  64.4 1.2 %project.8 = bf16[512,512]{1,0:T(8,128)(2,1)S(1)} custom-call(s32[2]{0:T(128)S(1)} %pad_add_fusion.at_ref, bf16[512,512]{1,0:T(8,128)(2,1)S(1)} %retrieve.2.a_own.a2, bf16[512,512]{1,0:T(8,128)(2,1)S(1)} %collective-permute-done.8.a_sib.a2, bf16[512,4096]{1,0:T(8,128)(2,1)S(1)} %copy-done, bf16[3,512,512]{2,1,0:T(8,128)(2,1)S(1)} %collective-permute-done.9.w_sib, ...), custom_call_target="tpu_custom_call" | custom-call | tf_op jit(solution)/shard_map/project/pallas_call | solution.py:275
  65.7 0.1 collective-permute-start.13
  65.8 6.0 %collective-permute-done.14.refs_0_ = bf16[512,512]{1,0:T(8,128)(2,1)S(1)} collective-permute-done((bf16[512,512]{1,0:T(8,128)(2,1)S(1)}, bf16[512,512]{1,0:T(8,128)(2,1)S(1)}, u32[]{:S(2)}, u32[]{:S(2)}) %collective-permute-start.14) | collective-permute-done | bytes 524320 | tf_op jit(solution)/shard_map/ppermute | solution.py:311
  71.8 1.3 %project.10.p_ref = f32[512,512]{1,0:T(8,128)S(1)} custom-call(s32[2]{0:T(128)S(1)} %pad_add_fusion.at_ref, bf16[512,512]{1,0:T(8,128)(2,1)S(1)} %retrieve.3.a1.a_own, bf16[512,512]{1,0:T(8,128)(2,1)S(1)} %collective-permute-done.11.a1.a_sib, bf16[512,4096]{1,0:T(8,128)(2,1)S(1)} %copy-done, bf16[3,512,512]{2,1,0:T(8,128)(2,1)S(1)} %collective-permute-done.9.w_sib, ...), custom_call_target="tpu_custom_call" | custom-call | tf_op jit(solution)/shard_map/project/pallas_call | solution.py:275
  73.1 0.8 collective-permute-done.10.refs_0_
  73.9 1.2 %project.7.p_ref = f32[512,512]{1,0:T(8,128)S(1)} custom-call(s32[2]{0:T(128)S(1)} %pad_add_fusion.at_ref, bf16[512,512]{1,0:T(8,128)(2,1)S(1)} %retrieve.2.a_own.a2, bf16[512,512]{1,0:T(8,128)(2,1)S(1)} %collective-permute-done.8.a_sib.a2, bf16[512,4096]{1,0:T(8,128)(2,1)S(1)} %copy-done, bf16[3,512,512]{2,1,0:T(8,128)(2,1)S(1)} %collective-permute-done.9.w_sib, ...), custom_call_target="tpu_custom_call" | custom-call | tf_op jit(solution)/shard_map/project/pallas_call | solution.py:275
  75.2 10.0 %collective-permute-done.16.r_ref = bf16[512,512]{1,0:T(8,128)(2,1)S(1)} collective-permute-done((bf16[512,512]{1,0:T(8,128)(2,1)S(1)}, bf16[512,512]{1,0:T(8,128)(2,1)S(1)}, u32[]{:S(2)}, u32[]{:S(2)}) %collective-permute-start.16) | collective-permute-done | bytes 524320 | tf_op jit(solution)/shard_map/ppermute | solution.py:311
  85.2 0.8 finish.2.refs_0_
  86.0 0.0 collective-permute-done.13.r_ref
  86.0 0.8 finish.3
  (3 shorter events, 0.1 us)
Async XLA Ops:
  2.4 5.0 %collective-permute-start = (bf16[528,128]{1,0:T(8,128)(2,1)S(1)}, bf16[528,128]{1,0:T(8,128)(2,1)S(1)}, u32[]{:S(2)}, u32[]{:S(2)}) collective-permute-start(bf16[528,128]{1,0:T(8,128)(2,1)S(1)} %delta.1), channel_id=1, source_target_pairs={{0,8},{8,0},{16,24},{24,16},{32,40},{40,32},{48,56},{56,48},{1,9},... | collective-permute-start | bytes 405512 | tf_op jit(solution)/shard_map/ppermute | solution.py:311
  5.0 10.6 %copy-start.1 = (f32[4]{0:T(128)S(1)}, f32[4]{0:T(128)}, u32[]{:S(2)}) copy-start(f32[4]{0:T(128)} %param.8) | copy-start | bytes 52
  7.4 17.3 %collective-permute-start.1 = (bf16[528,128]{1,0:T(8,128)(2,1)S(1)}, bf16[528,128]{1,0:T(8,128)(2,1)S(1)}, u32[]{:S(2)}, u32[]{:S(2)}) collective-permute-start(bf16[528,128]{1,0:T(8,128)(2,1)S(1)} %convert_element_type.40), channel_id=1, source_target_pairs={{0,16},{8,24},{16,0},{24,8},{32,48},{40,56},{48,32},{56,40},{1,17}... | collective-permute-start | bytes 405512 | tf_op jit(solution)/shard_map/ppermute | solution.py:311
  11.3 16.5 %collective-permute-start.2 = (bf16[528,128]{1,0:T(8,128)(2,1)S(1)}, bf16[528,128]{1,0:T(8,128)(2,1)S(1)}, u32[]{:S(2)}, u32[]{:S(2)}) collective-permute-start(bf16[528,128]{1,0:T(8,128)(2,1)S(1)} %convert_element_type.40), channel_id=1, source_target_pairs={{0,40},{8,32},{16,56},{24,48},{32,8},{40,0},{48,24},{56,16},{1,41}... | collective-permute-start | bytes 405512 | tf_op jit(solution)/shard_map/ppermute | solution.py:311
  15.6 12.2 %collective-permute-start.3 = (bf16[528,128]{1,0:T(8,128)(2,1)S(1)}, bf16[528,128]{1,0:T(8,128)(2,1)S(1)}, u32[]{:S(2)}, u32[]{:S(2)}) collective-permute-start(bf16[528,128]{1,0:T(8,128)(2,1)S(1)} %convert_element_type.40), channel_id=1, source_target_pairs={{0,48},{8,56},{16,32},{24,40},{32,16},{40,24},{48,0},{56,8},{1,49}... | collective-permute-start | bytes 405512 | tf_op jit(solution)/shard_map/ppermute | solution.py:311
  15.6 24.4 %collective-permute-start.7 = (bf16[512,512]{1,0:T(8,128)(2,1)S(1)}, bf16[512,512]{1,0:T(8,128)(2,1)S(1)}, u32[]{:S(2)}, u32[]{:S(2)}) collective-permute-start(bf16[512,512]{1,0:T(8,128)(2,1)S(1)} %get-tuple-element.62), channel_id=1, source_target_pairs={{0,1},{1,0},{2,3},{3,2},{4,5},{5,4},{6,7},{7,6},{8,9},{9,8},{10,11... | collective-permute-start | bytes 1572872 | tf_op jit(solution)/shard_map/ppermute | solution.py:311
  27.9 5.9 %collective-permute-start.4 = (bf16[528,128]{1,0:T(8,128)(2,1)S(1)}, bf16[528,128]{1,0:T(8,128)(2,1)S(1)}, u32[]{:S(2)}, u32[]{:S(2)}) collective-permute-start(bf16[528,128]{1,0:T(8,128)(2,1)S(1)} %convert_add_fusion), channel_id=1, source_target_pairs={{0,64},{64,0},{128,192},{192,128},{1,65},{65,1},{129,193},{193,129... | collective-permute-start | bytes 405512 | tf_op jit(solution)/shard_map/ppermute | solution.py:311
  29.3 7.8 %collective-permute-start.5 = (bf16[528,128]{1,0:T(8,128)(2,1)S(1)}, bf16[528,128]{1,0:T(8,128)(2,1)S(1)}, u32[]{:S(2)}, u32[]{:S(2)}) collective-permute-start(bf16[528,128]{1,0:T(8,128)(2,1)S(1)} %convert_add_fusion), channel_id=1, source_target_pairs={{0,128},{64,192},{128,0},{192,64},{1,129},{65,193},{129,1},{193,65... | collective-permute-start | bytes 405512 | tf_op jit(solution)/shard_map/ppermute | solution.py:311
  31.9 8.0 %collective-permute-start.6 = (bf16[528,128]{1,0:T(8,128)(2,1)S(1)}, bf16[528,128]{1,0:T(8,128)(2,1)S(1)}, u32[]{:S(2)}, u32[]{:S(2)}) collective-permute-start(bf16[528,128]{1,0:T(8,128)(2,1)S(1)} %convert_add_fusion), channel_id=1, source_target_pairs={{0,192},{64,128},{128,64},{192,0},{1,193},{65,129},{129,65},{193,1... | collective-permute-start | bytes 405512 | tf_op jit(solution)/shard_map/ppermute | solution.py:311
  40.0 10.2 %collective-permute-start.9 = (bf16[3,512,512]{2,1,0:T(8,128)(2,1)S(1)}, bf16[3,512,512]{2,1,0:T(8,128)(2,1)S(1)}, u32[]{:S(2)}, u32[]{:S(2)}) collective-permute-start(bf16[3,512,512]{2,1,0:T(8,128)(2,1)S(1)} %get-tuple-element.71), channel_id=1, source_target_pairs={{0,1},{1,0},{2,3},{3,2},{4,5},{5,4},{6,7},{7,6},{8,9},{9,8},{10,11... | collective-permute-start | bytes 4718600 | tf_op jit(solution)/shard_map/ppermute | solution.py:311
  41.6 2.7 %copy-start = (bf16[512,4096]{1,0:T(8,128)(2,1)S(1)}, bf16[512,4096]{1,0:T(8,128)(2,1)}, u32[]{:S(2)}) copy-start(bf16[512,4096]{1,0:T(8,128)(2,1)} %w_own.13) | copy-start | bytes 12582916
  43.7 2.0 %collective-permute-start.11 = (bf16[512,512]{1,0:T(8,128)(2,1)S(1)}, bf16[512,512]{1,0:T(8,128)(2,1)S(1)}, u32[]{:S(2)}, u32[]{:S(2)}) collective-permute-start(bf16[512,512]{1,0:T(8,128)(2,1)S(1)} %retrieve.3.a1.a_own), channel_id=1, source_target_pairs={{0,1},{1,0},{2,3},{3,2},{4,5},{5,4},{6,7},{7,6},{8,9},{9,8},{10,11... | collective-permute-start | bytes 1572872 | tf_op jit(solution)/shard_map/ppermute | solution.py:311
  43.8 2.6 %collective-permute-start.8 = (bf16[512,512]{1,0:T(8,128)(2,1)S(1)}, bf16[512,512]{1,0:T(8,128)(2,1)S(1)}, u32[]{:S(2)}, u32[]{:S(2)}) collective-permute-start(bf16[512,512]{1,0:T(8,128)(2,1)S(1)} %retrieve.2.a_own.a2), channel_id=1, source_target_pairs={{0,1},{1,0},{2,3},{3,2},{4,5},{5,4},{6,7},{7,6},{8,9},{9,8},{10,11... | collective-permute-start | bytes 1572872 | tf_op jit(solution)/shard_map/ppermute | solution.py:311
  47.1 13.5 %collective-permute-start.15 = (bf16[512,512]{1,0:T(8,128)(2,1)S(1)}, bf16[512,512]{1,0:T(8,128)(2,1)S(1)}, u32[]{:S(2)}, u32[]{:S(2)}) collective-permute-start(bf16[512,512]{1,0:T(8,128)(2,1)S(1)} %get-tuple-element.76), channel_id=1, source_target_pairs={{0,2},{2,0},{4,6},{6,4},{1,3},{3,1},{5,7},{7,5},{8,10},{10,8},{12,... | collective-permute-start | bytes 1572872 | tf_op jit(solution)/shard_map/ppermute | solution.py:311
  48.4 16.0 %collective-permute-start.12 = (bf16[512,512]{1,0:T(8,128)(2,1)S(1)}, bf16[512,512]{1,0:T(8,128)(2,1)S(1)}, u32[]{:S(2)}, u32[]{:S(2)}) collective-permute-start(bf16[512,512]{1,0:T(8,128)(2,1)S(1)} %get-tuple-element.75), channel_id=1, source_target_pairs={{0,6},{2,4},{4,2},{6,0},{1,7},{3,5},{5,3},{7,1},{8,14},{10,12},{12... | collective-permute-start | bytes 1572872 | tf_op jit(solution)/shard_map/ppermute | solution.py:311
  51.5 20.3 %collective-permute-start.14 = (bf16[512,512]{1,0:T(8,128)(2,1)S(1)}, bf16[512,512]{1,0:T(8,128)(2,1)S(1)}, u32[]{:S(2)}, u32[]{:S(2)}) collective-permute-start(bf16[512,512]{1,0:T(8,128)(2,1)S(1)} %project.9), channel_id=1, source_target_pairs={{0,2},{2,0},{4,6},{6,4},{1,3},{3,1},{5,7},{7,5},{8,10},{10,8},{12,... | collective-permute-start | bytes 1572872 | tf_op jit(solution)/shard_map/ppermute | solution.py:311
  53.3 20.6 %collective-permute-start.10 = (bf16[512,512]{1,0:T(8,128)(2,1)S(1)}, bf16[512,512]{1,0:T(8,128)(2,1)S(1)}, u32[]{:S(2)}, u32[]{:S(2)}) collective-permute-start(bf16[512,512]{1,0:T(8,128)(2,1)S(1)} %project.6), channel_id=1, source_target_pairs={{0,6},{2,4},{4,2},{6,0},{1,7},{3,5},{5,3},{7,1},{8,14},{10,12},{12... | collective-permute-start | bytes 1572872 | tf_op jit(solution)/shard_map/ppermute | solution.py:311
  61.9 23.3 %collective-permute-start.16 = (bf16[512,512]{1,0:T(8,128)(2,1)S(1)}, bf16[512,512]{1,0:T(8,128)(2,1)S(1)}, u32[]{:S(2)}, u32[]{:S(2)}) collective-permute-start(bf16[512,512]{1,0:T(8,128)(2,1)S(1)} %project.11), channel_id=1, source_target_pairs={{0,6},{2,4},{4,2},{6,0},{1,7},{3,5},{5,3},{7,1},{8,14},{10,12},{12... | collective-permute-start | bytes 1572872 | tf_op jit(solution)/shard_map/ppermute | solution.py:311
  65.7 20.3 %collective-permute-start.13 = (bf16[512,512]{1,0:T(8,128)(2,1)S(1)}, bf16[512,512]{1,0:T(8,128)(2,1)S(1)}, u32[]{:S(2)}, u32[]{:S(2)}) collective-permute-start(bf16[512,512]{1,0:T(8,128)(2,1)S(1)} %project.8), channel_id=1, source_target_pairs={{0,2},{2,0},{4,6},{6,4},{1,3},{3,1},{5,7},{7,5},{8,10},{10,8},{12,... | collective-permute-start | bytes 1572872 | tf_op jit(solution)/shard_map/ppermute | solution.py:311

commit v5 on v4

--- a/solution.py
+++ b/solution.py
@@ -339,9 +339,9 @@
         held, _ = lax.optimization_barrier(((queries, keys, values), done))
         return attention(gate, *held, 0, heads)
 
-    waiting = fold("z", z, (2, 5, 6), heads_after(total))
+    waiting = fold("z", z, (5, 2, 6), heads_after(total))
     waiting, _ = lax.optimization_barrier((waiting, total))
-    arrays, w_far = fold("y", y, (1, 2, 3), (preload(waiting), w_far))
+    arrays, w_far = fold("y", y, (2, 1, 3), (preload(waiting), w_far))
     state = before.astype(BF16)
     w_rest, state = lax.optimization_barrier((w_out[1], state))
     w_sib = swap(w_rest, "c", 1)

time: 87.1 us -> 84.1 us (0.966)
  waiting for transfers between devices: 33.7 us -> 30.1 us
    ppermute x17, waiting for transfers between devices: 33.7 us -> 30.1 us  [swap(): return lax.ppermute(array, axis, [(i, i ^ mask) for i in range(size)])]
  transfers between devices with their start and end apart: 17 -> 17, of which waited for: 10 -> 10; matrix products, arithmetic and copies ran while one was open for 0% -> 0% of each run, Pallas kernels for 27% -> 28%
where the time goes in v5:
time: 84.1 us; the launch traced here: 83.9 us
  waiting for transfers between devices  30.1 us (36%)
  starting transfers between devices  26.7 us (32%)
  Pallas kernels  26.5 us (32%)
    ppermute x17, waiting for transfers between devices, swap(): return lax.ppermute(array, axis, [(i, i ^ mask) for i in range(size)])  30.1 us
    ppermute x17, starting transfers between devices, swap(): return lax.ppermute(array, axis, [(i, i ^ mask) for i in range(size)])  26.7 us
    pallas_call x6, Pallas kernels, project(): pl.pallas_call(functools.partial(project_kernel, k), in_specs=[SMEM] + [V...  7.5 us
    pallas_call x1, Pallas kernels, attention(): pl.pallas_call(functools.partial(attention_kernel, first), grid=(count,),...  6.9 us
    pallas_call x1, Pallas kernels, delta(): pl.pallas_call(delta_kernel, grid=(rows // block,), in_specs=[spec, spec]...  2.37 us
    pallas_call x1, Pallas kernels, sibling_columns(): pl.pallas_call(sibling_kernel, in_specs=[SMEM, pl.BlockSpec(memory_space=...  2.11 us
    pallas_call x2, Pallas kernels, retrieve(): pl.pallas_call(functools.partial(retrieve_kernel, starts), in_specs=[SMEM...  2.1 us
    pallas_call x1, Pallas kernels, preload(): pl.pallas_call(preload_kernel, in_specs=[pl.BlockSpec(memory_space=pltpu....  1.87 us
  transfers between devices with their start and end apart: 17, of which 10 were waited for; matrix products, arithmetic and copies ran while one was open for 0% of the time, Pallas kernels for 28%

profile of v5, /device:TPU:1, one launch (start us, length us, event | category | flops | bytes accessed | tf_op | source)
XLA Modules:
  0.0 83.9 jit_solution(15765384000328412083)
XLA Ops:
  0.0 2.4 %delta.1 = bf16[528,128]{1,0:T(8,128)(2,1)S(1)} custom-call(bf16[1024,512]{1,0:T(8,128)(2,1)} %k_ref.2, bf16[1024,512]{1,0:T(8,128)(2,1)} %v_ref.2), custom_call_target="tpu_custom_call" | custom-call | tf_op jit(solution)/shard_map/delta/pallas_call | solution.py:70
  2.4 2.5 %collective-permute-start = (bf16[528,128]{1,0:T(8,128)(2,1)S(1)}, bf16[528,128]{1,0:T(8,128)(2,1)S(1)}, u32[]{:S(2)}, u32[]{:S(2)}) collective-permute-start(bf16[528,128]{1,0:T(8,128)(2,1)S(1)} %delta.1), channel_id=1, source_target_pairs={{0,8},{8,0},{16,24},{24,16},{32,40},{40,32},{48,56},{56,48},{1,9},... | collective-permute-start | bytes 405512 | tf_op jit(solution)/shard_map/ppermute | solution.py:311
  4.9 0.1 pad_add_fusion.at_ref
  5.0 0.0 copy-start.1
  5.0 2.1 %sibling_columns.1 = (bf16[512,512]{1,0:T(8,128)(2,1)S(1)}, bf16[3,512,512]{2,1,0:T(8,128)(2,1)S(1)}) custom-call(s32[2]{0:T(128)S(1)} %pad_add_fusion.at_ref, bf16[512,4096]{1,0:T(8,128)(2,1)} %w_own.13), custom_call_target="tpu_custom_call" | custom-call | tf_op jit(solution)/shard_map/sibling_columns/pallas_call | solution.py:206
  7.1 0.2 collective-permute-done
  7.4 7.0 %collective-permute-start.1 = (bf16[528,128]{1,0:T(8,128)(2,1)S(1)}, bf16[528,128]{1,0:T(8,128)(2,1)S(1)}, u32[]{:S(2)}, u32[]{:S(2)}) collective-permute-start(bf16[528,128]{1,0:T(8,128)(2,1)S(1)} %convert_element_type.40), channel_id=1, source_target_pairs={{0,40},{8,32},{16,56},{24,48},{32,8},{40,0},{48,24},{56,16},{1,41}... | collective-permute-start | bytes 405512 | tf_op jit(solution)/shard_map/ppermute | solution.py:311
  14.4 1.2 %collective-permute-start.2 = (bf16[528,128]{1,0:T(8,128)(2,1)S(1)}, bf16[528,128]{1,0:T(8,128)(2,1)S(1)}, u32[]{:S(2)}, u32[]{:S(2)}) collective-permute-start(bf16[528,128]{1,0:T(8,128)(2,1)S(1)} %convert_element_type.40), channel_id=1, source_target_pairs={{0,16},{8,24},{16,0},{24,8},{32,48},{40,56},{48,32},{56,40},{1,17}... | collective-permute-start | bytes 405512 | tf_op jit(solution)/shard_map/ppermute | solution.py:311
  15.6 0.0 collective-permute-start.3
  15.6 0.0 copy-done.1
  15.6 2.2 %collective-permute-start.7 = (bf16[512,512]{1,0:T(8,128)(2,1)S(1)}, bf16[512,512]{1,0:T(8,128)(2,1)S(1)}, u32[]{:S(2)}, u32[]{:S(2)}) collective-permute-start(bf16[512,512]{1,0:T(8,128)(2,1)S(1)} %get-tuple-element.62), channel_id=1, source_target_pairs={{0,1},{1,0},{2,3},{3,2},{4,5},{5,4},{6,7},{7,6},{8,9},{9,8},{10,11... | collective-permute-start | bytes 1572872 | tf_op jit(solution)/shard_map/ppermute | solution.py:311
  17.8 6.9 %attention.1 = (f32[4,1024,128]{2,1,0:T(8,128)}, bf16[4,1024,128]{2,1,0:T(8,128)(2,1)}) custom-call(f32[4]{0:T(128)S(1)} %add_divide_fusion.g_ref, bf16[1024,512]{1,0:T(8,128)(2,1)} %q_ref, bf16[1024,512]{1,0:T(8,128)(2,1)} %k_ref.2, bf16[1024,512]{1,0:T(8,128)(2,1)} %v_ref.2), custom_call_target="tpu_custom_call" | custom-call | tf_op jit(solution)/shard_map/attention/pallas_call | solution.py:123
  24.7 0.0 collective-permute-done.1
  24.7 2.0 %collective-permute-done.2 = bf16[528,128]{1,0:T(8,128)(2,1)S(1)} collective-permute-done((bf16[528,128]{1,0:T(8,128)(2,1)S(1)}, bf16[528,128]{1,0:T(8,128)(2,1)S(1)}, u32[]{:S(2)}, u32[]{:S(2)}) %collective-permute-start.2) | collective-permute-done | bytes 135200 | tf_op jit(solution)/shard_map/ppermute | solution.py:311
  26.7 0.0 collective-permute-done.3
  26.7 0.1 convert_add_fusion
  26.8 0.1 fusion.2
  26.9 3.0 %collective-permute-start.4 = (bf16[528,128]{1,0:T(8,128)(2,1)S(1)}, bf16[528,128]{1,0:T(8,128)(2,1)S(1)}, u32[]{:S(2)}, u32[]{:S(2)}) collective-permute-start(bf16[528,128]{1,0:T(8,128)(2,1)S(1)} %convert_add_fusion), channel_id=1, source_target_pairs={{0,128},{64,192},{128,0},{192,64},{1,129},{65,193},{129,1},{193,65... | collective-permute-start | bytes 405512 | tf_op jit(solution)/shard_map/ppermute | solution.py:311
  29.9 0.4 collective-permute-start.5
  30.3 0.4 collective-permute-start.6
  30.7 1.9 %preload.1 = (f32[4,1024,128]{2,1,0:T(8,128)S(1)}, bf16[4,1024,128]{2,1,0:T(8,128)(2,1)S(1)}) custom-call(f32[4,1024,128]{2,1,0:T(8,128)} %get-tuple-element.58.refs_0_, bf16[4,1024,128]{2,1,0:T(8,128)(2,1)} %get-tuple-element.59.refs_1_), custom_call_target="tpu_custom_call" | custom-call | tf_op jit(solution)/shard_map/preload/pallas_call | solution.py:147
  32.6 0.0 collective-permute-done.4
  32.6 2.9 %collective-permute-done.5 = bf16[528,128]{1,0:T(8,128)(2,1)S(1)} collective-permute-done((bf16[528,128]{1,0:T(8,128)(2,1)S(1)}, bf16[528,128]{1,0:T(8,128)(2,1)S(1)}, u32[]{:S(2)}, u32[]{:S(2)}) %collective-permute-start.5) | collective-permute-done | bytes 135200 | tf_op jit(solution)/shard_map/ppermute | solution.py:311
  35.5 0.6 collective-permute-done.6
  36.1 0.0 collective-permute-done.7.w_sib
  36.1 0.1 select_add_fusion.refs_2_
  36.2 2.4 %collective-permute-start.9 = (bf16[3,512,512]{2,1,0:T(8,128)(2,1)S(1)}, bf16[3,512,512]{2,1,0:T(8,128)(2,1)S(1)}, u32[]{:S(2)}, u32[]{:S(2)}) collective-permute-start(bf16[3,512,512]{2,1,0:T(8,128)(2,1)S(1)} %get-tuple-element.71), channel_id=1, source_target_pairs={{0,1},{1,0},{2,3},{3,2},{4,5},{5,4},{6,7},{7,6},{8,9},{9,8},{10,11... | collective-permute-start | bytes 4718600 | tf_op jit(solution)/shard_map/ppermute | solution.py:311
  38.6 0.0 copy-start
  38.6 1.0 %retrieve.3.a1.a_own = bf16[512,512]{1,0:T(8,128)(2,1)S(1)} custom-call(f32[4]{0:T(128)S(1)} %add_divide_fusion.g_ref, f32[4,1024,128]{2,1,0:T(8,128)S(1)} %get-tuple-element.63.refs_0_, bf16[4,1024,128]{2,1,0:T(8,128)(2,1)S(1)} %get-tuple-element.64.refs_1_, bf16[528,128]{1,0:T(8,128)(2,1)S(1)} %select_add_fusion.refs_2_), custom_call_target="tpu_custom_call" | custom-call | tf_op jit(solution)/shard_map/retrieve/pallas_call | solution.py:180
  39.6 1.0 %retrieve.2.a_own.a2 = bf16[512,512]{1,0:T(8,128)(2,1)S(1)} custom-call(f32[4]{0:T(128)S(1)} %add_divide_fusion.g_ref, f32[4,1024,128]{2,1,0:T(8,128)S(1)} %get-tuple-element.63.refs_0_, bf16[4,1024,128]{2,1,0:T(8,128)(2,1)S(1)} %get-tuple-element.64.refs_1_, bf16[528,128]{1,0:T(8,128)(2,1)S(1)} %select_add_fusion.refs_2_), custom_call_target="tpu_custom_call" | custom-call | tf_op jit(solution)/shard_map/retrieve/pallas_call | solution.py:180
  40.7 0.1 collective-permute-start.11
  40.8 0.5 collective-permute-start.8
  41.3 0.0 copy-done
  41.3 1.3 %project_far_own.1 = (f32[512,512]{1,0:T(8,128)S(1)}, f32[512,512]{1,0:T(8,128)S(1)}) custom-call(s32[2]{0:T(128)S(1)} %pad_add_fusion.at_ref, bf16[512,512]{1,0:T(8,128)(2,1)S(1)} %retrieve.3.a1.a_own, bf16[512,512]{1,0:T(8,128)(2,1)S(1)} %retrieve.2.a_own.a2, bf16[512,4096]{1,0:T(8,128)(2,1)S(1)} %copy-done), custom_call_target="tpu_custom_call" | custom-call | tf_op jit(solution)/shard_map/project_far_own/pallas_call | solution.py:241
  42.6 0.1 collective-permute-done.11.a1.a_sib
  42.7 0.7 collective-permute-done.8.a_sib.a2
  43.5 0.7 project_far.1
  44.2 1.3 %collective-permute-start.15 = (bf16[512,512]{1,0:T(8,128)(2,1)S(1)}, bf16[512,512]{1,0:T(8,128)(2,1)S(1)}, u32[]{:S(2)}, u32[]{:S(2)}) collective-permute-start(bf16[512,512]{1,0:T(8,128)(2,1)S(1)} %get-tuple-element.76), channel_id=1, source_target_pairs={{0,2},{2,0},{4,6},{6,4},{1,3},{3,1},{5,7},{7,5},{8,10},{10,8},{12,... | collective-permute-start | bytes 1572872 | tf_op jit(solution)/shard_map/ppermute | solution.py:311
  45.5 1.8 %collective-permute-start.12 = (bf16[512,512]{1,0:T(8,128)(2,1)S(1)}, bf16[512,512]{1,0:T(8,128)(2,1)S(1)}, u32[]{:S(2)}, u32[]{:S(2)}) collective-permute-start(bf16[512,512]{1,0:T(8,128)(2,1)S(1)} %get-tuple-element.75), channel_id=1, source_target_pairs={{0,6},{2,4},{4,2},{6,0},{1,7},{3,5},{5,3},{7,1},{8,14},{10,12},{12... | collective-permute-start | bytes 1572872 | tf_op jit(solution)/shard_map/ppermute | solution.py:311
  47.3 0.0 collective-permute-done.9.w_sib
  47.3 1.2 %project.9 = bf16[512,512]{1,0:T(8,128)(2,1)S(1)} custom-call(s32[2]{0:T(128)S(1)} %pad_add_fusion.at_ref, bf16[512,512]{1,0:T(8,128)(2,1)S(1)} %retrieve.3.a1.a_own, bf16[512,512]{1,0:T(8,128)(2,1)S(1)} %collective-permute-done.11.a1.a_sib, bf16[512,4096]{1,0:T(8,128)(2,1)S(1)} %copy-done, bf16[3,512,512]{2,1,0:T(8,128)(2,1)S(1)} %collective-permute-done.9.w_sib), custom_call_target="tpu_custom_call" | custom-call | tf_op jit(solution)/shard_map/project/pallas_call | solution.py:275
  48.6 0.6 collective-permute-start.14
  49.1 1.2 %project.6 = bf16[512,512]{1,0:T(8,128)(2,1)S(1)} custom-call(s32[2]{0:T(128)S(1)} %pad_add_fusion.at_ref, bf16[512,512]{1,0:T(8,128)(2,1)S(1)} %retrieve.2.a_own.a2, bf16[512,512]{1,0:T(8,128)(2,1)S(1)} %collective-permute-done.8.a_sib.a2, bf16[512,4096]{1,0:T(8,128)(2,1)S(1)} %copy-done, bf16[3,512,512]{2,1,0:T(8,128)(2,1)S(1)} %collective-permute-done.9.w_sib), custom_call_target="tpu_custom_call" | custom-call | tf_op jit(solution)/shard_map/project/pallas_call | solution.py:275
  50.4 0.7 collective-permute-start.10
  51.1 6.6 %collective-permute-done.15.refs_0_ = bf16[512,512]{1,0:T(8,128)(2,1)S(1)} collective-permute-done((bf16[512,512]{1,0:T(8,128)(2,1)S(1)}, bf16[512,512]{1,0:T(8,128)(2,1)S(1)}, u32[]{:S(2)}, u32[]{:S(2)}) %collective-permute-start.15) | collective-permute-done | bytes 524320 | tf_op jit(solution)/shard_map/ppermute | solution.py:311
  57.6 1.3 %project.11 = bf16[512,512]{1,0:T(8,128)(2,1)S(1)} custom-call(s32[2]{0:T(128)S(1)} %pad_add_fusion.at_ref, bf16[512,512]{1,0:T(8,128)(2,1)S(1)} %retrieve.3.a1.a_own, bf16[512,512]{1,0:T(8,128)(2,1)S(1)} %collective-permute-done.11.a1.a_sib, bf16[512,4096]{1,0:T(8,128)(2,1)S(1)} %copy-done, bf16[3,512,512]{2,1,0:T(8,128)(2,1)S(1)} %collective-permute-done.9.w_sib, ...), custom_call_target="tpu_custom_call" | custom-call | tf_op jit(solution)/shard_map/project/pallas_call | solution.py:275
  58.9 2.6 %collective-permute-start.16 = (bf16[512,512]{1,0:T(8,128)(2,1)S(1)}, bf16[512,512]{1,0:T(8,128)(2,1)S(1)}, u32[]{:S(2)}, u32[]{:S(2)}) collective-permute-start(bf16[512,512]{1,0:T(8,128)(2,1)S(1)} %project.11), channel_id=1, source_target_pairs={{0,6},{2,4},{4,2},{6,0},{1,7},{3,5},{5,3},{7,1},{8,14},{10,12},{12... | collective-permute-start | bytes 1572872 | tf_op jit(solution)/shard_map/ppermute | solution.py:311
  61.5 0.0 collective-permute-done.12.refs_0_
  61.5 1.2 %project.8 = bf16[512,512]{1,0:T(8,128)(2,1)S(1)} custom-call(s32[2]{0:T(128)S(1)} %pad_add_fusion.at_ref, bf16[512,512]{1,0:T(8,128)(2,1)S(1)} %retrieve.2.a_own.a2, bf16[512,512]{1,0:T(8,128)(2,1)S(1)} %collective-permute-done.8.a_sib.a2, bf16[512,4096]{1,0:T(8,128)(2,1)S(1)} %copy-done, bf16[3,512,512]{2,1,0:T(8,128)(2,1)S(1)} %collective-permute-done.9.w_sib, ...), custom_call_target="tpu_custom_call" | custom-call | tf_op jit(solution)/shard_map/project/pallas_call | solution.py:275
  62.7 0.1 collective-permute-start.13
  62.8 6.0 %collective-permute-done.14.refs_0_ = bf16[512,512]{1,0:T(8,128)(2,1)S(1)} collective-permute-done((bf16[512,512]{1,0:T(8,128)(2,1)S(1)}, bf16[512,512]{1,0:T(8,128)(2,1)S(1)}, u32[]{:S(2)}, u32[]{:S(2)}) %collective-permute-start.14) | collective-permute-done | bytes 524320 | tf_op jit(solution)/shard_map/ppermute | solution.py:311
  68.9 1.3 %project.10.p_ref = f32[512,512]{1,0:T(8,128)S(1)} custom-call(s32[2]{0:T(128)S(1)} %pad_add_fusion.at_ref, bf16[512,512]{1,0:T(8,128)(2,1)S(1)} %retrieve.3.a1.a_own, bf16[512,512]{1,0:T(8,128)(2,1)S(1)} %collective-permute-done.11.a1.a_sib, bf16[512,4096]{1,0:T(8,128)(2,1)S(1)} %copy-done, bf16[3,512,512]{2,1,0:T(8,128)(2,1)S(1)} %collective-permute-done.9.w_sib, ...), custom_call_target="tpu_custom_call" | custom-call | tf_op jit(solution)/shard_map/project/pallas_call | solution.py:275
  70.1 0.8 collective-permute-done.10.refs_0_
  71.0 1.2 %project.7.p_ref = f32[512,512]{1,0:T(8,128)S(1)} custom-call(s32[2]{0:T(128)S(1)} %pad_add_fusion.at_ref, bf16[512,512]{1,0:T(8,128)(2,1)S(1)} %retrieve.2.a_own.a2, bf16[512,512]{1,0:T(8,128)(2,1)S(1)} %collective-permute-done.8.a_sib.a2, bf16[512,4096]{1,0:T(8,128)(2,1)S(1)} %copy-done, bf16[3,512,512]{2,1,0:T(8,128)(2,1)S(1)} %collective-permute-done.9.w_sib, ...), custom_call_target="tpu_custom_call" | custom-call | tf_op jit(solution)/shard_map/project/pallas_call | solution.py:275
  72.2 10.0 %collective-permute-done.16.r_ref = bf16[512,512]{1,0:T(8,128)(2,1)S(1)} collective-permute-done((bf16[512,512]{1,0:T(8,128)(2,1)S(1)}, bf16[512,512]{1,0:T(8,128)(2,1)S(1)}, u32[]{:S(2)}, u32[]{:S(2)}) %collective-permute-start.16) | collective-permute-done | bytes 524320 | tf_op jit(solution)/shard_map/ppermute | solution.py:311
  82.2 0.8 finish.2.refs_0_
  83.0 0.0 collective-permute-done.13.r_ref
  83.1 0.8 %finish.3 = bf16[1024,512]{1,0:T(8,128)(2,1)} custom-call(f32[512,512]{1,0:T(8,128)S(1)} %project.7.p_ref, bf16[512,512]{1,0:T(8,128)(2,1)S(1)} %collective-permute-done.13.r_ref, bf16[1024,512]{1,0:T(8,128)(2,1)} %finish.2.refs_0_), custom_call_target="tpu_custom_call", output_to_operand_aliasing={{}: (2, {})} | custom-call | tf_op jit(solution)/shard_map/finish/pallas_call | solution.py:297
  (3 shorter events, 0.1 us)
Async XLA Ops:
  2.4 5.0 %collective-permute-start = (bf16[528,128]{1,0:T(8,128)(2,1)S(1)}, bf16[528,128]{1,0:T(8,128)(2,1)S(1)}, u32[]{:S(2)}, u32[]{:S(2)}) collective-permute-start(bf16[528,128]{1,0:T(8,128)(2,1)S(1)} %delta.1), channel_id=1, source_target_pairs={{0,8},{8,0},{16,24},{24,16},{32,40},{40,32},{48,56},{56,48},{1,9},... | collective-permute-start | bytes 405512 | tf_op jit(solution)/shard_map/ppermute | solution.py:311
  5.0 10.6 %copy-start.1 = (f32[4]{0:T(128)S(1)}, f32[4]{0:T(128)}, u32[]{:S(2)}) copy-start(f32[4]{0:T(128)} %param.8) | copy-start | bytes 52
  7.4 17.3 %collective-permute-start.1 = (bf16[528,128]{1,0:T(8,128)(2,1)S(1)}, bf16[528,128]{1,0:T(8,128)(2,1)S(1)}, u32[]{:S(2)}, u32[]{:S(2)}) collective-permute-start(bf16[528,128]{1,0:T(8,128)(2,1)S(1)} %convert_element_type.40), channel_id=1, source_target_pairs={{0,40},{8,32},{16,56},{24,48},{32,8},{40,0},{48,24},{56,16},{1,41}... | collective-permute-start | bytes 405512 | tf_op jit(solution)/shard_map/ppermute | solution.py:311
  14.4 12.4 %collective-permute-start.2 = (bf16[528,128]{1,0:T(8,128)(2,1)S(1)}, bf16[528,128]{1,0:T(8,128)(2,1)S(1)}, u32[]{:S(2)}, u32[]{:S(2)}) collective-permute-start(bf16[528,128]{1,0:T(8,128)(2,1)S(1)} %convert_element_type.40), channel_id=1, source_target_pairs={{0,16},{8,24},{16,0},{24,8},{32,48},{40,56},{48,32},{56,40},{1,17}... | collective-permute-start | bytes 405512 | tf_op jit(solution)/shard_map/ppermute | solution.py:311
  15.6 11.2 %collective-permute-start.3 = (bf16[528,128]{1,0:T(8,128)(2,1)S(1)}, bf16[528,128]{1,0:T(8,128)(2,1)S(1)}, u32[]{:S(2)}, u32[]{:S(2)}) collective-permute-start(bf16[528,128]{1,0:T(8,128)(2,1)S(1)} %convert_element_type.40), channel_id=1, source_target_pairs={{0,48},{8,56},{16,32},{24,40},{32,16},{40,24},{48,0},{56,8},{1,49}... | collective-permute-start | bytes 405512 | tf_op jit(solution)/shard_map/ppermute | solution.py:311
  15.6 20.6 %collective-permute-start.7 = (bf16[512,512]{1,0:T(8,128)(2,1)S(1)}, bf16[512,512]{1,0:T(8,128)(2,1)S(1)}, u32[]{:S(2)}, u32[]{:S(2)}) collective-permute-start(bf16[512,512]{1,0:T(8,128)(2,1)S(1)} %get-tuple-element.62), channel_id=1, source_target_pairs={{0,1},{1,0},{2,3},{3,2},{4,5},{5,4},{6,7},{7,6},{8,9},{9,8},{10,11... | collective-permute-start | bytes 1572872 | tf_op jit(solution)/shard_map/ppermute | solution.py:311
  26.9 5.7 %collective-permute-start.4 = (bf16[528,128]{1,0:T(8,128)(2,1)S(1)}, bf16[528,128]{1,0:T(8,128)(2,1)S(1)}, u32[]{:S(2)}, u32[]{:S(2)}) collective-permute-start(bf16[528,128]{1,0:T(8,128)(2,1)S(1)} %convert_add_fusion), channel_id=1, source_target_pairs={{0,128},{64,192},{128,0},{192,64},{1,129},{65,193},{129,1},{193,65... | collective-permute-start | bytes 405512 | tf_op jit(solution)/shard_map/ppermute | solution.py:311
  29.9 5.6 %collective-permute-start.5 = (bf16[528,128]{1,0:T(8,128)(2,1)S(1)}, bf16[528,128]{1,0:T(8,128)(2,1)S(1)}, u32[]{:S(2)}, u32[]{:S(2)}) collective-permute-start(bf16[528,128]{1,0:T(8,128)(2,1)S(1)} %convert_add_fusion), channel_id=1, source_target_pairs={{0,64},{64,0},{128,192},{192,128},{1,65},{65,1},{129,193},{193,129... | collective-permute-start | bytes 405512 | tf_op jit(solution)/shard_map/ppermute | solution.py:311
  30.3 5.8 %collective-permute-start.6 = (bf16[528,128]{1,0:T(8,128)(2,1)S(1)}, bf16[528,128]{1,0:T(8,128)(2,1)S(1)}, u32[]{:S(2)}, u32[]{:S(2)}) collective-permute-start(bf16[528,128]{1,0:T(8,128)(2,1)S(1)} %convert_add_fusion), channel_id=1, source_target_pairs={{0,192},{64,128},{128,64},{192,0},{1,193},{65,129},{129,65},{193,1... | collective-permute-start | bytes 405512 | tf_op jit(solution)/shard_map/ppermute | solution.py:311
  36.2 11.1 %collective-permute-start.9 = (bf16[3,512,512]{2,1,0:T(8,128)(2,1)S(1)}, bf16[3,512,512]{2,1,0:T(8,128)(2,1)S(1)}, u32[]{:S(2)}, u32[]{:S(2)}) collective-permute-start(bf16[3,512,512]{2,1,0:T(8,128)(2,1)S(1)} %get-tuple-element.71), channel_id=1, source_target_pairs={{0,1},{1,0},{2,3},{3,2},{4,5},{5,4},{6,7},{7,6},{8,9},{9,8},{10,11... | collective-permute-start | bytes 4718600 | tf_op jit(solution)/shard_map/ppermute | solution.py:311
  38.6 2.7 %copy-start = (bf16[512,4096]{1,0:T(8,128)(2,1)S(1)}, bf16[512,4096]{1,0:T(8,128)(2,1)}, u32[]{:S(2)}) copy-start(bf16[512,4096]{1,0:T(8,128)(2,1)} %w_own.13) | copy-start | bytes 12582916
  40.7 2.0 %collective-permute-start.11 = (bf16[512,512]{1,0:T(8,128)(2,1)S(1)}, bf16[512,512]{1,0:T(8,128)(2,1)S(1)}, u32[]{:S(2)}, u32[]{:S(2)}) collective-permute-start(bf16[512,512]{1,0:T(8,128)(2,1)S(1)} %retrieve.3.a1.a_own), channel_id=1, source_target_pairs={{0,1},{1,0},{2,3},{3,2},{4,5},{5,4},{6,7},{7,6},{8,9},{9,8},{10,11... | collective-permute-start | bytes 1572872 | tf_op jit(solution)/shard_map/ppermute | solution.py:311
  40.8 2.6 %collective-permute-start.8 = (bf16[512,512]{1,0:T(8,128)(2,1)S(1)}, bf16[512,512]{1,0:T(8,128)(2,1)S(1)}, u32[]{:S(2)}, u32[]{:S(2)}) collective-permute-start(bf16[512,512]{1,0:T(8,128)(2,1)S(1)} %retrieve.2.a_own.a2), channel_id=1, source_target_pairs={{0,1},{1,0},{2,3},{3,2},{4,5},{5,4},{6,7},{7,6},{8,9},{9,8},{10,11... | collective-permute-start | bytes 1572872 | tf_op jit(solution)/shard_map/ppermute | solution.py:311
  44.2 13.5 %collective-permute-start.15 = (bf16[512,512]{1,0:T(8,128)(2,1)S(1)}, bf16[512,512]{1,0:T(8,128)(2,1)S(1)}, u32[]{:S(2)}, u32[]{:S(2)}) collective-permute-start(bf16[512,512]{1,0:T(8,128)(2,1)S(1)} %get-tuple-element.76), channel_id=1, source_target_pairs={{0,2},{2,0},{4,6},{6,4},{1,3},{3,1},{5,7},{7,5},{8,10},{10,8},{12,... | collective-permute-start | bytes 1572872 | tf_op jit(solution)/shard_map/ppermute | solution.py:311
  45.5 16.0 %collective-permute-start.12 = (bf16[512,512]{1,0:T(8,128)(2,1)S(1)}, bf16[512,512]{1,0:T(8,128)(2,1)S(1)}, u32[]{:S(2)}, u32[]{:S(2)}) collective-permute-start(bf16[512,512]{1,0:T(8,128)(2,1)S(1)} %get-tuple-element.75), channel_id=1, source_target_pairs={{0,6},{2,4},{4,2},{6,0},{1,7},{3,5},{5,3},{7,1},{8,14},{10,12},{12... | collective-permute-start | bytes 1572872 | tf_op jit(solution)/shard_map/ppermute | solution.py:311
  48.6 20.3 %collective-permute-start.14 = (bf16[512,512]{1,0:T(8,128)(2,1)S(1)}, bf16[512,512]{1,0:T(8,128)(2,1)S(1)}, u32[]{:S(2)}, u32[]{:S(2)}) collective-permute-start(bf16[512,512]{1,0:T(8,128)(2,1)S(1)} %project.9), channel_id=1, source_target_pairs={{0,2},{2,0},{4,6},{6,4},{1,3},{3,1},{5,7},{7,5},{8,10},{10,8},{12,... | collective-permute-start | bytes 1572872 | tf_op jit(solution)/shard_map/ppermute | solution.py:311
  50.4 20.6 %collective-permute-start.10 = (bf16[512,512]{1,0:T(8,128)(2,1)S(1)}, bf16[512,512]{1,0:T(8,128)(2,1)S(1)}, u32[]{:S(2)}, u32[]{:S(2)}) collective-permute-start(bf16[512,512]{1,0:T(8,128)(2,1)S(1)} %project.6), channel_id=1, source_target_pairs={{0,6},{2,4},{4,2},{6,0},{1,7},{3,5},{5,3},{7,1},{8,14},{10,12},{12... | collective-permute-start | bytes 1572872 | tf_op jit(solution)/shard_map/ppermute | solution.py:311
  58.9 23.3 %collective-permute-start.16 = (bf16[512,512]{1,0:T(8,128)(2,1)S(1)}, bf16[512,512]{1,0:T(8,128)(2,1)S(1)}, u32[]{:S(2)}, u32[]{:S(2)}) collective-permute-start(bf16[512,512]{1,0:T(8,128)(2,1)S(1)} %project.11), channel_id=1, source_target_pairs={{0,6},{2,4},{4,2},{6,0},{1,7},{3,5},{5,3},{7,1},{8,14},{10,12},{12... | collective-permute-start | bytes 1572872 | tf_op jit(solution)/shard_map/ppermute | solution.py:311
  62.7 20.3 %collective-permute-start.13 = (bf16[512,512]{1,0:T(8,128)(2,1)S(1)}, bf16[512,512]{1,0:T(8,128)(2,1)S(1)}, u32[]{:S(2)}, u32[]{:S(2)}) collective-permute-start(bf16[512,512]{1,0:T(8,128)(2,1)S(1)} %project.8), channel_id=1, source_target_pairs={{0,2},{2,0},{4,6},{6,4},{1,3},{3,1},{5,7},{7,5},{8,10},{10,8},{12,... | collective-permute-start | bytes 1572872 | tf_op jit(solution)/shard_map/ppermute | solution.py:311

commit v6 on v5

--- a/solution.py
+++ b/solution.py
@@ -155,33 +155,34 @@
     )(*[far_memory(a) for a in arrays])
 
 
-def retrieve_kernel(starts, g_ref, *refs):
-    *groups, s_ref, o_ref = refs
+def retrieve_kernel(g_ref, *refs):
+    *groups, s_ref, o1, o2 = refs
+    rows = o1.shape[0]
     base = s_ref.shape[0] - PAD
-    block = o_ref.shape[0] // len(starts)
-    h = 0
-    for group in range(0, len(groups), 2):
-        local, feat = groups[group], groups[group + 1]
-        for at in range(local.shape[0]):
-            for i, lo in enumerate(starts):
-                f = feat[at, lo : lo + block, :]
+    for side, o_ref in enumerate((o1, o2)):
+        h = 0
+        part = slice(side * rows, (side + 1) * rows)
+        for group in range(0, len(groups), 2):
+            local, feat = groups[group], groups[group + 1]
+            for at in range(local.shape[0]):
+                f = feat[at, part, :]
                 numer = lax.dot_general(
                     f, s_ref[h * HD : (h + 1) * HD, :], NT, preferred_element_type=F32
                 )
                 denom = lax.dot_general(f, s_ref[base:, :], NT, preferred_element_type=F32)
                 scale = g_ref[h] / jnp.maximum(denom[:, h : h + 1], 1.0)
-                mixed = numer * scale + local[at, lo : lo + block, :]
-                o_ref[i * block : (i + 1) * block, h * HD : (h + 1) * HD] = mixed.astype(BF16)
-            h += 1
-
-
-def retrieve(gate, arrays, state, starts, rows):
+                mixed = numer * scale + local[at, part, :]
+                o_ref[:, h * HD : (h + 1) * HD] = mixed.astype(BF16)
+                h += 1
+
+
+def retrieve(gate, arrays, state, rows):
     cols = state.shape[0] - PAD
     return pl.pallas_call(
-        functools.partial(retrieve_kernel, starts),
+        retrieve_kernel,
         in_specs=[SMEM] + [VMEM] * (len(arrays) + 1),
-        out_specs=VMEM,
-        out_shape=pltpu.VMEM((rows, cols), BF16),
+        out_specs=[VMEM, VMEM],
+        out_shape=[pltpu.VMEM((rows // 2, cols), BF16)] * 2,
         compiler_params=PARAMS,
         name="retrieve",
     )(gate, *[near_core(a) for a in arrays], near_core(state))
@@ -282,28 +283,32 @@
     )(at, *[near_core(a) for a in (*half, w_own, w_sib, *adds)])
 
 
-def finish_kernel(p_ref, r_ref, *refs):
-    o_ref = refs[-1]
-    block = o_ref.shape[0]
-    part = pl.ds(pl.multiple_of(pl.program_id(0) * block, block), block)
-    o_ref[...] = (p_ref[part, :] + r_ref[part, :].astype(F32)).astype(o_ref.dtype)
-
-
-def finish(total, received, side, before):
-    rows, width = total.shape
-    block = 256
-    steps = rows // block
-    rest = [] if before is None else [before]
+def finish_kernel(p1, p2, r1, r2, o_ref, held, sems):
+    rows = p1.shape[0]
+    block = held.shape[0] // sems.shape[0]
+    copies = []
+    for i in range(sems.shape[0]):
+        p, r = (p1, r1) if i * block < rows else (p2, r2)
+        part = slice(i * block % rows, i * block % rows + block)
+        out = slice(i * block, (i + 1) * block)
+        held[out, :] = (p[part, :] + r[part, :].astype(F32)).astype(held.dtype)
+        copies.append(pltpu.make_async_copy(held.at[out], o_ref.at[out], sems.at[i]))
+        copies[-1].start()
+    for copy in copies:
+        copy.wait()
+
+
+def finish(p1, p2, r1, r2):
+    rows, width = p1.shape
     return pl.pallas_call(
         finish_kernel,
-        grid=(steps,),
-        in_specs=[VMEM, VMEM] + [pl.BlockSpec(memory_space=pl.ANY)] * len(rest),
-        out_specs=pl.BlockSpec((block, width), lambda i: (side * steps + i, 0)),
+        in_specs=[VMEM] * 4,
+        out_specs=pl.BlockSpec(memory_space=pltpu.HBM),
         out_shape=jax.ShapeDtypeStruct((2 * rows, width), BF16),
-        input_output_aliases={2: 0} if rest else {},
+        scratch_shapes=[pltpu.VMEM((2 * rows, width), BF16), pltpu.SemaphoreType.DMA((4,))],
         compiler_params=PARAMS,
         name="finish",
-    )(near_core(total), near_core(received), *rest)
+    )(*[near_core(a) for a in (p1, p2, r1, r2)])
 
 
 def swap(array, axis, mask):
@@ -339,18 +344,15 @@
         held, _ = lax.optimization_barrier(((queries, keys, values), done))
         return attention(gate, *held, 0, heads)
 
-    waiting = fold("z", z, (5, 2, 6), heads_after(total))
+    waiting = fold("z", z, (5, 6, 2), heads_after(total))
     waiting, _ = lax.optimization_barrier((waiting, total))
     arrays, w_far = fold("y", y, (2, 1, 3), (preload(waiting), w_far))
     state = before.astype(BF16)
     w_rest, state = lax.optimization_barrier((w_out[1], state))
     w_sib = swap(w_rest, "c", 1)
 
-    half = queries.shape[0] // 2
-    halves = []
-    for start in (0, half):
-        a_own = retrieve(gate, arrays, state, (start,), half)
-        halves.append((a_own, swap(a_own, "c", 1)))
+    attended = retrieve(gate, arrays, state, queries.shape[0])
+    halves = [(a_own, swap(a_own, "c", 1)) for a_own in attended]
 
     def mm(side, k, adds, dtype):
         return project(at, halves[side], w_own, w_sib, k, adds, dtype)
@@ -358,11 +360,12 @@
     hops = ((1, 3), (3, 1))
     far = project_far(at, halves, w_own, w_far)
     far = [swap(far[i], "x", hops[i][0]) for i in range(2)]
-    near = [swap(mm(i, hops[i][0], (), BF16), "x", hops[i][0]) for i in range(2)]
+    near = [mm(i, hops[i][0], (), BF16) for i in range(2)]
+    far = [lax.optimization_barrier((far[i], near))[0] for i in range(2)]
+    near = [swap(near[i], "x", hops[i][0]) for i in range(2)]
     passed = [swap(mm(i, hops[i][1], (far[i],), BF16), "x", hops[i][1]) for i in range(2)]
     mine = [mm(i, 0, (near[i],), F32) for i in range(2)]
-    out = finish(mine[0], passed[0], 0, None)
-    return finish(mine[1], passed[1], 1, out)
+    return finish(*mine, *passed)
 
 
 def solution(mesh):

time: 84.1 us -> 83.1 us (0.988)
  Pallas kernels: 26.5 us -> 25.3 us
    pallas_call x4 -> x2, Pallas kernels: 3.78 us -> 2.4 us  [the longest x1 1.35 us: retrieve(): pl.pallas_call(retrieve_kernel, in_specs=[SMEM] + [VMEM] * (len(arrays) +...]
  transfers between devices with their start and end apart: 17 -> 17, of which waited for: 10 -> 10; matrix products, arithmetic and copies ran while one was open for 0% -> 0% of each run, Pallas kernels for 28% -> 26%
where the time goes in v6:
time: 83.1 us; the launch traced here: 82.9 us
  waiting for transfers between devices  30.2 us (36%)
  starting transfers between devices  26.7 us (32%)
  Pallas kernels  25.3 us (30%)
    ppermute x17, waiting for transfers between devices, swap(): return lax.ppermute(array, axis, [(i, i ^ mask) for i in range(size)])  30.2 us
    ppermute x17, starting transfers between devices, swap(): return lax.ppermute(array, axis, [(i, i ^ mask) for i in range(size)])  26.7 us
    pallas_call x6, Pallas kernels, project(): pl.pallas_call(functools.partial(project_kernel, k), in_specs=[SMEM] + [V...  7.51 us
    pallas_call x1, Pallas kernels, attention(): pl.pallas_call(functools.partial(attention_kernel, first), grid=(count,),...  6.9 us
    pallas_call x1, Pallas kernels, delta(): pl.pallas_call(delta_kernel, grid=(rows // block,), in_specs=[spec, spec]...  2.37 us
    pallas_call x1, Pallas kernels, sibling_columns(): pl.pallas_call(sibling_kernel, in_specs=[SMEM, pl.BlockSpec(memory_space=...  2.11 us
    pallas_call x1, Pallas kernels, preload(): pl.pallas_call(preload_kernel, in_specs=[pl.BlockSpec(memory_space=pltpu....  2.02 us
  transfers between devices with their start and end apart: 17, of which 10 were waited for; matrix products, arithmetic and copies ran while one was open for 0% of the time, Pallas kernels for 26%

profile of v6, /device:TPU:1, one launch (start us, length us, event | category | flops | bytes accessed | tf_op | source)
XLA Modules:
  0.0 82.9 jit_solution(7897948521726531755)
XLA Ops:
  0.0 2.4 %delta.1 = bf16[528,128]{1,0:T(8,128)(2,1)S(1)} custom-call(bf16[1024,512]{1,0:T(8,128)(2,1)} %k_ref.2, bf16[1024,512]{1,0:T(8,128)(2,1)} %v_ref.2), custom_call_target="tpu_custom_call" | custom-call | tf_op jit(solution)/shard_map/delta/pallas_call | solution.py:70
  2.4 2.5 %collective-permute-start = (bf16[528,128]{1,0:T(8,128)(2,1)S(1)}, bf16[528,128]{1,0:T(8,128)(2,1)S(1)}, u32[]{:S(2)}, u32[]{:S(2)}) collective-permute-start(bf16[528,128]{1,0:T(8,128)(2,1)S(1)} %delta.1), channel_id=1, source_target_pairs={{0,8},{8,0},{16,24},{24,16},{32,40},{40,32},{48,56},{56,48},{1,9},... | collective-permute-start | bytes 405512 | tf_op jit(solution)/shard_map/ppermute | solution.py:316
  4.9 0.1 pad_add_fusion.at_ref
  5.0 0.0 copy-start.1
  5.0 2.1 %sibling_columns.1 = (bf16[512,512]{1,0:T(8,128)(2,1)S(1)}, bf16[3,512,512]{2,1,0:T(8,128)(2,1)S(1)}) custom-call(s32[2]{0:T(128)S(1)} %pad_add_fusion.at_ref, bf16[512,4096]{1,0:T(8,128)(2,1)} %w_own.13), custom_call_target="tpu_custom_call" | custom-call | tf_op jit(solution)/shard_map/sibling_columns/pallas_call | solution.py:207
  7.1 0.2 collective-permute-done
  7.4 7.0 %collective-permute-start.1 = (bf16[528,128]{1,0:T(8,128)(2,1)S(1)}, bf16[528,128]{1,0:T(8,128)(2,1)S(1)}, u32[]{:S(2)}, u32[]{:S(2)}) collective-permute-start(bf16[528,128]{1,0:T(8,128)(2,1)S(1)} %convert_element_type.40), channel_id=1, source_target_pairs={{0,40},{8,32},{16,56},{24,48},{32,8},{40,0},{48,24},{56,16},{1,41}... | collective-permute-start | bytes 405512 | tf_op jit(solution)/shard_map/ppermute | solution.py:316
  14.4 0.3 collective-permute-start.2
  14.6 0.9 %collective-permute-start.3 = (bf16[528,128]{1,0:T(8,128)(2,1)S(1)}, bf16[528,128]{1,0:T(8,128)(2,1)S(1)}, u32[]{:S(2)}, u32[]{:S(2)}) collective-permute-start(bf16[528,128]{1,0:T(8,128)(2,1)S(1)} %convert_element_type.40), channel_id=1, source_target_pairs={{0,16},{8,24},{16,0},{24,8},{32,48},{40,56},{48,32},{56,40},{1,17}... | collective-permute-start | bytes 405512 | tf_op jit(solution)/shard_map/ppermute | solution.py:316
  15.6 0.0 copy-done.1
  15.6 2.2 %collective-permute-start.7 = (bf16[512,512]{1,0:T(8,128)(2,1)S(1)}, bf16[512,512]{1,0:T(8,128)(2,1)S(1)}, u32[]{:S(2)}, u32[]{:S(2)}) collective-permute-start(bf16[512,512]{1,0:T(8,128)(2,1)S(1)} %get-tuple-element.66), channel_id=1, source_target_pairs={{0,1},{1,0},{2,3},{3,2},{4,5},{5,4},{6,7},{7,6},{8,9},{9,8},{10,11... | collective-permute-start | bytes 1572872 | tf_op jit(solution)/shard_map/ppermute | solution.py:316
  17.8 6.9 %attention.1 = (f32[4,1024,128]{2,1,0:T(8,128)}, bf16[4,1024,128]{2,1,0:T(8,128)(2,1)}) custom-call(f32[4]{0:T(128)S(1)} %add_divide_fusion.g_ref, bf16[1024,512]{1,0:T(8,128)(2,1)} %q_ref, bf16[1024,512]{1,0:T(8,128)(2,1)} %k_ref.2, bf16[1024,512]{1,0:T(8,128)(2,1)} %v_ref.2), custom_call_target="tpu_custom_call" | custom-call | tf_op jit(solution)/shard_map/attention/pallas_call | solution.py:123
  24.7 0.0 collective-permute-done.1
  24.7 1.0 %collective-permute-done.2 = bf16[528,128]{1,0:T(8,128)(2,1)S(1)} collective-permute-done((bf16[528,128]{1,0:T(8,128)(2,1)S(1)}, bf16[528,128]{1,0:T(8,128)(2,1)S(1)}, u32[]{:S(2)}, u32[]{:S(2)}) %collective-permute-start.2) | collective-permute-done | bytes 135200 | tf_op jit(solution)/shard_map/ppermute | solution.py:316
  25.7 1.0 %collective-permute-done.3 = bf16[528,128]{1,0:T(8,128)(2,1)S(1)} collective-permute-done((bf16[528,128]{1,0:T(8,128)(2,1)S(1)}, bf16[528,128]{1,0:T(8,128)(2,1)S(1)}, u32[]{:S(2)}, u32[]{:S(2)}) %collective-permute-start.3) | collective-permute-done | bytes 135200 | tf_op jit(solution)/shard_map/ppermute | solution.py:316
  26.7 0.1 convert_add_fusion
  26.8 0.1 fusion.2
  26.9 3.0 %collective-permute-start.4 = (bf16[528,128]{1,0:T(8,128)(2,1)S(1)}, bf16[528,128]{1,0:T(8,128)(2,1)S(1)}, u32[]{:S(2)}, u32[]{:S(2)}) collective-permute-start(bf16[528,128]{1,0:T(8,128)(2,1)S(1)} %convert_add_fusion), channel_id=1, source_target_pairs={{0,128},{64,192},{128,0},{192,64},{1,129},{65,193},{129,1},{193,65... | collective-permute-start | bytes 405512 | tf_op jit(solution)/shard_map/ppermute | solution.py:316
  29.9 0.4 collective-permute-start.5
  30.3 0.4 collective-permute-start.6
  30.7 0.0 copy-start
  30.7 2.0 %preload.1 = (f32[4,1024,128]{2,1,0:T(8,128)S(1)}, bf16[4,1024,128]{2,1,0:T(8,128)(2,1)S(1)}) custom-call(f32[4,1024,128]{2,1,0:T(8,128)} %get-tuple-element.62.refs_0_, bf16[4,1024,128]{2,1,0:T(8,128)(2,1)} %get-tuple-element.63.refs_1_), custom_call_target="tpu_custom_call" | custom-call | tf_op jit(solution)/shard_map/preload/pallas_call | solution.py:147
  32.7 0.0 collective-permute-done.4
  32.7 2.8 %collective-permute-done.5 = bf16[528,128]{1,0:T(8,128)(2,1)S(1)} collective-permute-done((bf16[528,128]{1,0:T(8,128)(2,1)S(1)}, bf16[528,128]{1,0:T(8,128)(2,1)S(1)}, u32[]{:S(2)}, u32[]{:S(2)}) %collective-permute-start.5) | collective-permute-done | bytes 135200 | tf_op jit(solution)/shard_map/ppermute | solution.py:316
  35.5 0.6 collective-permute-done.6
  36.1 0.0 collective-permute-done.7.w_sib
  36.1 0.1 select_add_fusion.refs_2_
  36.2 2.4 %collective-permute-start.9 = (bf16[3,512,512]{2,1,0:T(8,128)(2,1)S(1)}, bf16[3,512,512]{2,1,0:T(8,128)(2,1)S(1)}, u32[]{:S(2)}, u32[]{:S(2)}) collective-permute-start(bf16[3,512,512]{2,1,0:T(8,128)(2,1)S(1)} %get-tuple-element.76), channel_id=1, source_target_pairs={{0,1},{1,0},{2,3},{3,2},{4,5},{5,4},{6,7},{7,6},{8,9},{9,8},{10,11... | collective-permute-start | bytes 4718600 | tf_op jit(solution)/shard_map/ppermute | solution.py:316
  38.6 1.3 %retrieve.1 = (bf16[512,512]{1,0:T(8,128)(2,1)S(1)}, bf16[512,512]{1,0:T(8,128)(2,1)S(1)}) custom-call(f32[4]{0:T(128)S(1)} %add_divide_fusion.g_ref, f32[4,1024,128]{2,1,0:T(8,128)S(1)} %get-tuple-element.67.refs_0_, bf16[4,1024,128]{2,1,0:T(8,128)(2,1)S(1)} %get-tuple-element.68.refs_1_, bf16[528,128]{1,0:T(8,128)(2,1)S(1)} %select_add_fusion.refs_2_), custom_call_target="tpu_custom_call" | custom-call | tf_op jit(solution)/shard_map/retrieve/pallas_call | solution.py:181
  39.9 0.1 collective-permute-start.11
  40.0 0.5 collective-permute-start.8
  40.5 0.0 copy-done
  40.5 1.3 %project_far_own.1 = (f32[512,512]{1,0:T(8,128)S(1)}, f32[512,512]{1,0:T(8,128)S(1)}) custom-call(s32[2]{0:T(128)S(1)} %pad_add_fusion.at_ref, bf16[512,512]{1,0:T(8,128)(2,1)S(1)} %get-tuple-element.75.a_own.a1, bf16[512,512]{1,0:T(8,128)(2,1)S(1)} %get-tuple-element.77.a_own.a2, bf16[512,4096]{1,0:T(8,128)(2,1)S(1)} %copy-done), custom_call_target="tpu_custom_call" | custom-call | tf_op jit(solution)/shard_map/project_far_own/pallas_call | solution.py:242
  41.8 0.6 collective-permute-done.11.a_sib.a2
  42.4 0.7 collective-permute-done.8.a_sib.a1
  43.1 0.7 project_far.1
  43.8 2.6 %collective-permute-start.15 = (bf16[512,512]{1,0:T(8,128)(2,1)S(1)}, bf16[512,512]{1,0:T(8,128)(2,1)S(1)}, u32[]{:S(2)}, u32[]{:S(2)}) collective-permute-start(bf16[512,512]{1,0:T(8,128)(2,1)S(1)} %get-tuple-element.83), channel_id=1, source_target_pairs={{0,6},{2,4},{4,2},{6,0},{1,7},{3,5},{5,3},{7,1},{8,14},{10,12},{12... | collective-permute-start | bytes 1572872 | tf_op jit(solution)/shard_map/ppermute | solution.py:316
  46.4 0.0 collective-permute-start.13
  46.4 0.0 collective-permute-done.9.w_sib
  46.4 1.2 %project.8 = bf16[512,512]{1,0:T(8,128)(2,1)S(1)} custom-call(s32[2]{0:T(128)S(1)} %pad_add_fusion.at_ref, bf16[512,512]{1,0:T(8,128)(2,1)S(1)} %get-tuple-element.77.a_own.a2, bf16[512,512]{1,0:T(8,128)(2,1)S(1)} %collective-permute-done.11.a_sib.a2, bf16[512,4096]{1,0:T(8,128)(2,1)S(1)} %copy-done, bf16[3,512,512]{2,1,0:T(8,128)(2,1)S(1)} %collective-permute-done.9.w_sib), custom_call_target="tpu_custom_call" | custom-call | tf_op jit(solution)/shard_map/project/pallas_call | solution.py:276
  47.7 1.1 %collective-permute-start.12 = (bf16[512,512]{1,0:T(8,128)(2,1)S(1)}, bf16[512,512]{1,0:T(8,128)(2,1)S(1)}, u32[]{:S(2)}, u32[]{:S(2)}) collective-permute-start(bf16[512,512]{1,0:T(8,128)(2,1)S(1)} %project.8), channel_id=1, source_target_pairs={{0,6},{2,4},{4,2},{6,0},{1,7},{3,5},{5,3},{7,1},{8,14},{10,12},{12... | collective-permute-start | bytes 1572872 | tf_op jit(solution)/shard_map/ppermute | solution.py:316
  48.7 1.2 %project.6 = bf16[512,512]{1,0:T(8,128)(2,1)S(1)} custom-call(s32[2]{0:T(128)S(1)} %pad_add_fusion.at_ref, bf16[512,512]{1,0:T(8,128)(2,1)S(1)} %get-tuple-element.75.a_own.a1, bf16[512,512]{1,0:T(8,128)(2,1)S(1)} %collective-permute-done.8.a_sib.a1, bf16[512,4096]{1,0:T(8,128)(2,1)S(1)} %copy-done, bf16[3,512,512]{2,1,0:T(8,128)(2,1)S(1)} %collective-permute-done.9.w_sib), custom_call_target="tpu_custom_call" | custom-call | tf_op jit(solution)/shard_map/project/pallas_call | solution.py:276
  50.0 0.8 collective-permute-start.10
  50.8 7.5 %collective-permute-done.15.refs_0_ = bf16[512,512]{1,0:T(8,128)(2,1)S(1)} collective-permute-done((bf16[512,512]{1,0:T(8,128)(2,1)S(1)}, bf16[512,512]{1,0:T(8,128)(2,1)S(1)}, u32[]{:S(2)}, u32[]{:S(2)}) %collective-permute-start.15) | collective-permute-done | bytes 524320 | tf_op jit(solution)/shard_map/ppermute | solution.py:316
  58.3 1.3 %project.11 = bf16[512,512]{1,0:T(8,128)(2,1)S(1)} custom-call(s32[2]{0:T(128)S(1)} %pad_add_fusion.at_ref, bf16[512,512]{1,0:T(8,128)(2,1)S(1)} %get-tuple-element.77.a_own.a2, bf16[512,512]{1,0:T(8,128)(2,1)S(1)} %collective-permute-done.11.a_sib.a2, bf16[512,4096]{1,0:T(8,128)(2,1)S(1)} %copy-done, bf16[3,512,512]{2,1,0:T(8,128)(2,1)S(1)} %collective-permute-done.9.w_sib, ...), custom_call_target="tpu_custom_call" | custom-call | tf_op jit(solution)/shard_map/project/pallas_call | solution.py:276
  59.5 0.1 collective-permute-start.16
  59.6 0.0 collective-permute-done.13.refs_0_
  59.7 1.3 %project.10 = bf16[512,512]{1,0:T(8,128)(2,1)S(1)} custom-call(s32[2]{0:T(128)S(1)} %pad_add_fusion.at_ref, bf16[512,512]{1,0:T(8,128)(2,1)S(1)} %get-tuple-element.75.a_own.a1, bf16[512,512]{1,0:T(8,128)(2,1)S(1)} %collective-permute-done.8.a_sib.a1, bf16[512,4096]{1,0:T(8,128)(2,1)S(1)} %copy-done, bf16[3,512,512]{2,1,0:T(8,128)(2,1)S(1)} %collective-permute-done.9.w_sib, ...), custom_call_target="tpu_custom_call" | custom-call | tf_op jit(solution)/shard_map/project/pallas_call | solution.py:276
  60.9 2.6 %collective-permute-start.14 = (bf16[512,512]{1,0:T(8,128)(2,1)S(1)}, bf16[512,512]{1,0:T(8,128)(2,1)S(1)}, u32[]{:S(2)}, u32[]{:S(2)}) collective-permute-start(bf16[512,512]{1,0:T(8,128)(2,1)S(1)} %project.10), channel_id=1, source_target_pairs={{0,6},{2,4},{4,2},{6,0},{1,7},{3,5},{5,3},{7,1},{8,14},{10,12},{12... | collective-permute-start | bytes 1572872 | tf_op jit(solution)/shard_map/ppermute | solution.py:316
  63.5 6.0 %collective-permute-done.12.refs_0_ = bf16[512,512]{1,0:T(8,128)(2,1)S(1)} collective-permute-done((bf16[512,512]{1,0:T(8,128)(2,1)S(1)}, bf16[512,512]{1,0:T(8,128)(2,1)S(1)}, u32[]{:S(2)}, u32[]{:S(2)}) %collective-permute-start.12) | collective-permute-done | bytes 524320 | tf_op jit(solution)/shard_map/ppermute | solution.py:316
  69.5 1.3 %project.9.p2 = f32[512,512]{1,0:T(8,128)S(1)} custom-call(s32[2]{0:T(128)S(1)} %pad_add_fusion.at_ref, bf16[512,512]{1,0:T(8,128)(2,1)S(1)} %get-tuple-element.77.a_own.a2, bf16[512,512]{1,0:T(8,128)(2,1)S(1)} %collective-permute-done.11.a_sib.a2, bf16[512,4096]{1,0:T(8,128)(2,1)S(1)} %copy-done, bf16[3,512,512]{2,1,0:T(8,128)(2,1)S(1)} %collective-permute-done.9.w_sib, ...), custom_call_target="tpu_custom_call" | custom-call | tf_op jit(solution)/shard_map/project/pallas_call | solution.py:276
  70.8 0.0 collective-permute-done.10.refs_0_
  70.8 1.3 %project.7.p1 = f32[512,512]{1,0:T(8,128)S(1)} custom-call(s32[2]{0:T(128)S(1)} %pad_add_fusion.at_ref, bf16[512,512]{1,0:T(8,128)(2,1)S(1)} %get-tuple-element.75.a_own.a1, bf16[512,512]{1,0:T(8,128)(2,1)S(1)} %collective-permute-done.8.a_sib.a1, bf16[512,4096]{1,0:T(8,128)(2,1)S(1)} %copy-done, bf16[3,512,512]{2,1,0:T(8,128)(2,1)S(1)} %collective-permute-done.9.w_sib, ...), custom_call_target="tpu_custom_call" | custom-call | tf_op jit(solution)/shard_map/project/pallas_call | solution.py:276
  72.0 9.6 %collective-permute-done.16.r2 = bf16[512,512]{1,0:T(8,128)(2,1)S(1)} collective-permute-done((bf16[512,512]{1,0:T(8,128)(2,1)S(1)}, bf16[512,512]{1,0:T(8,128)(2,1)S(1)}, u32[]{:S(2)}, u32[]{:S(2)}) %collective-permute-start.16) | collective-permute-done | bytes 524320 | tf_op jit(solution)/shard_map/ppermute | solution.py:316
  81.7 0.0 collective-permute-done.14.r1
  81.7 1.1 %finish.1 = bf16[1024,512]{1,0:T(8,128)(2,1)} custom-call(f32[512,512]{1,0:T(8,128)S(1)} %project.7.p1, f32[512,512]{1,0:T(8,128)S(1)} %project.9.p2, bf16[512,512]{1,0:T(8,128)(2,1)S(1)} %collective-permute-done.14.r1, bf16[512,512]{1,0:T(8,128)(2,1)S(1)} %collective-permute-done.16.r2), custom_call_target="tpu_custom_call" | custom-call | tf_op jit(solution)/shard_map/finish/pallas_call | solution.py:303
  (3 shorter events, 0.1 us)
Async XLA Ops:
  2.4 5.0 %collective-permute-start = (bf16[528,128]{1,0:T(8,128)(2,1)S(1)}, bf16[528,128]{1,0:T(8,128)(2,1)S(1)}, u32[]{:S(2)}, u32[]{:S(2)}) collective-permute-start(bf16[528,128]{1,0:T(8,128)(2,1)S(1)} %delta.1), channel_id=1, source_target_pairs={{0,8},{8,0},{16,24},{24,16},{32,40},{40,32},{48,56},{56,48},{1,9},... | collective-permute-start | bytes 405512 | tf_op jit(solution)/shard_map/ppermute | solution.py:316
  5.0 10.6 %copy-start.1 = (f32[4]{0:T(128)S(1)}, f32[4]{0:T(128)}, u32[]{:S(2)}) copy-start(f32[4]{0:T(128)} %param.8) | copy-start | bytes 52
  7.4 17.3 %collective-permute-start.1 = (bf16[528,128]{1,0:T(8,128)(2,1)S(1)}, bf16[528,128]{1,0:T(8,128)(2,1)S(1)}, u32[]{:S(2)}, u32[]{:S(2)}) collective-permute-start(bf16[528,128]{1,0:T(8,128)(2,1)S(1)} %convert_element_type.40), channel_id=1, source_target_pairs={{0,40},{8,32},{16,56},{24,48},{32,8},{40,0},{48,24},{56,16},{1,41}... | collective-permute-start | bytes 405512 | tf_op jit(solution)/shard_map/ppermute | solution.py:316
  14.4 11.3 %collective-permute-start.2 = (bf16[528,128]{1,0:T(8,128)(2,1)S(1)}, bf16[528,128]{1,0:T(8,128)(2,1)S(1)}, u32[]{:S(2)}, u32[]{:S(2)}) collective-permute-start(bf16[528,128]{1,0:T(8,128)(2,1)S(1)} %convert_element_type.40), channel_id=1, source_target_pairs={{0,48},{8,56},{16,32},{24,40},{32,16},{40,24},{48,0},{56,8},{1,49}... | collective-permute-start | bytes 405512 | tf_op jit(solution)/shard_map/ppermute | solution.py:316
  14.6 12.1 %collective-permute-start.3 = (bf16[528,128]{1,0:T(8,128)(2,1)S(1)}, bf16[528,128]{1,0:T(8,128)(2,1)S(1)}, u32[]{:S(2)}, u32[]{:S(2)}) collective-permute-start(bf16[528,128]{1,0:T(8,128)(2,1)S(1)} %convert_element_type.40), channel_id=1, source_target_pairs={{0,16},{8,24},{16,0},{24,8},{32,48},{40,56},{48,32},{56,40},{1,17}... | collective-permute-start | bytes 405512 | tf_op jit(solution)/shard_map/ppermute | solution.py:316
  15.6 20.6 %collective-permute-start.7 = (bf16[512,512]{1,0:T(8,128)(2,1)S(1)}, bf16[512,512]{1,0:T(8,128)(2,1)S(1)}, u32[]{:S(2)}, u32[]{:S(2)}) collective-permute-start(bf16[512,512]{1,0:T(8,128)(2,1)S(1)} %get-tuple-element.66), channel_id=1, source_target_pairs={{0,1},{1,0},{2,3},{3,2},{4,5},{5,4},{6,7},{7,6},{8,9},{9,8},{10,11... | collective-permute-start | bytes 1572872 | tf_op jit(solution)/shard_map/ppermute | solution.py:316
  26.9 5.8 %collective-permute-start.4 = (bf16[528,128]{1,0:T(8,128)(2,1)S(1)}, bf16[528,128]{1,0:T(8,128)(2,1)S(1)}, u32[]{:S(2)}, u32[]{:S(2)}) collective-permute-start(bf16[528,128]{1,0:T(8,128)(2,1)S(1)} %convert_add_fusion), channel_id=1, source_target_pairs={{0,128},{64,192},{128,0},{192,64},{1,129},{65,193},{129,1},{193,65... | collective-permute-start | bytes 405512 | tf_op jit(solution)/shard_map/ppermute | solution.py:316
  29.9 5.6 %collective-permute-start.5 = (bf16[528,128]{1,0:T(8,128)(2,1)S(1)}, bf16[528,128]{1,0:T(8,128)(2,1)S(1)}, u32[]{:S(2)}, u32[]{:S(2)}) collective-permute-start(bf16[528,128]{1,0:T(8,128)(2,1)S(1)} %convert_add_fusion), channel_id=1, source_target_pairs={{0,64},{64,0},{128,192},{192,128},{1,65},{65,1},{129,193},{193,129... | collective-permute-start | bytes 405512 | tf_op jit(solution)/shard_map/ppermute | solution.py:316
  30.3 5.8 %collective-permute-start.6 = (bf16[528,128]{1,0:T(8,128)(2,1)S(1)}, bf16[528,128]{1,0:T(8,128)(2,1)S(1)}, u32[]{:S(2)}, u32[]{:S(2)}) collective-permute-start(bf16[528,128]{1,0:T(8,128)(2,1)S(1)} %convert_add_fusion), channel_id=1, source_target_pairs={{0,192},{64,128},{128,64},{192,0},{1,193},{65,129},{129,65},{193,1... | collective-permute-start | bytes 405512 | tf_op jit(solution)/shard_map/ppermute | solution.py:316
  30.7 9.9 %copy-start = (bf16[512,4096]{1,0:T(8,128)(2,1)S(1)}, bf16[512,4096]{1,0:T(8,128)(2,1)}, u32[]{:S(2)}) copy-start(bf16[512,4096]{1,0:T(8,128)(2,1)} %w_own.13) | copy-start | bytes 12582916
  36.2 10.2 %collective-permute-start.9 = (bf16[3,512,512]{2,1,0:T(8,128)(2,1)S(1)}, bf16[3,512,512]{2,1,0:T(8,128)(2,1)S(1)}, u32[]{:S(2)}, u32[]{:S(2)}) collective-permute-start(bf16[3,512,512]{2,1,0:T(8,128)(2,1)S(1)} %get-tuple-element.76), channel_id=1, source_target_pairs={{0,1},{1,0},{2,3},{3,2},{4,5},{5,4},{6,7},{7,6},{8,9},{9,8},{10,11... | collective-permute-start | bytes 4718600 | tf_op jit(solution)/shard_map/ppermute | solution.py:316
  39.9 2.4 %collective-permute-start.11 = (bf16[512,512]{1,0:T(8,128)(2,1)S(1)}, bf16[512,512]{1,0:T(8,128)(2,1)S(1)}, u32[]{:S(2)}, u32[]{:S(2)}) collective-permute-start(bf16[512,512]{1,0:T(8,128)(2,1)S(1)} %get-tuple-element.77.a_own.a2), channel_id=1, source_target_pairs={{0,1},{1,0},{2,3},{3,2},{4,5},{5,4},{6,7},{7,6},{8,9},{9,8},{10,11... | collective-permute-start | bytes 1572872 | tf_op jit(solution)/shard_map/ppermute | solution.py:316
  40.0 3.1 %collective-permute-start.8 = (bf16[512,512]{1,0:T(8,128)(2,1)S(1)}, bf16[512,512]{1,0:T(8,128)(2,1)S(1)}, u32[]{:S(2)}, u32[]{:S(2)}) collective-permute-start(bf16[512,512]{1,0:T(8,128)(2,1)S(1)} %get-tuple-element.75.a_own.a1), channel_id=1, source_target_pairs={{0,1},{1,0},{2,3},{3,2},{4,5},{5,4},{6,7},{7,6},{8,9},{9,8},{10,11... | collective-permute-start | bytes 1572872 | tf_op jit(solution)/shard_map/ppermute | solution.py:316
  43.8 14.4 %collective-permute-start.15 = (bf16[512,512]{1,0:T(8,128)(2,1)S(1)}, bf16[512,512]{1,0:T(8,128)(2,1)S(1)}, u32[]{:S(2)}, u32[]{:S(2)}) collective-permute-start(bf16[512,512]{1,0:T(8,128)(2,1)S(1)} %get-tuple-element.83), channel_id=1, source_target_pairs={{0,6},{2,4},{4,2},{6,0},{1,7},{3,5},{5,3},{7,1},{8,14},{10,12},{12... | collective-permute-start | bytes 1572872 | tf_op jit(solution)/shard_map/ppermute | solution.py:316
  46.4 13.2 %collective-permute-start.13 = (bf16[512,512]{1,0:T(8,128)(2,1)S(1)}, bf16[512,512]{1,0:T(8,128)(2,1)S(1)}, u32[]{:S(2)}, u32[]{:S(2)}) collective-permute-start(bf16[512,512]{1,0:T(8,128)(2,1)S(1)} %get-tuple-element.81), channel_id=1, source_target_pairs={{0,2},{2,0},{4,6},{6,4},{1,3},{3,1},{5,7},{7,5},{8,10},{10,8},{12,... | collective-permute-start | bytes 1572872 | tf_op jit(solution)/shard_map/ppermute | solution.py:316
  47.7 21.8 %collective-permute-start.12 = (bf16[512,512]{1,0:T(8,128)(2,1)S(1)}, bf16[512,512]{1,0:T(8,128)(2,1)S(1)}, u32[]{:S(2)}, u32[]{:S(2)}) collective-permute-start(bf16[512,512]{1,0:T(8,128)(2,1)S(1)} %project.8), channel_id=1, source_target_pairs={{0,6},{2,4},{4,2},{6,0},{1,7},{3,5},{5,3},{7,1},{8,14},{10,12},{12... | collective-permute-start | bytes 1572872 | tf_op jit(solution)/shard_map/ppermute | solution.py:316
  50.0 20.8 %collective-permute-start.10 = (bf16[512,512]{1,0:T(8,128)(2,1)S(1)}, bf16[512,512]{1,0:T(8,128)(2,1)S(1)}, u32[]{:S(2)}, u32[]{:S(2)}) collective-permute-start(bf16[512,512]{1,0:T(8,128)(2,1)S(1)} %project.6), channel_id=1, source_target_pairs={{0,2},{2,0},{4,6},{6,4},{1,3},{3,1},{5,7},{7,5},{8,10},{10,8},{12,... | collective-permute-start | bytes 1572872 | tf_op jit(solution)/shard_map/ppermute | solution.py:316
  59.5 22.2 %collective-permute-start.16 = (bf16[512,512]{1,0:T(8,128)(2,1)S(1)}, bf16[512,512]{1,0:T(8,128)(2,1)S(1)}, u32[]{:S(2)}, u32[]{:S(2)}) collective-permute-start(bf16[512,512]{1,0:T(8,128)(2,1)S(1)} %project.11), channel_id=1, source_target_pairs={{0,2},{2,0},{4,6},{6,4},{1,3},{3,1},{5,7},{7,5},{8,10},{10,8},{12,... | collective-permute-start | bytes 1572872 | tf_op jit(solution)/shard_map/ppermute | solution.py:316
  60.9 20.8 %collective-permute-start.14 = (bf16[512,512]{1,0:T(8,128)(2,1)S(1)}, bf16[512,512]{1,0:T(8,128)(2,1)S(1)}, u32[]{:S(2)}, u32[]{:S(2)}) collective-permute-start(bf16[512,512]{1,0:T(8,128)(2,1)S(1)} %project.10), channel_id=1, source_target_pairs={{0,6},{2,4},{4,2},{6,0},{1,7},{3,5},{5,3},{7,1},{8,14},{10,12},{12... | collective-permute-start | bytes 1572872 | tf_op jit(solution)/shard_map/ppermute | solution.py:316

commit v7 on v6

--- a/solution.py
+++ b/solution.py
@@ -10,7 +10,7 @@
 from jax.sharding import PartitionSpec as P
 
 HD = 128
-REST = {0: 0, 1: 1, 3: 2}
+REST = {0: 0, 1: 0, 3: 1}
 PAD = 16
 QB = 256
 NT = (((1,), (1,)), ((), ()))
@@ -188,13 +188,13 @@
     )(gate, *[near_core(a) for a in arrays], near_core(state))
 
 
-def sibling_kernel(at_ref, w_ref, far_ref, rest_ref, sems):
+def sibling_kernel(at_ref, w_ref, far_ref, near_ref, mine_ref, sems):
     width = far_ref.shape[1]
     copies = []
     for k in range(4):
         to = lax.bitwise_xor(at_ref[0], k)
         cols = pl.ds(pl.multiple_of((2 * to + 1 - at_ref[1]) * width, width), width)
-        target = far_ref if k == 2 else rest_ref.at[REST[k]]
+        target = far_ref if k == 2 else (near_ref if k else mine_ref).at[REST[k]]
         copies.append(pltpu.make_async_copy(w_ref.at[:, cols], target, sems.at[k]))
     for copy in copies:
         copy.start()
@@ -207,10 +207,11 @@
     return pl.pallas_call(
         sibling_kernel,
         in_specs=[SMEM, pl.BlockSpec(memory_space=pltpu.HBM)],
-        out_specs=[VMEM, VMEM],
+        out_specs=[VMEM] * 3,
         out_shape=[
             pltpu.VMEM((depth, cols // 8), BF16),
-            pltpu.VMEM((3, depth, cols // 8), BF16),
+            pltpu.VMEM((2, depth, cols // 8), BF16),
+            pltpu.VMEM((1, depth, cols // 8), BF16),
         ],
         scratch_shapes=[pltpu.SemaphoreType.DMA((4,))],
         compiler_params=PARAMS,
@@ -355,13 +356,15 @@
     halves = [(a_own, swap(a_own, "c", 1)) for a_own in attended]
 
     def mm(side, k, adds, dtype):
-        return project(at, halves[side], w_own, w_sib, k, adds, dtype)
+        return project(at, halves[side], w_own, w_sib if k else w_mine, k, adds, dtype)
 
     hops = ((1, 3), (3, 1))
     far = project_far(at, halves, w_own, w_far)
     far = [swap(far[i], "x", hops[i][0]) for i in range(2)]
     near = [mm(i, hops[i][0], (), BF16) for i in range(2)]
     far = [lax.optimization_barrier((far[i], near))[0] for i in range(2)]
+    w_mine, _ = lax.optimization_barrier((w_out[2], near))
+    w_mine = swap(w_mine, "c", 1)
     near = [swap(near[i], "x", hops[i][0]) for i in range(2)]
     passed = [swap(mm(i, hops[i][1], (far[i],), BF16), "x", hops[i][1]) for i in range(2)]
     mine = [mm(i, 0, (near[i],), F32) for i in range(2)]

time: 83.1 us -> 82.2 us (0.989)
  waiting for transfers between devices: 30.2 us -> 27.3 us
  starting transfers between devices: 26.7 us -> 28.7 us
    ppermute x17 -> x18, waiting for transfers between devices: 30.2 us -> 27.3 us  [swap(): return lax.ppermute(array, axis, [(i, i ^ mask) for i in range(size)])]
    ppermute x17 -> x18, starting transfers between devices: 26.7 us -> 28.7 us  [swap(): return lax.ppermute(array, axis, [(i, i ^ mask) for i in range(size)])]
  transfers between devices with their start and end apart: 17 -> 18, of which waited for: 10 -> 9; matrix products, arithmetic and copies ran while one was open for 0% -> 0% of each run, Pallas kernels for 26% -> 25%
where the time goes in v7:
time: 82.2 us; the launch traced here: 82 us
  starting transfers between devices  28.7 us (35%)
  waiting for transfers between devices  27.3 us (33%)
  Pallas kernels  25.3 us (31%)
    ppermute x18, starting transfers between devices, swap(): return lax.ppermute(array, axis, [(i, i ^ mask) for i in range(size)])  28.7 us
    ppermute x18, waiting for transfers between devices, swap(): return lax.ppermute(array, axis, [(i, i ^ mask) for i in range(size)])  27.3 us
    pallas_call x6, Pallas kernels, project(): pl.pallas_call(functools.partial(project_kernel, k), in_specs=[SMEM] + [V...  7.49 us
    pallas_call x1, Pallas kernels, attention(): pl.pallas_call(functools.partial(attention_kernel, first), grid=(count,),...  6.9 us
    pallas_call x1, Pallas kernels, delta(): pl.pallas_call(delta_kernel, grid=(rows // block,), in_specs=[spec, spec]...  2.37 us
    pallas_call x1, Pallas kernels, sibling_columns(): pl.pallas_call(sibling_kernel, in_specs=[SMEM, pl.BlockSpec(memory_space=...  2.11 us
    pallas_call x1, Pallas kernels, preload(): pl.pallas_call(preload_kernel, in_specs=[pl.BlockSpec(memory_space=pltpu....  2.02 us
  transfers between devices with their start and end apart: 18, of which 9 were waited for; matrix products, arithmetic and copies ran while one was open for 0% of the time, Pallas kernels for 25%

profile of v7, /device:TPU:1, one launch (start us, length us, event | category | flops | bytes accessed | tf_op | source)
XLA Modules:
  0.0 82.0 jit_solution(14431009820569392229)
XLA Ops:
  0.0 2.4 %delta.1 = bf16[528,128]{1,0:T(8,128)(2,1)S(1)} custom-call(bf16[1024,512]{1,0:T(8,128)(2,1)} %k_ref.2, bf16[1024,512]{1,0:T(8,128)(2,1)} %v_ref.2), custom_call_target="tpu_custom_call" | custom-call | tf_op jit(solution)/shard_map/delta/pallas_call | solution.py:70
  2.4 2.5 %collective-permute-start = (bf16[528,128]{1,0:T(8,128)(2,1)S(1)}, bf16[528,128]{1,0:T(8,128)(2,1)S(1)}, u32[]{:S(2)}, u32[]{:S(2)}) collective-permute-start(bf16[528,128]{1,0:T(8,128)(2,1)S(1)} %delta.1), channel_id=1, source_target_pairs={{0,8},{8,0},{16,24},{24,16},{32,40},{40,32},{48,56},{56,48},{1,9},... | collective-permute-start | bytes 405512 | tf_op jit(solution)/shard_map/ppermute | solution.py:317
  4.9 0.1 pad_add_fusion.at_ref
  5.0 0.0 copy-start.1
  5.0 2.1 %sibling_columns.1 = (bf16[512,512]{1,0:T(8,128)(2,1)S(1)}, bf16[2,512,512]{2,1,0:T(8,128)(2,1)S(1)}, bf16[1,512,512]{2,1,0:T(8,128)(2,1)S(1)}) custom-call(s32[2]{0:T(128)S(1)} %pad_add_fusion.at_ref, bf16[512,4096]{1,0:T(8,128)(2,1)} %w_own.13), custom_call_target="tpu_custom_call" | custom-call | tf_op jit(solution)/shard_map/sibling_columns/pallas_call | solution.py:207
  7.1 0.2 collective-permute-done
  7.4 7.0 %collective-permute-start.1 = (bf16[528,128]{1,0:T(8,128)(2,1)S(1)}, bf16[528,128]{1,0:T(8,128)(2,1)S(1)}, u32[]{:S(2)}, u32[]{:S(2)}) collective-permute-start(bf16[528,128]{1,0:T(8,128)(2,1)S(1)} %convert_element_type.40), channel_id=1, source_target_pairs={{0,40},{8,32},{16,56},{24,48},{32,8},{40,0},{48,24},{56,16},{1,41}... | collective-permute-start | bytes 405512 | tf_op jit(solution)/shard_map/ppermute | solution.py:317
  14.4 0.3 collective-permute-start.2
  14.6 0.9 %collective-permute-start.3 = (bf16[528,128]{1,0:T(8,128)(2,1)S(1)}, bf16[528,128]{1,0:T(8,128)(2,1)S(1)}, u32[]{:S(2)}, u32[]{:S(2)}) collective-permute-start(bf16[528,128]{1,0:T(8,128)(2,1)S(1)} %convert_element_type.40), channel_id=1, source_target_pairs={{0,16},{8,24},{16,0},{24,8},{32,48},{40,56},{48,32},{56,40},{1,17}... | collective-permute-start | bytes 405512 | tf_op jit(solution)/shard_map/ppermute | solution.py:317
  15.6 0.0 copy-done.1
  15.6 2.2 %collective-permute-start.7 = (bf16[512,512]{1,0:T(8,128)(2,1)S(1)}, bf16[512,512]{1,0:T(8,128)(2,1)S(1)}, u32[]{:S(2)}, u32[]{:S(2)}) collective-permute-start(bf16[512,512]{1,0:T(8,128)(2,1)S(1)} %get-tuple-element.70), channel_id=1, source_target_pairs={{0,1},{1,0},{2,3},{3,2},{4,5},{5,4},{6,7},{7,6},{8,9},{9,8},{10,11... | collective-permute-start | bytes 1572872 | tf_op jit(solution)/shard_map/ppermute | solution.py:317
  17.8 6.9 %attention.1 = (f32[4,1024,128]{2,1,0:T(8,128)}, bf16[4,1024,128]{2,1,0:T(8,128)(2,1)}) custom-call(f32[4]{0:T(128)S(1)} %add_divide_fusion.g_ref, bf16[1024,512]{1,0:T(8,128)(2,1)} %q_ref, bf16[1024,512]{1,0:T(8,128)(2,1)} %k_ref.2, bf16[1024,512]{1,0:T(8,128)(2,1)} %v_ref.2), custom_call_target="tpu_custom_call" | custom-call | tf_op jit(solution)/shard_map/attention/pallas_call | solution.py:123
  24.7 0.0 collective-permute-done.1
  24.7 1.0 %collective-permute-done.2 = bf16[528,128]{1,0:T(8,128)(2,1)S(1)} collective-permute-done((bf16[528,128]{1,0:T(8,128)(2,1)S(1)}, bf16[528,128]{1,0:T(8,128)(2,1)S(1)}, u32[]{:S(2)}, u32[]{:S(2)}) %collective-permute-start.2) | collective-permute-done | bytes 135200 | tf_op jit(solution)/shard_map/ppermute | solution.py:317
  25.7 1.0 %collective-permute-done.3 = bf16[528,128]{1,0:T(8,128)(2,1)S(1)} collective-permute-done((bf16[528,128]{1,0:T(8,128)(2,1)S(1)}, bf16[528,128]{1,0:T(8,128)(2,1)S(1)}, u32[]{:S(2)}, u32[]{:S(2)}) %collective-permute-start.3) | collective-permute-done | bytes 135200 | tf_op jit(solution)/shard_map/ppermute | solution.py:317
  26.7 0.1 convert_add_fusion
  26.8 0.1 fusion.2
  26.9 3.0 %collective-permute-start.4 = (bf16[528,128]{1,0:T(8,128)(2,1)S(1)}, bf16[528,128]{1,0:T(8,128)(2,1)S(1)}, u32[]{:S(2)}, u32[]{:S(2)}) collective-permute-start(bf16[528,128]{1,0:T(8,128)(2,1)S(1)} %convert_add_fusion), channel_id=1, source_target_pairs={{0,128},{64,192},{128,0},{192,64},{1,129},{65,193},{129,1},{193,65... | collective-permute-start | bytes 405512 | tf_op jit(solution)/shard_map/ppermute | solution.py:317
  29.9 0.4 collective-permute-start.5
  30.3 0.4 collective-permute-start.6
  30.7 0.0 copy-start
  30.7 2.0 %preload.1 = (f32[4,1024,128]{2,1,0:T(8,128)S(1)}, bf16[4,1024,128]{2,1,0:T(8,128)(2,1)S(1)}) custom-call(f32[4,1024,128]{2,1,0:T(8,128)} %get-tuple-element.66.refs_0_, bf16[4,1024,128]{2,1,0:T(8,128)(2,1)} %get-tuple-element.67.refs_1_), custom_call_target="tpu_custom_call" | custom-call | tf_op jit(solution)/shard_map/preload/pallas_call | solution.py:147
  32.7 0.0 collective-permute-done.4
  32.7 2.8 %collective-permute-done.5 = bf16[528,128]{1,0:T(8,128)(2,1)S(1)} collective-permute-done((bf16[528,128]{1,0:T(8,128)(2,1)S(1)}, bf16[528,128]{1,0:T(8,128)(2,1)S(1)}, u32[]{:S(2)}, u32[]{:S(2)}) %collective-permute-start.5) | collective-permute-done | bytes 135200 | tf_op jit(solution)/shard_map/ppermute | solution.py:317
  35.5 0.6 collective-permute-done.6
  36.1 0.0 collective-permute-done.7.w_sib
  36.1 0.1 select_add_fusion.refs_2_
  36.2 1.4 %retrieve.1 = (bf16[512,512]{1,0:T(8,128)(2,1)S(1)}, bf16[512,512]{1,0:T(8,128)(2,1)S(1)}) custom-call(f32[4]{0:T(128)S(1)} %add_divide_fusion.g_ref, f32[4,1024,128]{2,1,0:T(8,128)S(1)} %get-tuple-element.71.refs_0_, bf16[4,1024,128]{2,1,0:T(8,128)(2,1)S(1)} %get-tuple-element.72.refs_1_, bf16[528,128]{1,0:T(8,128)(2,1)S(1)} %select_add_fusion.refs_2_), custom_call_target="tpu_custom_call" | custom-call | tf_op jit(solution)/shard_map/retrieve/pallas_call | solution.py:181
  37.6 2.4 %collective-permute-start.10 = (bf16[512,512]{1,0:T(8,128)(2,1)S(1)}, bf16[512,512]{1,0:T(8,128)(2,1)S(1)}, u32[]{:S(2)}, u32[]{:S(2)}) collective-permute-start(bf16[512,512]{1,0:T(8,128)(2,1)S(1)} %get-tuple-element.82.a_own.a2), channel_id=1, source_target_pairs={{0,1},{1,0},{2,3},{3,2},{4,5},{5,4},{6,7},{7,6},{8,9},{9,8},{10,11... | collective-permute-start | bytes 1572872 | tf_op jit(solution)/shard_map/ppermute | solution.py:317
  39.9 0.1 collective-permute-start.8
  40.0 0.4 collective-permute-start.9
  40.5 0.0 copy-done
  40.5 1.3 %project_far_own.1 = (f32[512,512]{1,0:T(8,128)S(1)}, f32[512,512]{1,0:T(8,128)S(1)}) custom-call(s32[2]{0:T(128)S(1)} %pad_add_fusion.at_ref, bf16[512,512]{1,0:T(8,128)(2,1)S(1)} %get-tuple-element.79.a_own.a1, bf16[512,512]{1,0:T(8,128)(2,1)S(1)} %get-tuple-element.82.a_own.a2, bf16[512,4096]{1,0:T(8,128)(2,1)S(1)} %copy-done), custom_call_target="tpu_custom_call" | custom-call | tf_op jit(solution)/shard_map/project_far_own/pallas_call | solution.py:243
  41.7 0.0 collective-permute-done.10.a_sib.a2
  41.7 0.5 collective-permute-done.8.a_sib.a1
  42.2 0.7 project_far.1
  43.0 2.6 %collective-permute-start.16 = (bf16[512,512]{1,0:T(8,128)(2,1)S(1)}, bf16[512,512]{1,0:T(8,128)(2,1)S(1)}, u32[]{:S(2)}, u32[]{:S(2)}) collective-permute-start(bf16[512,512]{1,0:T(8,128)(2,1)S(1)} %get-tuple-element.89), channel_id=1, source_target_pairs={{0,6},{2,4},{4,2},{6,0},{1,7},{3,5},{5,3},{7,1},{8,14},{10,12},{12... | collective-permute-start | bytes 1572872 | tf_op jit(solution)/shard_map/ppermute | solution.py:317
  45.5 0.0 collective-permute-start.14
  45.5 0.0 collective-permute-done.9.w_sib
  45.5 1.2 %project.7 = bf16[512,512]{1,0:T(8,128)(2,1)S(1)} custom-call(s32[2]{0:T(128)S(1)} %pad_add_fusion.at_ref, bf16[512,512]{1,0:T(8,128)(2,1)S(1)} %get-tuple-element.82.a_own.a2, bf16[512,512]{1,0:T(8,128)(2,1)S(1)} %collective-permute-done.10.a_sib.a2, bf16[512,4096]{1,0:T(8,128)(2,1)S(1)} %copy-done, bf16[2,512,512]{2,1,0:T(8,128)(2,1)S(1)} %collective-permute-done.9.w_sib), custom_call_target="tpu_custom_call" | custom-call | tf_op jit(solution)/shard_map/project/pallas_call | solution.py:277
  46.8 1.1 %collective-permute-start.13 = (bf16[512,512]{1,0:T(8,128)(2,1)S(1)}, bf16[512,512]{1,0:T(8,128)(2,1)S(1)}, u32[]{:S(2)}, u32[]{:S(2)}) collective-permute-start(bf16[512,512]{1,0:T(8,128)(2,1)S(1)} %project.7), channel_id=1, source_target_pairs={{0,6},{2,4},{4,2},{6,0},{1,7},{3,5},{5,3},{7,1},{8,14},{10,12},{12... | collective-permute-start | bytes 1572872 | tf_op jit(solution)/shard_map/ppermute | solution.py:317
  47.8 1.2 %project.6 = bf16[512,512]{1,0:T(8,128)(2,1)S(1)} custom-call(s32[2]{0:T(128)S(1)} %pad_add_fusion.at_ref, bf16[512,512]{1,0:T(8,128)(2,1)S(1)} %get-tuple-element.79.a_own.a1, bf16[512,512]{1,0:T(8,128)(2,1)S(1)} %collective-permute-done.8.a_sib.a1, bf16[512,4096]{1,0:T(8,128)(2,1)S(1)} %copy-done, bf16[2,512,512]{2,1,0:T(8,128)(2,1)S(1)} %collective-permute-done.9.w_sib), custom_call_target="tpu_custom_call" | custom-call | tf_op jit(solution)/shard_map/project/pallas_call | solution.py:277
  49.1 0.8 collective-permute-start.12
  49.9 7.5 %collective-permute-done.16.refs_0_ = bf16[512,512]{1,0:T(8,128)(2,1)S(1)} collective-permute-done((bf16[512,512]{1,0:T(8,128)(2,1)S(1)}, bf16[512,512]{1,0:T(8,128)(2,1)S(1)}, u32[]{:S(2)}, u32[]{:S(2)}) %collective-permute-start.16) | collective-permute-done | bytes 524320 | tf_op jit(solution)/shard_map/ppermute | solution.py:317
  57.4 1.3 %project.11 = bf16[512,512]{1,0:T(8,128)(2,1)S(1)} custom-call(s32[2]{0:T(128)S(1)} %pad_add_fusion.at_ref, bf16[512,512]{1,0:T(8,128)(2,1)S(1)} %get-tuple-element.82.a_own.a2, bf16[512,512]{1,0:T(8,128)(2,1)S(1)} %collective-permute-done.10.a_sib.a2, bf16[512,4096]{1,0:T(8,128)(2,1)S(1)} %copy-done, bf16[2,512,512]{2,1,0:T(8,128)(2,1)S(1)} %collective-permute-done.9.w_sib, ...), custom_call_target="tpu_custom_call" | custom-call | tf_op jit(solution)/shard_map/project/pallas_call | solution.py:277
  58.7 0.1 collective-permute-start.17
  58.8 2.3 %collective-permute-start.11 = (bf16[1,512,512]{2,1,0:T(8,128)(2,1)S(1)}, bf16[1,512,512]{2,1,0:T(8,128)(2,1)S(1)}, u32[]{:S(2)}, u32[]{:S(2)}) collective-permute-start(bf16[1,512,512]{2,1,0:T(8,128)(2,1)S(1)} %get-tuple-element.83), channel_id=1, source_target_pairs={{0,1},{1,0},{2,3},{3,2},{4,5},{5,4},{6,7},{7,6},{8,9},{9,8},{10,11... | collective-permute-start | bytes 1572872 | tf_op jit(solution)/shard_map/ppermute | solution.py:317
  61.0 0.0 collective-permute-done.14.refs_0_
  61.0 1.2 %project.10 = bf16[512,512]{1,0:T(8,128)(2,1)S(1)} custom-call(s32[2]{0:T(128)S(1)} %pad_add_fusion.at_ref, bf16[512,512]{1,0:T(8,128)(2,1)S(1)} %get-tuple-element.79.a_own.a1, bf16[512,512]{1,0:T(8,128)(2,1)S(1)} %collective-permute-done.8.a_sib.a1, bf16[512,4096]{1,0:T(8,128)(2,1)S(1)} %copy-done, bf16[2,512,512]{2,1,0:T(8,128)(2,1)S(1)} %collective-permute-done.9.w_sib, ...), custom_call_target="tpu_custom_call" | custom-call | tf_op jit(solution)/shard_map/project/pallas_call | solution.py:277
  62.3 2.4 %collective-permute-start.15 = (bf16[512,512]{1,0:T(8,128)(2,1)S(1)}, bf16[512,512]{1,0:T(8,128)(2,1)S(1)}, u32[]{:S(2)}, u32[]{:S(2)}) collective-permute-start(bf16[512,512]{1,0:T(8,128)(2,1)S(1)} %project.10), channel_id=1, source_target_pairs={{0,6},{2,4},{4,2},{6,0},{1,7},{3,5},{5,3},{7,1},{8,14},{10,12},{12... | collective-permute-start | bytes 1572872 | tf_op jit(solution)/shard_map/ppermute | solution.py:317
  64.7 0.0 collective-permute-done.11.w_sib
  64.7 4.0 %collective-permute-done.13.refs_0_ = bf16[512,512]{1,0:T(8,128)(2,1)S(1)} collective-permute-done((bf16[512,512]{1,0:T(8,128)(2,1)S(1)}, bf16[512,512]{1,0:T(8,128)(2,1)S(1)}, u32[]{:S(2)}, u32[]{:S(2)}) %collective-permute-start.13) | collective-permute-done | bytes 524320 | tf_op jit(solution)/shard_map/ppermute | solution.py:317
  68.6 1.3 %project.9.p2 = f32[512,512]{1,0:T(8,128)S(1)} custom-call(s32[2]{0:T(128)S(1)} %pad_add_fusion.at_ref, bf16[512,512]{1,0:T(8,128)(2,1)S(1)} %get-tuple-element.82.a_own.a2, bf16[512,512]{1,0:T(8,128)(2,1)S(1)} %collective-permute-done.10.a_sib.a2, bf16[512,4096]{1,0:T(8,128)(2,1)S(1)} %copy-done, bf16[1,512,512]{2,1,0:T(8,128)(2,1)S(1)} %collective-permute-done.11.w_sib, ...), custom_call_target="tpu_custom_call" | custom-call | tf_op jit(solution)/shard_map/project/pallas_call | solution.py:277
  69.9 0.0 collective-permute-done.12.refs_0_
  69.9 1.3 %project.8.p1 = f32[512,512]{1,0:T(8,128)S(1)} custom-call(s32[2]{0:T(128)S(1)} %pad_add_fusion.at_ref, bf16[512,512]{1,0:T(8,128)(2,1)S(1)} %get-tuple-element.79.a_own.a1, bf16[512,512]{1,0:T(8,128)(2,1)S(1)} %collective-permute-done.8.a_sib.a1, bf16[512,4096]{1,0:T(8,128)(2,1)S(1)} %copy-done, bf16[1,512,512]{2,1,0:T(8,128)(2,1)S(1)} %collective-permute-done.11.w_sib, ...), custom_call_target="tpu_custom_call" | custom-call | tf_op jit(solution)/shard_map/project/pallas_call | solution.py:277
  71.2 9.6 %collective-permute-done.17.r2 = bf16[512,512]{1,0:T(8,128)(2,1)S(1)} collective-permute-done((bf16[512,512]{1,0:T(8,128)(2,1)S(1)}, bf16[512,512]{1,0:T(8,128)(2,1)S(1)}, u32[]{:S(2)}, u32[]{:S(2)}) %collective-permute-start.17) | collective-permute-done | bytes 524320 | tf_op jit(solution)/shard_map/ppermute | solution.py:317
  80.8 0.0 collective-permute-done.15.r1
  80.8 1.0 %finish.1 = bf16[1024,512]{1,0:T(8,128)(2,1)} custom-call(f32[512,512]{1,0:T(8,128)S(1)} %project.8.p1, f32[512,512]{1,0:T(8,128)S(1)} %project.9.p2, bf16[512,512]{1,0:T(8,128)(2,1)S(1)} %collective-permute-done.15.r1, bf16[512,512]{1,0:T(8,128)(2,1)S(1)} %collective-permute-done.17.r2), custom_call_target="tpu_custom_call" | custom-call | tf_op jit(solution)/shard_map/finish/pallas_call | solution.py:304
  (3 shorter events, 0.1 us)
Async XLA Ops:
  2.4 5.0 %collective-permute-start = (bf16[528,128]{1,0:T(8,128)(2,1)S(1)}, bf16[528,128]{1,0:T(8,128)(2,1)S(1)}, u32[]{:S(2)}, u32[]{:S(2)}) collective-permute-start(bf16[528,128]{1,0:T(8,128)(2,1)S(1)} %delta.1), channel_id=1, source_target_pairs={{0,8},{8,0},{16,24},{24,16},{32,40},{40,32},{48,56},{56,48},{1,9},... | collective-permute-start | bytes 405512 | tf_op jit(solution)/shard_map/ppermute | solution.py:317
  5.0 10.6 %copy-start.1 = (f32[4]{0:T(128)S(1)}, f32[4]{0:T(128)}, u32[]{:S(2)}) copy-start(f32[4]{0:T(128)} %param.8) | copy-start | bytes 52
  7.4 17.3 %collective-permute-start.1 = (bf16[528,128]{1,0:T(8,128)(2,1)S(1)}, bf16[528,128]{1,0:T(8,128)(2,1)S(1)}, u32[]{:S(2)}, u32[]{:S(2)}) collective-permute-start(bf16[528,128]{1,0:T(8,128)(2,1)S(1)} %convert_element_type.40), channel_id=1, source_target_pairs={{0,40},{8,32},{16,56},{24,48},{32,8},{40,0},{48,24},{56,16},{1,41}... | collective-permute-start | bytes 405512 | tf_op jit(solution)/shard_map/ppermute | solution.py:317
  14.4 11.3 %collective-permute-start.2 = (bf16[528,128]{1,0:T(8,128)(2,1)S(1)}, bf16[528,128]{1,0:T(8,128)(2,1)S(1)}, u32[]{:S(2)}, u32[]{:S(2)}) collective-permute-start(bf16[528,128]{1,0:T(8,128)(2,1)S(1)} %convert_element_type.40), channel_id=1, source_target_pairs={{0,48},{8,56},{16,32},{24,40},{32,16},{40,24},{48,0},{56,8},{1,49}... | collective-permute-start | bytes 405512 | tf_op jit(solution)/shard_map/ppermute | solution.py:317
  14.6 12.1 %collective-permute-start.3 = (bf16[528,128]{1,0:T(8,128)(2,1)S(1)}, bf16[528,128]{1,0:T(8,128)(2,1)S(1)}, u32[]{:S(2)}, u32[]{:S(2)}) collective-permute-start(bf16[528,128]{1,0:T(8,128)(2,1)S(1)} %convert_element_type.40), channel_id=1, source_target_pairs={{0,16},{8,24},{16,0},{24,8},{32,48},{40,56},{48,32},{56,40},{1,17}... | collective-permute-start | bytes 405512 | tf_op jit(solution)/shard_map/ppermute | solution.py:317
  15.6 20.6 %collective-permute-start.7 = (bf16[512,512]{1,0:T(8,128)(2,1)S(1)}, bf16[512,512]{1,0:T(8,128)(2,1)S(1)}, u32[]{:S(2)}, u32[]{:S(2)}) collective-permute-start(bf16[512,512]{1,0:T(8,128)(2,1)S(1)} %get-tuple-element.70), channel_id=1, source_target_pairs={{0,1},{1,0},{2,3},{3,2},{4,5},{5,4},{6,7},{7,6},{8,9},{9,8},{10,11... | collective-permute-start | bytes 1572872 | tf_op jit(solution)/shard_map/ppermute | solution.py:317
  26.9 5.8 %collective-permute-start.4 = (bf16[528,128]{1,0:T(8,128)(2,1)S(1)}, bf16[528,128]{1,0:T(8,128)(2,1)S(1)}, u32[]{:S(2)}, u32[]{:S(2)}) collective-permute-start(bf16[528,128]{1,0:T(8,128)(2,1)S(1)} %convert_add_fusion), channel_id=1, source_target_pairs={{0,128},{64,192},{128,0},{192,64},{1,129},{65,193},{129,1},{193,65... | collective-permute-start | bytes 405512 | tf_op jit(solution)/shard_map/ppermute | solution.py:317
  29.9 5.6 %collective-permute-start.5 = (bf16[528,128]{1,0:T(8,128)(2,1)S(1)}, bf16[528,128]{1,0:T(8,128)(2,1)S(1)}, u32[]{:S(2)}, u32[]{:S(2)}) collective-permute-start(bf16[528,128]{1,0:T(8,128)(2,1)S(1)} %convert_add_fusion), channel_id=1, source_target_pairs={{0,64},{64,0},{128,192},{192,128},{1,65},{65,1},{129,193},{193,129... | collective-permute-start | bytes 405512 | tf_op jit(solution)/shard_map/ppermute | solution.py:317
  30.3 5.8 %collective-permute-start.6 = (bf16[528,128]{1,0:T(8,128)(2,1)S(1)}, bf16[528,128]{1,0:T(8,128)(2,1)S(1)}, u32[]{:S(2)}, u32[]{:S(2)}) collective-permute-start(bf16[528,128]{1,0:T(8,128)(2,1)S(1)} %convert_add_fusion), channel_id=1, source_target_pairs={{0,192},{64,128},{128,64},{192,0},{1,193},{65,129},{129,65},{193,1... | collective-permute-start | bytes 405512 | tf_op jit(solution)/shard_map/ppermute | solution.py:317
  30.7 9.8 %copy-start = (bf16[512,4096]{1,0:T(8,128)(2,1)S(1)}, bf16[512,4096]{1,0:T(8,128)(2,1)}, u32[]{:S(2)}) copy-start(bf16[512,4096]{1,0:T(8,128)(2,1)} %w_own.13) | copy-start | bytes 12582916
  37.6 4.1 %collective-permute-start.10 = (bf16[512,512]{1,0:T(8,128)(2,1)S(1)}, bf16[512,512]{1,0:T(8,128)(2,1)S(1)}, u32[]{:S(2)}, u32[]{:S(2)}) collective-permute-start(bf16[512,512]{1,0:T(8,128)(2,1)S(1)} %get-tuple-element.82.a_own.a2), channel_id=1, source_target_pairs={{0,1},{1,0},{2,3},{3,2},{4,5},{5,4},{6,7},{7,6},{8,9},{9,8},{10,11... | collective-permute-start | bytes 1572872 | tf_op jit(solution)/shard_map/ppermute | solution.py:317
  39.9 2.3 %collective-permute-start.8 = (bf16[512,512]{1,0:T(8,128)(2,1)S(1)}, bf16[512,512]{1,0:T(8,128)(2,1)S(1)}, u32[]{:S(2)}, u32[]{:S(2)}) collective-permute-start(bf16[512,512]{1,0:T(8,128)(2,1)S(1)} %get-tuple-element.79.a_own.a1), channel_id=1, source_target_pairs={{0,1},{1,0},{2,3},{3,2},{4,5},{5,4},{6,7},{7,6},{8,9},{9,8},{10,11... | collective-permute-start | bytes 1572872 | tf_op jit(solution)/shard_map/ppermute | solution.py:317
  40.0 5.5 %collective-permute-start.9 = (bf16[2,512,512]{2,1,0:T(8,128)(2,1)S(1)}, bf16[2,512,512]{2,1,0:T(8,128)(2,1)S(1)}, u32[]{:S(2)}, u32[]{:S(2)}) collective-permute-start(bf16[2,512,512]{2,1,0:T(8,128)(2,1)S(1)} %get-tuple-element.81), channel_id=1, source_target_pairs={{0,1},{1,0},{2,3},{3,2},{4,5},{5,4},{6,7},{7,6},{8,9},{9,8},{10,11... | collective-permute-start | bytes 3145736 | tf_op jit(solution)/shard_map/ppermute | solution.py:317
  43.0 14.4 %collective-permute-start.16 = (bf16[512,512]{1,0:T(8,128)(2,1)S(1)}, bf16[512,512]{1,0:T(8,128)(2,1)S(1)}, u32[]{:S(2)}, u32[]{:S(2)}) collective-permute-start(bf16[512,512]{1,0:T(8,128)(2,1)S(1)} %get-tuple-element.89), channel_id=1, source_target_pairs={{0,6},{2,4},{4,2},{6,0},{1,7},{3,5},{5,3},{7,1},{8,14},{10,12},{12... | collective-permute-start | bytes 1572872 | tf_op jit(solution)/shard_map/ppermute | solution.py:317
  45.5 15.5 %collective-permute-start.14 = (bf16[512,512]{1,0:T(8,128)(2,1)S(1)}, bf16[512,512]{1,0:T(8,128)(2,1)S(1)}, u32[]{:S(2)}, u32[]{:S(2)}) collective-permute-start(bf16[512,512]{1,0:T(8,128)(2,1)S(1)} %get-tuple-element.87), channel_id=1, source_target_pairs={{0,2},{2,0},{4,6},{6,4},{1,3},{3,1},{5,7},{7,5},{8,10},{10,8},{12,... | collective-permute-start | bytes 1572872 | tf_op jit(solution)/shard_map/ppermute | solution.py:317
  46.8 21.8 %collective-permute-start.13 = (bf16[512,512]{1,0:T(8,128)(2,1)S(1)}, bf16[512,512]{1,0:T(8,128)(2,1)S(1)}, u32[]{:S(2)}, u32[]{:S(2)}) collective-permute-start(bf16[512,512]{1,0:T(8,128)(2,1)S(1)} %project.7), channel_id=1, source_target_pairs={{0,6},{2,4},{4,2},{6,0},{1,7},{3,5},{5,3},{7,1},{8,14},{10,12},{12... | collective-permute-start | bytes 1572872 | tf_op jit(solution)/shard_map/ppermute | solution.py:317
  49.1 20.8 %collective-permute-start.12 = (bf16[512,512]{1,0:T(8,128)(2,1)S(1)}, bf16[512,512]{1,0:T(8,128)(2,1)S(1)}, u32[]{:S(2)}, u32[]{:S(2)}) collective-permute-start(bf16[512,512]{1,0:T(8,128)(2,1)S(1)} %project.6), channel_id=1, source_target_pairs={{0,2},{2,0},{4,6},{6,4},{1,3},{3,1},{5,7},{7,5},{8,10},{10,8},{12,... | collective-permute-start | bytes 1572872 | tf_op jit(solution)/shard_map/ppermute | solution.py:317
  58.7 22.2 %collective-permute-start.17 = (bf16[512,512]{1,0:T(8,128)(2,1)S(1)}, bf16[512,512]{1,0:T(8,128)(2,1)S(1)}, u32[]{:S(2)}, u32[]{:S(2)}) collective-permute-start(bf16[512,512]{1,0:T(8,128)(2,1)S(1)} %project.11), channel_id=1, source_target_pairs={{0,2},{2,0},{4,6},{6,4},{1,3},{3,1},{5,7},{7,5},{8,10},{10,8},{12,... | collective-permute-start | bytes 1572872 | tf_op jit(solution)/shard_map/ppermute | solution.py:317
  58.8 5.9 %collective-permute-start.11 = (bf16[1,512,512]{2,1,0:T(8,128)(2,1)S(1)}, bf16[1,512,512]{2,1,0:T(8,128)(2,1)S(1)}, u32[]{:S(2)}, u32[]{:S(2)}) collective-permute-start(bf16[1,512,512]{2,1,0:T(8,128)(2,1)S(1)} %get-tuple-element.83), channel_id=1, source_target_pairs={{0,1},{1,0},{2,3},{3,2},{4,5},{5,4},{6,7},{7,6},{8,9},{9,8},{10,11... | collective-permute-start | bytes 1572872 | tf_op jit(solution)/shard_map/ppermute | solution.py:317
  62.3 18.5 %collective-permute-start.15 = (bf16[512,512]{1,0:T(8,128)(2,1)S(1)}, bf16[512,512]{1,0:T(8,128)(2,1)S(1)}, u32[]{:S(2)}, u32[]{:S(2)}) collective-permute-start(bf16[512,512]{1,0:T(8,128)(2,1)S(1)} %project.10), channel_id=1, source_target_pairs={{0,6},{2,4},{4,2},{6,0},{1,7},{3,5},{5,3},{7,1},{8,14},{10,12},{12... | collective-permute-start | bytes 1572872 | tf_op jit(solution)/shard_map/ppermute | solution.py:317
